TPU v7x, 256 devices: a whole 4x4x8 slice. The times are simulated.
256 devices in a mesh: rep: 8 (over x, y_lo), ep: 32 (over y_hi, z, core).
Axes of the slice: x: 4, y: 4 (y_hi: 2, y_lo: 2; y = y_hi * 2 + y_lo), z: 8, core: 2. Of those that a mesh axis runs over, the one named last changes fastest.
Arguments:
- tokens: bfloat16 [2, 32, 8, 4, 4096], P(None, 'ep', 'rep'), may hold values from -6 to 6
- norm_gain: float32 [4096], replicated, may hold values from 0.5 to 1.5
- expert_ids: int32 [2, 32, 8, 4, 8], P(None, 'ep'), may hold values from 0 to 63, all different within a row; in each aligned block of 32 rows (0 to 31, 32 to 63, ..., all dimensions but the last counted through in order) at most 5 rows name the same one
- route_weights: float32 [2, 32, 8, 4, 8], P(None, 'ep'), may hold values from 0.05 to 1
- w_gate: bfloat16 [64, 1536, 4096], P('ep', 'rep'), may hold values from -0.09375 to 0.09375
- w_up: bfloat16 [64, 1536, 4096], P('ep', 'rep'), may hold values from -0.09375 to 0.09375
- w_down: bfloat16 [64, 1536, 4096], P('ep', 'rep'), may hold values from -0.15625 to 0.15625
Outputs:
- mixed: bfloat16 [2, 32, 8, 4, 4096], P(None, 'ep', 'rep')
Inputs may be any that keep to these rules, and one draw needn't show every extreme that they name: `expert_ids`: each row names 8 different experts. In each step, among the rows of one index of ep (32 rows, an aligned block), no expert is named by more than 5 rows, a bound that some block reaches.
All inputs are finite; a program needn't handle non-finite values.
Results may differ from a plain program's by a relative error of at most 0.014.
Values may be sent and summed in bfloat16 or wider, within the bound.
No kernel may reach another device: no remote copies, remote signals or barrier semaphores. Data moves between devices by JAX's collectives and lax.ppermute only.
A program may use at most 128 MiB of HBM per device.

v0:
```python
import jax
import jax.numpy as jnp
from jax import lax
from jax.sharding import PartitionSpec as P

epsilon = 1e-06


def in_order(tiles, dim):
    tiles = jnp.moveaxis(tiles, 0, dim)
    shape = tiles.shape
    return tiles.reshape(*shape[:dim], shape[dim] * shape[dim + 1], *shape[dim + 2 :])


def from_everyone(array, axis):
    copies = jnp.broadcast_to(array, (lax.axis_size(axis), *array.shape))
    return lax.all_to_all(copies, axis, split_axis=0, concat_axis=0, tiled=True)


def gathered_copies(array, axis, dim):
    return in_order(from_everyone(array, axis), dim)


def cut_along(array, dim, size):
    before, after = (array.shape[:dim], array.shape[dim + 1 :])
    return jnp.moveaxis(array.reshape(*before, size, -1, *after), dim, 0)


def sent_and_summed(array, axis, dim):
    tiles = cut_along(array, dim, lax.axis_size(axis))
    arrived = lax.all_to_all(tiles, axis, split_axis=0, concat_axis=0, tiled=True)
    return arrived.astype(jnp.float32).sum(axis=0)


def norm_rows(values, gain_values):
    widened = values.astype(jnp.float32)
    scaled = lax.rsqrt(jnp.mean(widened * widened, axis=-1, keepdims=True) + epsilon)
    return (widened * scaled * gain_values).astype(jnp.bfloat16)


def expert_partial(slot_rows, gate_weight, up_weight, down_weight):
    contract_last = (((1,), (1,)), ((), ()))
    gate_out = lax.dot_general(
        slot_rows, gate_weight, contract_last, preferred_element_type=jnp.float32
    )
    up_out = lax.dot_general(
        slot_rows, up_weight, contract_last, preferred_element_type=jnp.float32
    )
    hidden = (jax.nn.silu(gate_out) * up_out).astype(jnp.bfloat16)
    return jnp.dot(hidden, down_weight, preferred_element_type=jnp.float32).astype(jnp.bfloat16)


def weigh_choices(shares, picked):
    choice_total = picked.shape[1]
    weighted = shares[:, 0:1] * picked[:, 0]
    for which in range(1, choice_total):
        weighted = weighted + shares[:, which : which + 1] * picked[:, which]
    return weighted


def on_device(tokens, norm_gain, expert_ids, route_weights, w_gate, w_up, w_down):
    ep_size = lax.axis_size("ep")
    rep_size = lax.axis_size("rep")
    step_count = tokens.shape[0]
    row_count = tokens.shape[3]
    model_width = tokens.shape[4]
    choice_count = expert_ids.shape[4]
    local_experts = w_gate.shape[0]
    experts = local_experts * ep_size
    block_rows = rep_size * row_count
    capacity = block_rows * choice_count * 5 // (4 * experts)
    column_width = model_width // rep_size
    assigned = block_rows * choice_count
    row_of = jnp.arange(assigned, dtype=jnp.int32) // choice_count
    outputs = []
    for step_index in range(step_count):
        own_normed = norm_rows(tokens[step_index, 0, 0], norm_gain)
        step_weights = route_weights[step_index].reshape(block_rows, choice_count)
        shares = step_weights / jnp.sum(step_weights, axis=1, keepdims=True)
        chosen_ids = expert_ids[step_index].reshape(assigned)
        target = chosen_ids // local_experts
        slot_index = chosen_ids % local_experts
        buckets = ep_size * local_experts
        bucket = target * local_experts + slot_index
        onehot = (bucket[:, None] == jnp.arange(buckets, dtype=jnp.int32)[None, :]).astype(
            jnp.int32
        )
        position = jnp.sum((jnp.cumsum(onehot, axis=0) - onehot) * onehot, axis=1)
        flat_index = bucket * capacity + position
        source_row = (
            jnp.full((buckets * capacity,), block_rows, jnp.int32).at[flat_index].set(row_of)
        )
        own_part = lax.all_to_all(own_normed, "rep", split_axis=1, concat_axis=0, tiled=True)
        padded = jnp.concatenate([own_part, jnp.zeros((1, column_width), jnp.bfloat16)], axis=0)
        outgoing = jnp.take(padded, source_row, axis=0).reshape(
            ep_size, local_experts, capacity, column_width
        )
        received = lax.all_to_all(outgoing, "ep", split_axis=0, concat_axis=0, tiled=True)
        arrived = gathered_copies(received, "rep", 3)
        slot_results = []
        for local_slot in range(local_experts):
            weights_now = (w_gate[local_slot], w_up[local_slot], w_down[local_slot])
            slot_rows = arrived[:, local_slot].reshape(ep_size * capacity, model_width)
            slot_out = expert_partial(slot_rows, weights_now[0], weights_now[1], weights_now[2])
            slot_results.append(slot_out.reshape(ep_size, capacity, model_width))
        results_out = jnp.stack(slot_results, axis=1)
        summed = sent_and_summed(results_out.astype(jnp.float32).astype(jnp.bfloat16), "rep", 3)
        back = lax.all_to_all(
            summed.astype(jnp.bfloat16), "ep", split_axis=0, concat_axis=0, tiled=True
        ).astype(summed.dtype)
        picked = jnp.take(back.reshape(buckets * capacity, column_width), flat_index, axis=0)
        picked = picked.reshape(block_rows, choice_count, column_width)
        weighted = weigh_choices(shares, picked)
        mixed = (
            lax.all_to_all(
                weighted.astype(jnp.bfloat16), "rep", split_axis=0, concat_axis=1, tiled=True
            )
            .astype(weighted.dtype)
            .astype(jnp.bfloat16)
        )
        outputs.append(mixed)
    return jnp.stack(outputs)[:, None, None]


def solution(mesh):
    return jax.shard_map(
        on_device,
        mesh=mesh,
        in_specs=(
            P(None, "ep", "rep", None, None),
            P(),
            P(None, "ep", None, None, None),
            P(None, "ep", None, None, None),
            P("ep", "rep", None),
            P("ep", "rep", None),
            P("ep", "rep", None),
        ),
        out_specs=P(None, "ep", "rep", None, None),
        check_vma=False,
    )
```

profile of v0, /device:TPU:8, one launch (start us, length us, event | category | flops | bytes accessed | tf_op | source)
XLA Modules:
  0.0 303.8 jit_solution(15188012363127883104)
XLA Ops:
  3.2 5.8 %all-to-all-start = ((bf16[4,8,512]{2,0,1:T(4,128)(2,1)}), bf16[4,8,512]{2,0,1:T(4,128)(2,1)S(1)}, u32[]{:S(2)}, u32[]{:S(2)}) async-start(bf16[4,8,512]{2,0,1:T(4,128)(2,1)} %get-tuple-element.57), calls=%async_computation | async-start | bytes 65536 | tf_op jit(solution)/shard_map/all_to_all | solution.py:93
  15.2 5.7 %all-to-all-start.6 = ((bf16[4,8,512]{2,0,1:T(4,128)(2,1)}), bf16[4,8,512]{2,0,1:T(4,128)(2,1)S(1)}, u32[]{:S(2)}, u32[]{:S(2)}) async-start(bf16[4,8,512]{2,0,1:T(4,128)(2,1)} %get-tuple-element.58), calls=%async_computation.6 | async-start | bytes 65536 | tf_op jit(solution)/shard_map/all_to_all | solution.py:93
  25.8 10.6 %all-to-all-start.1 = ((bf16[32,2,5,512]{3,1,2,0:T(2,128)(2,1)}), bf16[32,2,5,512]{3,1,2,0:T(2,128)(2,1)S(1)}, u32[]{:S(2)}, u32[]{:S(2)}) async-start(bf16[32,2,5,512]{3,1,2,0:T(2,128)(2,1)} %copy.143), calls=%async_computation.1 | async-start | bytes 655360 | tf_op jit(solution)/shard_map/all_to_all | solution.py:98
  39.8 12.6 %all-to-all-done.1 = bf16[32,2,5,512]{3,1,2,0:T(2,128)(2,1)S(1)} async-done(((bf16[32,2,5,512]{3,1,2,0:T(2,128)(2,1)}), bf16[32,2,5,512]{3,1,2,0:T(2,128)(2,1)S(1)}, u32[]{:S(2)}, u32[]{:S(2)}) %all-to-all-start.1) | async-done | bytes 327712 | tf_op jit(solution)/shard_map/all_to_all | solution.py:98
  52.4 3.9 %all-to-all-start.7 = ((bf16[32,2,5,512]{3,1,2,0:T(2,128)(2,1)}), bf16[32,2,5,512]{3,1,2,0:T(2,128)(2,1)S(1)}, u32[]{:S(2)}, u32[]{:S(2)}) async-start(bf16[32,2,5,512]{3,1,2,0:T(2,128)(2,1)} %copy.157), calls=%async_computation.7 | async-start | bytes 655360 | tf_op jit(solution)/shard_map/all_to_all | solution.py:98
  56.3 15.9 %all-to-all-done.7 = bf16[32,2,5,512]{3,1,2,0:T(2,128)(2,1)S(1)} async-done(((bf16[32,2,5,512]{3,1,2,0:T(2,128)(2,1)}), bf16[32,2,5,512]{3,1,2,0:T(2,128)(2,1)S(1)}, u32[]{:S(2)}, u32[]{:S(2)}) %all-to-all-start.7) | async-done | bytes 327712 | tf_op jit(solution)/shard_map/all_to_all | solution.py:98
  74.1 5.5 %all-to-all-start.2 = ((bf16[8,32,2,5,512]{4,1,3,2,0:T(8,128)(2,1)}), bf16[8,32,2,5,512]{4,1,3,2,0:T(8,128)(2,1)S(1)}, u32[]{:S(2)}, u32[]{:S(2)}) async-start(bf16[8,32,2,5,512]{4,1,3,2,0:T(8,128)(2,1)} %broadcast_in_dim.24), calls=%async_computation.2 | async-start | bytes 5242880 | tf_op jit(solution)/shard_map/all_to_all | solution.py:17
  79.6 34.8 %all-to-all-done.2 = bf16[8,32,2,5,512]{4,1,3,2,0:T(8,128)(2,1)S(1)} async-done(((bf16[8,32,2,5,512]{4,1,3,2,0:T(8,128)(2,1)}), bf16[8,32,2,5,512]{4,1,3,2,0:T(8,128)(2,1)S(1)}, u32[]{:S(2)}, u32[]{:S(2)}) %all-to-all-start.2) | async-done | bytes 2621472 | tf_op jit(solution)/shard_map/all_to_all | solution.py:17
  116.7 6.2 %all-to-all-start.8 = ((bf16[8,32,2,5,512]{4,1,3,2,0:T(8,128)(2,1)}), bf16[8,32,2,5,512]{4,1,3,2,0:T(8,128)(2,1)S(1)}, u32[]{:S(2)}, u32[]{:S(2)}) async-start(bf16[8,32,2,5,512]{4,1,3,2,0:T(8,128)(2,1)} %broadcast_in_dim.25), calls=%async_computation.8 | async-start | bytes 5242880 | tf_op jit(solution)/shard_map/all_to_all | solution.py:17
  133.5 5.0 %convolution_convert_fusion.3 = bf16[160,4096]{1,0:T(8,128)(2,1)} fusion(bf16[2,192,4096]{2,1,0:T(8,128)(2,1)} %param.17, bf16[160,4096]{1,0:T(8,128)(2,1)} %reshape_squeeze.36, bf16[2,192,4096]{2,1,0:T(8,128)(2,1)} %param.16, f32[160,192]{1,0:T(8,128)S(1)} %fusion.18), kind=kOutput, calls=%fused_computation.9 | convolution fusion | flops 504156160 | bytes 5890048 | tf_op jit(solution)/shard_map/dot_general | solution.py:50
  149.0 5.0 %convolution_convert_fusion.2 = bf16[160,4096]{1,0:T(8,128)(2,1)} fusion(bf16[2,192,4096]{2,1,0:T(8,128)(2,1)} %param.17, bf16[160,4096]{1,0:T(8,128)(2,1)} %reshape_squeeze.37, bf16[2,192,4096]{2,1,0:T(8,128)(2,1)} %param.16, f32[160,192]{1,0:T(8,128)S(1)} %fusion.8), kind=kOutput, calls=%fused_computation.8 | convolution fusion | flops 504156160 | bytes 5890048 | tf_op jit(solution)/shard_map/dot_general | solution.py:50
  160.4 5.7 %all-to-all-start.3 = ((bf16[8,32,2,5,512]{4,1,3,2,0:T(8,128)(2,1)}), bf16[8,32,2,5,512]{4,1,3,2,0:T(8,128)(2,1)S(1)}, u32[]{:S(2)}, u32[]{:S(2)}) async-start(bf16[8,32,2,5,512]{4,1,3,2,0:T(8,128)(2,1)} %maximum_bitcast_fusion), calls=%async_computation.3 | async-start | bytes 5242880 | tf_op jit(solution)/shard_map/all_to_all | solution.py:31
  171.6 2.7 reshape_squeeze.42
  176.8 5.0 %convolution_convert_fusion.1 = bf16[160,4096]{1,0:T(8,128)(2,1)} fusion(bf16[2,192,4096]{2,1,0:T(8,128)(2,1)} %param.17, bf16[160,4096]{1,0:T(8,128)(2,1)} %reshape_squeeze.42, bf16[2,192,4096]{2,1,0:T(8,128)(2,1)} %param.16, f32[160,192]{1,0:T(8,128)S(1)} %fusion.16), kind=kOutput, calls=%fused_computation.7 | convolution fusion | flops 504156160 | bytes 5890048 | tf_op jit(solution)/shard_map/dot_general | solution.py:50
  187.3 2.7 reshape_squeeze.43
  192.4 5.0 %convolution_convert_fusion = bf16[160,4096]{1,0:T(8,128)(2,1)} fusion(bf16[2,192,4096]{2,1,0:T(8,128)(2,1)} %param.17, bf16[160,4096]{1,0:T(8,128)(2,1)} %reshape_squeeze.43, bf16[2,192,4096]{2,1,0:T(8,128)(2,1)} %param.16, f32[160,192]{1,0:T(8,128)S(1)} %fusion.6), kind=kOutput, calls=%fused_computation.6 | convolution fusion | flops 504156160 | bytes 5890048 | tf_op jit(solution)/shard_map/dot_general | solution.py:50
  202.3 5.8 %all-to-all-start.9 = ((bf16[8,32,2,5,512]{4,1,3,2,0:T(8,128)(2,1)}), bf16[8,32,2,5,512]{4,1,3,2,0:T(8,128)(2,1)}, u32[]{:S(2)}, u32[]{:S(2)}) async-start(bf16[8,32,2,5,512]{4,1,3,2,0:T(8,128)(2,1)} %maximum_bitcast_fusion.1), calls=%async_computation.9 | async-start | bytes 5242880 | tf_op jit(solution)/shard_map/all_to_all | solution.py:31
  211.5 27.3 %all-to-all-done.9 = bf16[8,32,2,5,512]{4,1,3,2,0:T(8,128)(2,1)} async-done(((bf16[8,32,2,5,512]{4,1,3,2,0:T(8,128)(2,1)}), bf16[8,32,2,5,512]{4,1,3,2,0:T(8,128)(2,1)}, u32[]{:S(2)}, u32[]{:S(2)}) %all-to-all-start.9) | async-done | bytes 2621472 | tf_op jit(solution)/shard_map/all_to_all | solution.py:31
  238.8 8.4 %all-to-all-start.4 = ((bf16[32,2,5,512]{3,1,2,0:T(2,128)(2,1)}), bf16[32,2,5,512]{3,1,2,0:T(2,128)(2,1)S(1)}, u32[]{:S(2)}, u32[]{:S(2)}) async-start(bf16[32,2,5,512]{3,1,2,0:T(2,128)(2,1)} %copy.151), calls=%async_computation.4 | async-start | bytes 655360 | tf_op jit(solution)/shard_map/all_to_all | solution.py:108
  250.6 12.6 %all-to-all-done.4 = bf16[32,2,5,512]{3,1,2,0:T(2,128)(2,1)S(1)} async-done(((bf16[32,2,5,512]{3,1,2,0:T(2,128)(2,1)}), bf16[32,2,5,512]{3,1,2,0:T(2,128)(2,1)S(1)}, u32[]{:S(2)}, u32[]{:S(2)}) %all-to-all-start.4) | async-done | bytes 327712 | tf_op jit(solution)/shard_map/all_to_all | solution.py:108
  263.2 4.1 %all-to-all-start.10 = ((bf16[32,2,5,512]{3,1,2,0:T(2,128)(2,1)}), bf16[32,2,5,512]{3,1,2,0:T(2,128)(2,1)S(1)}, u32[]{:S(2)}, u32[]{:S(2)}) async-start(bf16[32,2,5,512]{3,1,2,0:T(2,128)(2,1)} %copy.165), calls=%async_computation.10 | async-start | bytes 655360 | tf_op jit(solution)/shard_map/all_to_all | solution.py:108
  271.4 11.7 %all-to-all-done.10 = bf16[32,2,5,512]{3,1,2,0:T(2,128)(2,1)S(1)} async-done(((bf16[32,2,5,512]{3,1,2,0:T(2,128)(2,1)}), bf16[32,2,5,512]{3,1,2,0:T(2,128)(2,1)S(1)}, u32[]{:S(2)}, u32[]{:S(2)}) %all-to-all-start.10) | async-done | bytes 327712 | tf_op jit(solution)/shard_map/all_to_all | solution.py:108
  283.1 6.1 %all-to-all-start.5 = ((bf16[8,4,512]{2,1,0:T(4,128)(2,1)}), bf16[8,4,512]{2,1,0:T(4,128)(2,1)S(1)}, u32[]{:S(2)}, u32[]{:S(2)}) async-start(bf16[8,4,512]{2,1,0:T(4,128)(2,1)} %add_convert_fusion.1), calls=%async_computation.5 | async-start | bytes 65536 | tf_op jit(solution)/shard_map/all_to_all | solution.py:115
  294.1 9.0 %all_to_all.98 = bf16[8,4,512]{2,1,0:T(4,128)(2,1)S(1)} all-to-all(bf16[8,4,512]{2,1,0:T(4,128)(2,1)S(1)} %add_convert_fusion), channel_id=1, replica_groups=mesh['rep'=8,'ep'=32] {'rep'}, dimensions={0} | all-to-all | bytes 65536 | tf_op jit(solution)/shard_map/all_to_all | solution.py:115
  (161 shorter events, 85.9 us)
Async XLA Ops:
  3.2 12.0 %all-to-all-start = ((bf16[4,8,512]{2,0,1:T(4,128)(2,1)}), bf16[4,8,512]{2,0,1:T(4,128)(2,1)S(1)}, u32[]{:S(2)}, u32[]{:S(2)}) async-start(bf16[4,8,512]{2,0,1:T(4,128)(2,1)} %get-tuple-element.57), calls=%async_computation | async-start | bytes 65536 | tf_op jit(solution)/shard_map/all_to_all | solution.py:93
  15.2 10.6 %all-to-all-start.6 = ((bf16[4,8,512]{2,0,1:T(4,128)(2,1)}), bf16[4,8,512]{2,0,1:T(4,128)(2,1)S(1)}, u32[]{:S(2)}, u32[]{:S(2)}) async-start(bf16[4,8,512]{2,0,1:T(4,128)(2,1)} %get-tuple-element.58), calls=%async_computation.6 | async-start | bytes 65536 | tf_op jit(solution)/shard_map/all_to_all | solution.py:93
  25.8 26.6 %all-to-all-start.1 = ((bf16[32,2,5,512]{3,1,2,0:T(2,128)(2,1)}), bf16[32,2,5,512]{3,1,2,0:T(2,128)(2,1)S(1)}, u32[]{:S(2)}, u32[]{:S(2)}) async-start(bf16[32,2,5,512]{3,1,2,0:T(2,128)(2,1)} %copy.143), calls=%async_computation.1 | async-start | bytes 655360 | tf_op jit(solution)/shard_map/all_to_all | solution.py:98
  52.4 19.9 %all-to-all-start.7 = ((bf16[32,2,5,512]{3,1,2,0:T(2,128)(2,1)}), bf16[32,2,5,512]{3,1,2,0:T(2,128)(2,1)S(1)}, u32[]{:S(2)}, u32[]{:S(2)}) async-start(bf16[32,2,5,512]{3,1,2,0:T(2,128)(2,1)} %copy.157), calls=%async_computation.7 | async-start | bytes 655360 | tf_op jit(solution)/shard_map/all_to_all | solution.py:98
  74.1 40.3 %all-to-all-start.2 = ((bf16[8,32,2,5,512]{4,1,3,2,0:T(8,128)(2,1)}), bf16[8,32,2,5,512]{4,1,3,2,0:T(8,128)(2,1)S(1)}, u32[]{:S(2)}, u32[]{:S(2)}) async-start(bf16[8,32,2,5,512]{4,1,3,2,0:T(8,128)(2,1)} %broadcast_in_dim.24), calls=%async_computation.2 | async-start | bytes 5242880 | tf_op jit(solution)/shard_map/all_to_all | solution.py:17
  114.3 2.3 copy-start.1
  116.7 42.2 %all-to-all-start.8 = ((bf16[8,32,2,5,512]{4,1,3,2,0:T(8,128)(2,1)}), bf16[8,32,2,5,512]{4,1,3,2,0:T(8,128)(2,1)S(1)}, u32[]{:S(2)}, u32[]{:S(2)}) async-start(bf16[8,32,2,5,512]{4,1,3,2,0:T(8,128)(2,1)} %broadcast_in_dim.25), calls=%async_computation.8 | async-start | bytes 5242880 | tf_op jit(solution)/shard_map/all_to_all | solution.py:17
  140.3 1.5 copy-start.2
  155.9 1.3 copy-start.3
  158.9 1.5 copy-start
  160.4 41.9 %all-to-all-start.3 = ((bf16[8,32,2,5,512]{4,1,3,2,0:T(8,128)(2,1)}), bf16[8,32,2,5,512]{4,1,3,2,0:T(8,128)(2,1)S(1)}, u32[]{:S(2)}, u32[]{:S(2)}) async-start(bf16[8,32,2,5,512]{4,1,3,2,0:T(8,128)(2,1)} %maximum_bitcast_fusion), calls=%async_computation.3 | async-start | bytes 5242880 | tf_op jit(solution)/shard_map/all_to_all | solution.py:31
  183.7 1.5 copy-start.4
  199.3 1.3 copy-start.5
  202.3 5.8 %copy-start.6 = (f32[2,1,8,4,8]{4,3,2,1,0:T(4,128)S(1)}, f32[2,1,8,4,8]{4,3,2,1,0:T(4,128)}, u32[]{:S(2)}) copy-start(f32[2,1,8,4,8]{4,3,2,1,0:T(4,128)} %param.14) | copy-start | bytes 6148
  202.3 36.5 %all-to-all-start.9 = ((bf16[8,32,2,5,512]{4,1,3,2,0:T(8,128)(2,1)}), bf16[8,32,2,5,512]{4,1,3,2,0:T(8,128)(2,1)}, u32[]{:S(2)}, u32[]{:S(2)}) async-start(bf16[8,32,2,5,512]{4,1,3,2,0:T(8,128)(2,1)} %maximum_bitcast_fusion.1), calls=%async_computation.9 | async-start | bytes 5242880 | tf_op jit(solution)/shard_map/all_to_all | solution.py:31
  238.8 24.4 %all-to-all-start.4 = ((bf16[32,2,5,512]{3,1,2,0:T(2,128)(2,1)}), bf16[32,2,5,512]{3,1,2,0:T(2,128)(2,1)S(1)}, u32[]{:S(2)}, u32[]{:S(2)}) async-start(bf16[32,2,5,512]{3,1,2,0:T(2,128)(2,1)} %copy.151), calls=%async_computation.4 | async-start | bytes 655360 | tf_op jit(solution)/shard_map/all_to_all | solution.py:108
  263.2 19.9 %all-to-all-start.10 = ((bf16[32,2,5,512]{3,1,2,0:T(2,128)(2,1)}), bf16[32,2,5,512]{3,1,2,0:T(2,128)(2,1)S(1)}, u32[]{:S(2)}, u32[]{:S(2)}) async-start(bf16[32,2,5,512]{3,1,2,0:T(2,128)(2,1)} %copy.165), calls=%async_computation.10 | async-start | bytes 655360 | tf_op jit(solution)/shard_map/all_to_all | solution.py:108
  283.1 11.0 %all-to-all-start.5 = ((bf16[8,4,512]{2,1,0:T(4,128)(2,1)}), bf16[8,4,512]{2,1,0:T(4,128)(2,1)S(1)}, u32[]{:S(2)}, u32[]{:S(2)}) async-start(bf16[8,4,512]{2,1,0:T(4,128)(2,1)} %add_convert_fusion.1), calls=%async_computation.5 | async-start | bytes 65536 | tf_op jit(solution)/shard_map/all_to_all | solution.py:115
where the time goes:
time: 306 us; the launch traced here: 304 us
  waiting for transfers between devices  118 us (39%)
  starting transfers between devices  67.8 us (22%)
  local copies, waits for them, and re-layouts  65.7 us (21%)
  matrix products  29.9 us (10%)
  other arithmetic  12.7 us (4%)
  blocking collectives  8.95 us (3%)
    all_to_all x2, waiting for transfers between devices, from_everyone(): return lax.all_to_all(copies, axis, split_axis=0, concat_axis=0, tiled=True)  34.8 us
    all_to_all x2, waiting for transfers between devices, on_device(): lax.all_to_all(outgoing, 'ep', split_axis=0, concat_axis=0, tiled=True)  28.6 us
    all_to_all x2, waiting for transfers between devices, sent_and_summed(): lax.all_to_all(tiles, axis, split_axis=0, concat_axis=0, tiled=True)  27.3 us
    all_to_all x2, waiting for transfers between devices, on_device(): lax.all_to_all(summed.astype(jnp.bfloat16), 'ep', split_axis=0, concat_ax...  24.3 us
    dot_general x4, matrix products, expert_partial(): jnp.dot(hidden, down_weight, preferred_element_type=jnp.float32)  20.1 us
    all_to_all x2, starting transfers between devices, on_device(): lax.all_to_all(outgoing, 'ep', split_axis=0, concat_axis=0, tiled=True)  14.5 us
    all_to_all x2, starting transfers between devices, on_device(): lax.all_to_all(summed.astype(jnp.bfloat16), 'ep', split_axis=0, concat_ax...  12.6 us
    all_to_all x2, starting transfers between devices, from_everyone(): return lax.all_to_all(copies, axis, split_axis=0, concat_axis=0, tiled=True)  11.7 us
  transfers between devices with their start and end apart: 11, of which 8 were waited for; matrix products, arithmetic and copies ran while one was open for 32% of the time, Pallas kernels for 0%

commit v1 on v0

v1 whole, which is shorter than its diff:
```python
import jax
import jax.numpy as jnp
from jax import lax
from jax.experimental import pallas as pl
from jax.experimental.pallas import tpu as pltpu
from jax.sharding import PartitionSpec as P

epsilon = 1e-06

STEPS = 2
N_REP = 8
N_EP = 32
ROWS = 4
D = 4096
FR = 192
LOCAL = 2
EXPERTS = 64
CAP = 5
TOPK = 8
COLS = D // N_REP
LANES = 128
Q = COLS // LANES
SLOTS = LOCAL * CAP
CHUNK = Q * SLOTS
ALL_ROWS = N_REP * STEPS * ROWS
HALF = N_EP * CAP
GROUP = 16
GROUP_ROWS = GROUP * CHUNK
BLOCK = GROUP * CAP


SMEM = pl.BlockSpec(memory_space=pltpu.SMEM)
HBM = pl.BlockSpec(memory_space=pltpu.HBM)
bf16 = jnp.bfloat16
f32 = jnp.float32


def nt(a, b):
    return lax.dot_general(a, b, (((1,), (1,)), ((), ())), preferred_element_type=f32)


def nn(a, b):
    return lax.dot_general(a, b, (((1,), (0,)), ((), ())), preferred_element_type=f32)


def small_div(value, by):
    return (value * ((1 << 20) // by + 1)) >> 20


def whole(shape):
    return pl.BlockSpec(
        shape, lambda index: (0,) * len(shape), pipeline_mode=pl.Buffered(buffer_count=1)
    )


def call(kernel, out_shapes, operands, memory=None, scratch=(), limit=12, hbm=()):
    memory = memory or {}
    many = isinstance(out_shapes, (list, tuple))
    out_specs = [whole(each.shape) for each in out_shapes] if many else whole(out_shapes.shape)
    operands = [
        pltpu.with_memory_space_constraint(each, pltpu.HBM)
        if at in hbm or memory.get(at) is HBM
        else each
        for at, each in enumerate(operands)
    ]
    return pl.pallas_call(
        kernel,
        out_shape=out_shapes,
        grid=(1,),
        in_specs=[memory.get(at, whole(each.shape)) for at, each in enumerate(operands)],
        out_specs=out_specs,
        scratch_shapes=list(scratch),
        compiler_params=pltpu.CompilerParams(vmem_limit_bytes=limit << 20),
    )(*operands)


def norm_kernel(tokens, gain, out):
    parts = []
    for step in range(STEPS):
        widened = tokens[step].astype(f32)
        mean = jnp.mean(widened * widened, axis=-1, keepdims=True)
        parts.append(widened * lax.rsqrt(mean + epsilon) * gain[...])
    both = jnp.concatenate(parts, axis=0).astype(bf16)
    for part in range(N_REP):
        out[part] = both[:, part * COLS : (part + 1) * COLS]


def tables_kernel(ids, weights, send, keep_hi, keep_lo, sort, unsort):
    shares = weights[...] / jnp.sum(weights[...], axis=-1, keepdims=True)
    chosen = ids[...]
    expert = lax.broadcasted_iota(jnp.int32, (ALL_ROWS, EXPERTS), 1)
    member = jnp.zeros((ALL_ROWS, EXPERTS), f32)
    share = jnp.zeros((ALL_ROWS, EXPERTS), f32)
    for which in range(TOPK):
        hit = chosen[:, which : which + 1] == expert
        member = member + jnp.where(hit, 1.0, 0.0)
        share = share + jnp.where(hit, shares[:, which : which + 1], 0.0)
    row = lax.broadcasted_iota(jnp.int32, (ALL_ROWS, ALL_ROWS), 0)
    other = lax.broadcasted_iota(jnp.int32, (ALL_ROWS, ALL_ROWS), 1)
    earlier = (other < row) & (((row >> 2) & 1) == ((other >> 2) & 1))
    position = nn(jnp.where(earlier, 1.0, 0.0).astype(bf16), member.astype(bf16))
    position = jnp.where(member > 0.5, position, 100.0).astype(bf16)
    share_hi = share.astype(bf16)
    share_lo = (share - share_hi.astype(f32)).astype(bf16)
    position = jnp.concatenate([position] * Q, axis=0)
    share_hi = jnp.concatenate([share_hi] * Q, axis=0)
    share_lo = jnp.concatenate([share_lo] * Q, axis=0)

    def split(line, by_target):
        target = small_div(line, by_target)
        rest = line - target * by_target
        step = (rest >= CHUNK).astype(jnp.int32)
        rest = rest - step * CHUNK
        part = small_div(rest, SLOTS)
        slot = rest - part * SLOTS
        local = (slot >= CAP).astype(jnp.int32)
        return target * LOCAL + local, step, part, slot - local * CAP

    wide = 256

    def send_block(index, carry):
        at = pl.multiple_of(index * wide, wide)
        line = lax.broadcasted_iota(jnp.int32, (wide, 1), 0) + at
        bucket, step, part, place = split(line, 2 * CHUNK)
        pick = lax.broadcasted_iota(jnp.int32, (wide, EXPERTS), 1) == bucket
        found = nt(jnp.where(pick, 1.0, 0.0).astype(bf16), position)
        column = lax.broadcasted_iota(jnp.int32, (wide, Q * ALL_ROWS), 1)
        right = (found == place.astype(f32)) & (
            (column >> 6) * 2 + ((column >> 2) & 1) == part * 2 + step
        )
        send[pl.ds(at, wide), :] = jnp.where(right, 1.0, 0.0).astype(bf16)
        return carry

    lax.fori_loop(0, STEPS * N_EP * CHUNK // wide, send_block, 0)

    def keep_block(index, carry):
        at = pl.multiple_of(index * wide, wide)
        line = lax.broadcasted_iota(jnp.int32, (1, wide), 1) + at
        bucket, _, part, place = split(line, CHUNK)
        pick = lax.broadcasted_iota(jnp.int32, (EXPERTS, wide), 0) == bucket
        pick = jnp.where(pick, 1.0, 0.0).astype(bf16)
        found = nn(position, pick)
        high = nn(share_hi, pick)
        low = nn(share_lo, pick)
        line = lax.broadcasted_iota(jnp.int32, (Q * ALL_ROWS, wide), 0)
        right = (found == place.astype(f32)) & ((line >> 6) == part)
        for step in range(STEPS):
            now = right & (((line >> 2) & 1) == step)
            keep_hi[step, :, pl.ds(at, wide)] = jnp.where(now, high, 0.0).astype(bf16)
            keep_lo[step, :, pl.ds(at, wide)] = jnp.where(now, low, 0.0).astype(bf16)
        return carry

    lax.fori_loop(0, N_EP * CHUNK // wide, keep_block, 0)

    def stacked_from(line):
        part = small_div(line, 2 * BLOCK)
        rest = line - part * (2 * BLOCK)
        local = (rest >= BLOCK).astype(jnp.int32)
        rest = rest - local * BLOCK
        source = small_div(rest, CAP)
        place = rest - source * CAP
        return source * CHUNK + part * SLOTS + local * CAP + place

    across = stacked_from(lax.broadcasted_iota(jnp.int32, (1, GROUP_ROWS), 1))

    def sort_block(index, carry):
        at = pl.multiple_of(index * LANES, LANES)
        line = lax.broadcasted_iota(jnp.int32, (LANES, 1), 0) + at
        match = lax.broadcasted_iota(jnp.int32, (LANES, GROUP_ROWS), 1) == stacked_from(line)
        sort[pl.ds(at, LANES), :] = jnp.where(match, 1.0, 0.0).astype(bf16)
        unsort[pl.ds(at, LANES), :] = jnp.where(across == line, 1.0, 0.0).astype(bf16)
        return carry

    lax.fori_loop(0, GROUP_ROWS // LANES, sort_block, 0)


def send_kernel(rows, table, out):
    own = rows[...].reshape(ALL_ROWS, COLS)
    stacked = jnp.concatenate(
        [own[:, part * LANES : (part + 1) * LANES] for part in range(Q)], axis=0
    )
    out[...] = nn(table[...], stacked).astype(bf16)


def receive_kernel(step, arrived, table, out):
    for group in range(N_EP // GROUP):
        part = arrived[group * GROUP : (group + 1) * GROUP, step * CHUNK : (step + 1) * CHUNK, :]
        part = part.astype(f32).reshape(GROUP_ROWS, LANES).astype(bf16)
        sorted_rows = nn(table[...], part).astype(bf16)
        for piece in range(Q):
            for local in range(LOCAL):
                at = (piece * LOCAL + local) * BLOCK
                to = local * HALF + group * BLOCK
                out[to : to + BLOCK, piece * LANES : (piece + 1) * LANES] = sorted_rows[
                    at : at + BLOCK
                ]


def hidden_kernel(first, count, order, *refs):
    chunks = refs[:count]
    refs = refs[count:]
    before = None
    if first > 0:
        before, refs = refs[0], refs[1:]
    gate_all, up_all = refs[:2]
    outs = refs[2:-3]
    gate, up, sems = refs[-3:]

    def copies(index):
        at = pl.ds(pl.multiple_of(order[first + index] * COLS, COLS), COLS)
        return (
            pltpu.make_async_copy(gate_all.at[:, :, at], gate.at[index], sems.at[0, index]),
            pltpu.make_async_copy(up_all.at[:, :, at], up.at[index], sems.at[1, index]),
        )

    for index in range(count):
        for copy in copies(index):
            copy.start()
    if before is None:
        sums = [jnp.zeros((HALF, FR), f32) for _ in range(2 * LOCAL)]
    else:
        sums = [before[at] for at in range(2 * LOCAL)]
    for index in range(count):
        for copy in copies(index):
            copy.wait()
        for local in range(LOCAL):
            rows = chunks[index][local * HALF : (local + 1) * HALF, :]
            sums[2 * local] = sums[2 * local] + nt(rows, gate[index, local])
            sums[2 * local + 1] = sums[2 * local + 1] + nt(rows, up[index, local])
    if before is None:
        for at in range(2 * LOCAL):
            outs[0][at] = sums[at]
        return
    for local in range(LOCAL):
        value = (jax.nn.silu(sums[2 * local]) * sums[2 * local + 1]).astype(bf16)
        outs[0][:, local * FR : (local + 1) * FR] = value


def down_kernel(place, own, a, b, c, all_own, from_before, from_next, far_first, far_second, *refs):
    out, buffer, sems = refs
    mine = pl.ds(pl.multiple_of(place[0], COLS), COLS)
    inside = pl.ds(pl.multiple_of(place[1], COLS), COLS)
    copies = [
        pltpu.make_async_copy(all_own.at[:, :, mine], buffer.at[0], sems.at[0]),
        pltpu.make_async_copy(from_before.at[:, :, inside], buffer.at[1], sems.at[1]),
        pltpu.make_async_copy(from_next.at[:, :, inside], buffer.at[2], sems.at[2]),
        pltpu.make_async_copy(far_first.at[:, inside], buffer.at[3, 0], sems.at[3]),
        pltpu.make_async_copy(far_second.at[:, inside], buffer.at[3, 1], sems.at[4]),
    ]
    for copy in copies:
        copy.start()
    sums = [jnp.zeros((HALF, COLS), f32) for _ in range(LOCAL)]
    for index in range(4):
        copies[index].wait()
        if index == 3:
            copies[4].wait()
        units = (own, a, b, c)[index][...]
        for local in range(LOCAL):
            sums[local] = sums[local] + nn(
                units[:, local * FR : (local + 1) * FR], buffer[index, local]
            )
    for local in range(LOCAL):
        out[local * HALF : (local + 1) * HALF, :] = sums[local].astype(out.dtype)


def return_kernel(mine, other, table, out):
    total = (mine[...] + other[...].astype(f32)).astype(bf16)
    for group in range(N_EP // GROUP):
        pieces = []
        for piece in range(Q):
            for local in range(LOCAL):
                at = local * HALF + group * BLOCK
                pieces.append(total[at : at + BLOCK, piece * LANES : (piece + 1) * LANES])
        stacked = jnp.concatenate(pieces, axis=0)
        out[group * GROUP_ROWS : (group + 1) * GROUP_ROWS, :] = nn(table[...], stacked).astype(bf16)


def mix_kernel(first, second, high, low, out):
    total = jnp.zeros((Q * ALL_ROWS, LANES), f32)
    for step, back in enumerate((first, second)):
        rows = back[...]
        total = total + nn(high[step], rows) + nn(low[step], rows)
    total = total.astype(bf16)
    for part in range(Q):
        piece = total[part * ALL_ROWS : (part + 1) * ALL_ROWS]
        out[:, part * LANES : (part + 1) * LANES] = piece


def final_kernel(arrived, out):
    for part in range(N_REP):
        rows = arrived[part].astype(f32)
        for step in range(STEPS):
            out[step, :, part * COLS : (part + 1) * COLS] = rows[
                step * ROWS : (step + 1) * ROWS
            ].astype(bf16)


def rep_index(x, y):
    return (x % 4) * 2 + y % 2


NEXT = [(rep_index(x, y), rep_index(x + 1, y)) for x in range(4) for y in range(2)]
BEFORE = [(rep_index(x, y), rep_index(x - 1, y)) for x in range(4) for y in range(2)]
BESIDE = [(rep_index(x, y), rep_index(x, y + 1)) for x in range(4) for y in range(2)]


def go(value, pairs):
    return lax.ppermute(value, "rep", pairs)


def swap(value, axis):
    return lax.all_to_all(value, axis, split_axis=0, concat_axis=0, tiled=True)


def gathered(step, own):
    c = go(own, BESIDE)
    a = go(own, NEXT)
    b = go(own, BEFORE)
    if step == 0:
        f = go(a, NEXT)
    else:
        f = go(b, BEFORE)
    d = go(c, NEXT)
    e = go(c, BEFORE)
    k = go(f, BESIDE)
    return (own, a, b, c), (d, e, f, k)


def on_device(tokens, norm_gain, expert_ids, route_weights, w_gate, w_up, w_down):
    sds = jax.ShapeDtypeStruct
    me = lax.axis_index("rep")
    my_x = me // 2
    my_y = me % 2
    offset_x = jnp.array([0, 3, 1, 0, 3, 1, 2, 2], jnp.int32)
    offset_y = jnp.array([0, 0, 0, 1, 1, 1, 0, 1], jnp.int32)
    order = ((my_x + offset_x) % 4) * 2 + (my_y + offset_y) % 2
    here = jnp.arange(2, dtype=jnp.int32)
    place_mine = me * COLS * (1 - here) + my_y * COLS * here
    place_other = (me + 1 - 2 * my_y) * COLS * (1 - here) + (1 - my_y) * COLS * here

    normed = call(
        norm_kernel,
        sds((N_REP, STEPS * ROWS, COLS), bf16),
        (tokens.reshape(STEPS, ROWS, D), norm_gain.reshape(1, D)),
    )
    own = swap(normed, "rep")

    def slab(ahead, start, count):
        at = ((my_x + ahead) % 4) * 2 * COLS
        return lax.dynamic_slice(w_down, (start, 0, at), (count, FR, 2 * COLS))

    far = slab(2, 0, 1).reshape(FR, 2 * COLS), slab(2, 1, 1).reshape(FR, 2 * COLS)
    near = slab(1, 0, LOCAL), slab(3, 0, LOCAL)
    far, near, normed = lax.optimization_barrier((far, near, normed))
    far_first = go(far[0], NEXT)
    far_second = go(far[1], BEFORE)
    from_before = go(near[0], NEXT)
    from_next = go(near[1], BEFORE)
    far_first = go(far_first, NEXT)
    far_second = go(far_second, BEFORE)

    ids = expert_ids.reshape(STEPS, N_REP, ROWS, TOPK).swapaxes(0, 1).reshape(ALL_ROWS, TOPK)
    weights = route_weights.reshape(STEPS, N_REP, ROWS, TOPK).swapaxes(0, 1)
    send, keep_hi, keep_lo, sort, unsort = call(
        tables_kernel,
        [
            sds((STEPS * N_EP * CHUNK, Q * ALL_ROWS), bf16),
            sds((STEPS, Q * ALL_ROWS, N_EP * CHUNK), bf16),
            sds((STEPS, Q * ALL_ROWS, N_EP * CHUNK), bf16),
            sds((GROUP_ROWS, GROUP_ROWS), bf16),
            sds((GROUP_ROWS, GROUP_ROWS), bf16),
        ],
        (ids, weights.reshape(ALL_ROWS, TOPK)),
        limit=24,
    )

    outgoing = call(send_kernel, sds((STEPS * N_EP * CHUNK, LANES), bf16), (own, send), hbm=(1,))
    arrived = swap(outgoing.reshape(N_EP, STEPS * CHUNK, LANES), "ep")

    backs = []
    for step in range(STEPS):
        rows = call(
            lambda *refs, step=step: receive_kernel(step, *refs),
            sds((LOCAL * HALF, COLS), bf16),
            (arrived, sort),
            hbm=(1,),
        )
        sums = ()
        for first, parts in zip((0, 4), gathered(step, rows)):
            count = len(parts)
            operands = (order, *parts, *sums, w_gate, w_up)
            shape = sds((2 * LOCAL, HALF, FR), f32)
            if first > 0:
                shape = sds((HALF, LOCAL * FR), bf16)
            sums = [
                call(
                    lambda *refs, first=first, count=count: hidden_kernel(first, count, *refs),
                    shape,
                    operands,
                    memory={0: SMEM, len(operands) - 2: HBM, len(operands) - 1: HBM},
                    scratch=[
                        pltpu.VMEM((count, LOCAL, FR, COLS), bf16),
                        pltpu.VMEM((count, LOCAL, FR, COLS), bf16),
                        pltpu.SemaphoreType.DMA((2, count)),
                    ],
                    limit=16,
                )
            ]
        hidden = sums[0]
        a, b = go(hidden, NEXT), go(hidden, BEFORE)
        if step == 0:
            c = go(a, NEXT)
        else:
            c = go(b, BEFORE)

        def down(place, dtype):
            operands = (place, hidden, a, b, c, w_down)
            operands += (from_before, from_next, far_first, far_second)
            return call(
                down_kernel,
                sds((LOCAL * HALF, COLS), dtype),
                operands,
                memory={0: SMEM, **{at: HBM for at in range(5, 10)}},
                scratch=[
                    pltpu.VMEM((4, LOCAL, FR, COLS), bf16),
                    pltpu.SemaphoreType.DMA((5,)),
                ],
            )

        other = go(down(place_other, bf16), BESIDE)
        mine = down(place_mine, f32)
        results = call(
            return_kernel, sds((N_EP * CHUNK, LANES), bf16), (mine, other, unsort), hbm=(2,)
        )
        back = swap(results.reshape(N_EP, CHUNK, LANES), "ep")
        backs.append(back.reshape(N_EP * CHUNK, LANES))

    mixed = call(mix_kernel, sds((ALL_ROWS, COLS), bf16), (*backs, keep_hi, keep_lo), hbm=(2, 3))
    mixed = swap(mixed.reshape(N_REP, STEPS * ROWS, COLS), "rep")
    out = call(final_kernel, sds((STEPS, ROWS, D), bf16), (mixed,))
    return out[:, None, None]


def solution(mesh):
    return jax.shard_map(
        on_device,
        mesh=mesh,
        in_specs=(
            P(None, "ep", "rep", None, None),
            P(),
            P(None, "ep", None, None, None),
            P(None, "ep", None, None, None),
            P("ep", "rep", None),
            P("ep", "rep", None),
            P("ep", "rep", None),
        ),
        out_specs=P(None, "ep", "rep", None, None),
        check_vma=False,
    )
```

time: 306 us -> 218 us (0.71)
  local copies, waits for them, and re-layouts: 65.7 us -> 13.5 us
  waiting for transfers between devices: 118 us -> 67 us
  Pallas kernels: 0 us -> 42 us
  matrix products: 29.9 us -> 0 us
  blocking collectives: 8.95 us -> 36.2 us
  other arithmetic: 12.7 us -> 0.02 us
  starting transfers between devices: 67.8 us -> 57.7 us
    all_to_all x11 -> x3, waiting for transfers between devices: 118 us -> 15.1 us  [swap(): return lax.all_to_all(value, axis, split_axis=0, concat_axis=0, tiled=True)]
    ppermute x0 -> x28, waiting for transfers between devices: none -> 51.9 us  [go(): return lax.ppermute(value, 'rep', pairs)]
    all_to_all x11 -> x3, starting transfers between devices: 67.8 us -> 23 us  [swap(): return lax.all_to_all(value, axis, split_axis=0, concat_axis=0, tiled=True)]
    pallas_call x0 -> x17, Pallas kernels: none -> 42 us  [call(): pl.pallas_call(kernel, out_shape=out_shapes, grid=(1,), in_specs=[memory....]
    ppermute x0 -> x28, starting transfers between devices: none -> 34.6 us  [go(): return lax.ppermute(value, 'rep', pairs)]
    dot_general x8 -> x0, matrix products: 29.9 us -> none  [the longest x4 20.1 us: expert_partial(): jnp.dot(hidden, down_weight, preferred_element_type=jnp.float32)]
    all_to_all x1 -> x2, blocking collectives: 8.95 us -> 36.2 us  [swap(): return lax.all_to_all(value, axis, split_axis=0, concat_axis=0, tiled=True)]
    another operation x19 -> x0, local copies, waits for them, and re-layouts: 15.4 us -> none  [the longest x4 10.7 us: on_device(): slot_rows = arrived[:, local_slot].reshape(ep_size * capacity, model_width)]
  transfers between devices with their start and end apart: 11 -> 31, of which waited for: 8 -> 11; matrix products, arithmetic and copies ran while one was open for 32% -> 2% of each run, Pallas kernels for 0% -> 16%
where the time goes in v1:
time: 218 us; the launch traced here: 217 us
  waiting for transfers between devices  67 us (31%)
  starting transfers between devices  57.7 us (26%)
  Pallas kernels  42 us (19%)
  blocking collectives  36.2 us (17%)
  local copies, waits for them, and re-layouts  13.5 us (6%)
    ppermute x28, waiting for transfers between devices, go(): return lax.ppermute(value, 'rep', pairs)  51.9 us
    pallas_call x17, Pallas kernels, call(): pl.pallas_call(kernel, out_shape=out_shapes, grid=(1,), in_specs=[memory....  42 us
    all_to_all x2, blocking collectives, swap(): return lax.all_to_all(value, axis, split_axis=0, concat_axis=0, tiled=True)  36.2 us
    ppermute x28, starting transfers between devices, go(): return lax.ppermute(value, 'rep', pairs)  34.6 us
    all_to_all x3, starting transfers between devices, swap(): return lax.all_to_all(value, axis, split_axis=0, concat_axis=0, tiled=True)  23 us
    all_to_all x3, waiting for transfers between devices, swap(): return lax.all_to_all(value, axis, split_axis=0, concat_axis=0, tiled=True)  15.1 us
    unnamed x28, local copies, waits for them, and re-layouts  8.13 us
  transfers between devices with their start and end apart: 31, of which 11 were waited for; matrix products, arithmetic and copies ran while one was open for 2% of the time, Pallas kernels for 16%

profile of v1, /device:TPU:8, one launch (start us, length us, event | category | flops | bytes accessed | tf_op | source)
XLA Modules:
  0.0 216.7 jit_solution(1541557881773104382)
XLA Ops:
  2.3 5.8 %all-to-all-start = ((bf16[8,8,512]{2,1,0:T(8,128)(2,1)}), bf16[8,8,512]{2,1,0:T(8,128)(2,1)S(1)}, u32[]{:S(2)}, u32[]{:S(2)}) async-start(bf16[8,8,512]{2,1,0:T(8,128)(2,1)} %shard_map.91), calls=%async_computation | async-start | bytes 131072 | tf_op jit(solution)/shard_map/all_to_all | solution.py:312
  9.6 4.8 %shard_map.92 = (bf16[2560,256]{1,0:T(8,128)(2,1)S(1)}, bf16[2,256,1280]{2,1,0:T(8,128)(2,1)S(1)}, bf16[2,256,1280]{2,1,0:T(8,128)(2,1)S(1)}, bf16[640,640]{1,0:T(8,128)(2,1)S(1)}, bf16[640,640]{1,0:T(8,128)(2,1)S(1)}) custom-call(s32[64,8]{1,0:T(8,128)S(1)} %bitcast.27, f32[64,8]{1,0:T(8,128)S(1)} %bitcast.28), custom_call_target="tpu_custom_call" | custom-call | tf_op jit(solution)/shard_map/pallas_call | solution.py:66
  22.1 10.6 %all-to-all-start.1 = ((bf16[32,80,128]{2,1,0:T(8,128)(2,1)}), bf16[32,80,128]{2,1,0:T(8,128)(2,1)S(1)}, u32[]{:S(2)}, u32[]{:S(2)}) async-start(bf16[32,80,128]{2,1,0:T(8,128)(2,1)} %bitcast.8), calls=%async_computation.1 | async-start | bytes 1310720 | tf_op jit(solution)/shard_map/all_to_all | solution.py:312
  39.9 15.0 %all-to-all-done.1.refs_0_ = bf16[32,80,128]{2,1,0:T(8,128)(2,1)S(1)} async-done(((bf16[32,80,128]{2,1,0:T(8,128)(2,1)}), bf16[32,80,128]{2,1,0:T(8,128)(2,1)S(1)}, u32[]{:S(2)}, u32[]{:S(2)}) %all-to-all-start.1) | async-done | bytes 655392 | tf_op jit(solution)/shard_map/all_to_all | solution.py:312
  62.7 5.9 %collective-permute-done.3.refs_2_ = bf16[320,512]{1,0:T(8,128)(2,1)S(1)} collective-permute-done((bf16[320,512]{1,0:T(8,128)(2,1)S(1)}, bf16[320,512]{1,0:T(8,128)(2,1)S(1)}, u32[]{:S(2)}, u32[]{:S(2)}) %collective-permute-start.3) | collective-permute-done | bytes 327712 | tf_op jit(solution)/shard_map/ppermute | solution.py:308
  70.6 3.1 %collective-permute-start.20 = (bf16[320,512]{1,0:T(8,128)(2,1)S(1)}, bf16[320,512]{1,0:T(8,128)(2,1)S(1)}, u32[]{:S(2)}, u32[]{:S(2)}) collective-permute-start(bf16[320,512]{1,0:T(8,128)(2,1)S(1)} %shard_map.100.refs_1_), channel_id=1, source_target_pairs={{0,192},{32,224},{64,0},{96,32},{128,64},{160,96},{192,128},{224,1... | collective-permute-start | bytes 983048 | tf_op jit(solution)/shard_map/ppermute | solution.py:308
  74.0 3.1 %collective-permute-done.13.far_first = bf16[192,1024]{1,0:T(8,128)(2,1)S(1)} collective-permute-done((bf16[192,1024]{1,0:T(8,128)(2,1)}, bf16[192,1024]{1,0:T(8,128)(2,1)S(1)}, u32[]{:S(2)}, u32[]{:S(2)}) %collective-permute-start.13) | collective-permute-done | bytes 393248 | tf_op jit(solution)/shard_map/ppermute | solution.py:308
  78.8 5.3 %collective-permute-done.4.refs_3_ = bf16[320,512]{1,0:T(8,128)(2,1)S(1)} collective-permute-done((bf16[320,512]{1,0:T(8,128)(2,1)S(1)}, bf16[320,512]{1,0:T(8,128)(2,1)S(1)}, u32[]{:S(2)}, u32[]{:S(2)}) %collective-permute-start.4) | collective-permute-done | bytes 327712 | tf_op jit(solution)/shard_map/ppermute | solution.py:308
  88.3 17.1 %collective-permute-done.1.refs_1_ = bf16[320,512]{1,0:T(8,128)(2,1)S(1)} collective-permute-done((bf16[320,512]{1,0:T(8,128)(2,1)S(1)}, bf16[320,512]{1,0:T(8,128)(2,1)S(1)}, u32[]{:S(2)}, u32[]{:S(2)}) %collective-permute-start.1) | collective-permute-done | bytes 327712 | tf_op jit(solution)/shard_map/ppermute | solution.py:308
  108.9 3.2 %shard_map.95.refs_5_ = f32[4,160,192]{2,1,0:T(8,128)S(1)} custom-call(s32[8]{0:T(128)S(1)} %fusion.refs_0_, bf16[320,512]{1,0:T(8,128)(2,1)S(1)} %shard_map.94.refs_1_, bf16[320,512]{1,0:T(8,128)(2,1)S(1)} %collective-permute-done.3.refs_2_, bf16[320,512]{1,0:T(8,128)(2,1)S(1)} %collective-permute-done.6.refs_3_, ...), custom_call_target="tpu_custom_call" | custom-call | tf_op jit(solution)/shard_map/pallas_call | solution.py:66
  112.1 3.5 %shard_map.96.own = bf16[160,384]{1,0:T(8,128)(2,1)S(1)} custom-call(s32[8]{0:T(128)S(1)} %fusion.refs_0_, bf16[320,512]{1,0:T(8,128)(2,1)S(1)} %copy-done.8, bf16[320,512]{1,0:T(8,128)(2,1)S(1)} %collective-permute-done.2.refs_2_, bf16[320,512]{1,0:T(8,128)(2,1)S(1)} %copy-done.6, bf16[320,512]{1,0:T(8,128)(2,1)} %collective-permute-done.5.refs_4_, ...), custom_call_target="tpu_custom_call" | custom-call | tf_op jit(solution)/shard_map/pallas_call | solution.py:66
  116.0 3.0 %collective-permute-start.8 = (bf16[160,384]{1,0:T(8,128)(2,1)S(1)}, bf16[160,384]{1,0:T(8,128)(2,1)S(1)}, u32[]{:S(2)}, u32[]{:S(2)}) collective-permute-start(bf16[160,384]{1,0:T(8,128)(2,1)S(1)} %shard_map.96.own), channel_id=1, source_target_pairs={{0,192},{32,224},{64,0},{96,32},{128,64},{160,96},{192,128},{224,1... | collective-permute-start | bytes 368648 | tf_op jit(solution)/shard_map/ppermute | solution.py:308
  118.9 3.0 %collective-permute-done.7.a = bf16[160,384]{1,0:T(8,128)(2,1)S(1)} collective-permute-done((bf16[160,384]{1,0:T(8,128)(2,1)S(1)}, bf16[160,384]{1,0:T(8,128)(2,1)S(1)}, u32[]{:S(2)}, u32[]{:S(2)}) %collective-permute-start.7) | collective-permute-done | bytes 122912 | tf_op jit(solution)/shard_map/ppermute | solution.py:308
  122.0 6.1 %collective-permute-done.9.c = bf16[160,384]{1,0:T(8,128)(2,1)S(1)} collective-permute-done((bf16[160,384]{1,0:T(8,128)(2,1)S(1)}, bf16[160,384]{1,0:T(8,128)(2,1)S(1)}, u32[]{:S(2)}, u32[]{:S(2)}) %collective-permute-start.9) | collective-permute-done | bytes 122912 | tf_op jit(solution)/shard_map/ppermute | solution.py:308
  128.0 3.0 %shard_map.98 = bf16[320,512]{1,0:T(8,128)(2,1)} custom-call(s32[2]{0:T(128)S(1)} %multiply_add_fusion.place, bf16[160,384]{1,0:T(8,128)(2,1)S(1)} %shard_map.96.own, bf16[160,384]{1,0:T(8,128)(2,1)S(1)} %collective-permute-done.7.a, bf16[160,384]{1,0:T(8,128)(2,1)S(1)} %collective-permute-done.8.b, bf16[160,384]{1,0:T(8,128)(2,1)S(1)} %collective-permute-done.9.c, ...), custom_call_target="tpu_custom_call" | custom-call | tf_op jit(solution)/shard_map/pallas_call | solution.py:66
  132.1 3.2 %collective-permute-start.19 = (bf16[320,512]{1,0:T(8,128)(2,1)S(1)}, bf16[320,512]{1,0:T(8,128)(2,1)S(1)}, u32[]{:S(2)}, u32[]{:S(2)}) collective-permute-start(bf16[320,512]{1,0:T(8,128)(2,1)S(1)} %collective-permute-done.17.refs_4_), channel_id=1, source_target_pairs={{0,192},{32,224},{64,0},{96,32},{128,64},{160,96},{192,128},{224,1... | collective-permute-start | bytes 983048 | tf_op jit(solution)/shard_map/ppermute | solution.py:308
  142.0 6.7 %all-to-all-start.2 = ((bf16[32,40,128]{2,1,0:T(8,128)(2,1)}), bf16[32,40,128]{2,1,0:T(8,128)(2,1)S(1)}, u32[]{:S(2)}, u32[]{:S(2)}) async-start(bf16[32,40,128]{2,1,0:T(8,128)(2,1)} %bitcast.11), calls=%async_computation.2 | async-start | bytes 655360 | tf_op jit(solution)/shard_map/all_to_all | solution.py:312
  148.7 3.2 %shard_map.101.refs_5_ = f32[4,160,192]{2,1,0:T(8,128)S(1)} custom-call(s32[8]{0:T(128)S(1)} %fusion.refs_0_, bf16[320,512]{1,0:T(8,128)(2,1)S(1)} %shard_map.100.refs_1_, bf16[320,512]{1,0:T(8,128)(2,1)S(1)} %collective-permute-done.23.refs_2_, bf16[320,512]{1,0:T(8,128)(2,1)S(1)} %collective-permute-done.20.refs_3_, ...), custom_call_target="tpu_custom_call" | custom-call | tf_op jit(solution)/shard_map/pallas_call | solution.py:66
  152.0 3.1 %shard_map.102.own = bf16[160,384]{1,0:T(8,128)(2,1)S(1)} custom-call(s32[8]{0:T(128)S(1)} %fusion.refs_0_, bf16[320,512]{1,0:T(8,128)(2,1)S(1)} %collective-permute-done.18.refs_1_, bf16[320,512]{1,0:T(8,128)(2,1)S(1)} %collective-permute-done.19.refs_2_, bf16[320,512]{1,0:T(8,128)(2,1)S(1)} %collective-permute-done.21.refs_3_, ...), custom_call_target="tpu_custom_call" | custom-call | tf_op jit(solution)/shard_map/pallas_call | solution.py:66
  157.1 3.3 %collective-permute-done.25.b = bf16[160,384]{1,0:T(8,128)(2,1)S(1)} collective-permute-done((bf16[160,384]{1,0:T(8,128)(2,1)S(1)}, bf16[160,384]{1,0:T(8,128)(2,1)S(1)}, u32[]{:S(2)}, u32[]{:S(2)}) %collective-permute-start.25) | collective-permute-done | bytes 122912 | tf_op jit(solution)/shard_map/ppermute | solution.py:308
  161.9 3.4 %collective-permute-done.26.c = bf16[160,384]{1,0:T(8,128)(2,1)S(1)} collective-permute-done((bf16[160,384]{1,0:T(8,128)(2,1)S(1)}, bf16[160,384]{1,0:T(8,128)(2,1)S(1)}, u32[]{:S(2)}, u32[]{:S(2)}) %collective-permute-start.26) | collective-permute-done | bytes 122912 | tf_op jit(solution)/shard_map/ppermute | solution.py:308
  171.6 4.0 %collective-permute-done.27.other = bf16[320,512]{1,0:T(8,128)(2,1)S(1)} collective-permute-done((bf16[320,512]{1,0:T(8,128)(2,1)S(1)}, bf16[320,512]{1,0:T(8,128)(2,1)S(1)}, u32[]{:S(2)}, u32[]{:S(2)}) %collective-permute-start.27) | collective-permute-done | bytes 327712 | tf_op jit(solution)/shard_map/ppermute | solution.py:308
  177.4 25.2 %all_to_all.25 = bf16[32,40,128]{2,1,0:T(8,128)(2,1)S(1)} all-to-all(bf16[32,40,128]{2,1,0:T(8,128)(2,1)S(1)} %bitcast.25), channel_id=1, replica_groups=mesh['rep'=8,'ep'=32] {'ep'}, dimensions={0} | all-to-all | bytes 655360 | tf_op jit(solution)/shard_map/all_to_all | solution.py:312
  205.2 10.9 %all_to_all.26.arrived = bf16[8,8,512]{2,1,0:T(8,128)(2,1)S(1)} all-to-all(bf16[8,8,512]{2,1,0:T(8,128)(2,1)S(1)} %bitcast.26), channel_id=1, replica_groups=mesh['rep'=8,'ep'=32] {'rep'}, dimensions={0} | all-to-all | bytes 131072 | tf_op jit(solution)/shard_map/all_to_all | solution.py:312
  (92 shorter events, 60.9 us)
Async XLA Ops:
  2.3 17.1 %all-to-all-start = ((bf16[8,8,512]{2,1,0:T(8,128)(2,1)}), bf16[8,8,512]{2,1,0:T(8,128)(2,1)S(1)}, u32[]{:S(2)}, u32[]{:S(2)}) async-start(bf16[8,8,512]{2,1,0:T(8,128)(2,1)} %shard_map.91), calls=%async_computation | async-start | bytes 131072 | tf_op jit(solution)/shard_map/all_to_all | solution.py:312
  22.1 32.8 %all-to-all-start.1 = ((bf16[32,80,128]{2,1,0:T(8,128)(2,1)}), bf16[32,80,128]{2,1,0:T(8,128)(2,1)S(1)}, u32[]{:S(2)}, u32[]{:S(2)}) async-start(bf16[32,80,128]{2,1,0:T(8,128)(2,1)} %bitcast.8), calls=%async_computation.1 | async-start | bytes 1310720 | tf_op jit(solution)/shard_map/all_to_all | solution.py:312
  36.7 21.6 %collective-permute-start.12 = (bf16[192,1024]{1,0:T(8,128)(2,1)S(1)}, bf16[192,1024]{1,0:T(8,128)(2,1)}, u32[]{:S(2)}, u32[]{:S(2)}) collective-permute-start(bf16[192,1024]{1,0:T(8,128)(2,1)S(1)} %get-tuple-element.18), channel_id=1, source_target_pairs={{0,64},{32,96},{64,128},{96,160},{128,192},{160,224},{192,0},{224,... | collective-permute-start | bytes 1179656 | tf_op jit(solution)/shard_map/ppermute | solution.py:308
  38.2 32.4 %collective-permute-start.14 = (bf16[192,1024]{1,0:T(8,128)(2,1)S(1)}, bf16[192,1024]{1,0:T(8,128)(2,1)}, u32[]{:S(2)}, u32[]{:S(2)}) collective-permute-start(bf16[192,1024]{1,0:T(8,128)(2,1)S(1)} %get-tuple-element.19), channel_id=1, source_target_pairs={{0,192},{32,224},{64,0},{96,32},{128,64},{160,96},{192,128},{224,1... | collective-permute-start | bytes 1179656 | tf_op jit(solution)/shard_map/ppermute | solution.py:308
  56.7 11.9 %collective-permute-start.3 = (bf16[320,512]{1,0:T(8,128)(2,1)S(1)}, bf16[320,512]{1,0:T(8,128)(2,1)S(1)}, u32[]{:S(2)}, u32[]{:S(2)}) collective-permute-start(bf16[320,512]{1,0:T(8,128)(2,1)S(1)} %shard_map.94.refs_1_), channel_id=1, source_target_pairs={{0,64},{32,96},{64,128},{96,160},{128,192},{160,224},{192,0},{224,... | collective-permute-start | bytes 983048 | tf_op jit(solution)/shard_map/ppermute | solution.py:308
  58.3 18.8 %collective-permute-start.13 = (bf16[192,1024]{1,0:T(8,128)(2,1)}, bf16[192,1024]{1,0:T(8,128)(2,1)S(1)}, u32[]{:S(2)}, u32[]{:S(2)}) collective-permute-start(bf16[192,1024]{1,0:T(8,128)(2,1)} %collective-permute-done.12), channel_id=1, source_target_pairs={{0,64},{32,96},{64,128},{96,160},{128,192},{160,224},{192,0},{224,... | collective-permute-start | bytes 1179656 | tf_op jit(solution)/shard_map/ppermute | solution.py:308
  59.7 13.9 %collective-permute-start = (bf16[320,512]{1,0:T(8,128)(2,1)S(1)}, bf16[320,512]{1,0:T(8,128)(2,1)S(1)}, u32[]{:S(2)}, u32[]{:S(2)}) collective-permute-start(bf16[320,512]{1,0:T(8,128)(2,1)S(1)} %shard_map.94.refs_1_), channel_id=1, source_target_pairs={{0,32},{32,0},{64,96},{96,64},{128,160},{160,128},{192,224},{224,1... | collective-permute-start | bytes 983048 | tf_op jit(solution)/shard_map/ppermute | solution.py:308
  60.9 16.4 %collective-permute-start.6 = (bf16[320,512]{1,0:T(8,128)(2,1)S(1)}, bf16[320,512]{1,0:T(8,128)(2,1)S(1)}, u32[]{:S(2)}, u32[]{:S(2)}) collective-permute-start(bf16[320,512]{1,0:T(8,128)(2,1)S(1)} %shard_map.94.refs_1_), channel_id=1, source_target_pairs={{0,192},{32,224},{64,0},{96,32},{128,64},{160,96},{192,128},{224,1... | collective-permute-start | bytes 983048 | tf_op jit(solution)/shard_map/ppermute | solution.py:308
  68.6 15.4 %collective-permute-start.4 = (bf16[320,512]{1,0:T(8,128)(2,1)S(1)}, bf16[320,512]{1,0:T(8,128)(2,1)S(1)}, u32[]{:S(2)}, u32[]{:S(2)}) collective-permute-start(bf16[320,512]{1,0:T(8,128)(2,1)S(1)} %collective-permute-done.3.refs_2_), channel_id=1, source_target_pairs={{0,64},{32,96},{64,128},{96,160},{128,192},{160,224},{192,0},{224,... | collective-permute-start | bytes 983048 | tf_op jit(solution)/shard_map/ppermute | solution.py:308
  70.6 14.8 %collective-permute-start.20 = (bf16[320,512]{1,0:T(8,128)(2,1)S(1)}, bf16[320,512]{1,0:T(8,128)(2,1)S(1)}, u32[]{:S(2)}, u32[]{:S(2)}) collective-permute-start(bf16[320,512]{1,0:T(8,128)(2,1)S(1)} %shard_map.100.refs_1_), channel_id=1, source_target_pairs={{0,192},{32,224},{64,0},{96,32},{128,64},{160,96},{192,128},{224,1... | collective-permute-start | bytes 983048 | tf_op jit(solution)/shard_map/ppermute | solution.py:308
  73.7 13.8 %collective-permute-start.2 = (bf16[320,512]{1,0:T(8,128)(2,1)S(1)}, bf16[320,512]{1,0:T(8,128)(2,1)S(1)}, u32[]{:S(2)}, u32[]{:S(2)}) collective-permute-start(bf16[320,512]{1,0:T(8,128)(2,1)S(1)} %collective-permute-done.refs_4_), channel_id=1, source_target_pairs={{0,192},{32,224},{64,0},{96,32},{128,64},{160,96},{192,128},{224,1... | collective-permute-start | bytes 983048 | tf_op jit(solution)/shard_map/ppermute | solution.py:308
  77.0 38.9 %collective-permute-start.10 = (bf16[2,192,1024]{2,1,0:T(8,128)(2,1)}, bf16[2,192,1024]{2,1,0:T(8,128)(2,1)}, u32[]{:S(2)}, u32[]{:S(2)}) collective-permute-start(bf16[2,192,1024]{2,1,0:T(8,128)(2,1)} %get-tuple-element.16), channel_id=1, source_target_pairs={{0,64},{32,96},{64,128},{96,160},{128,192},{160,224},{192,0},{224,... | collective-permute-start | bytes 2359304 | tf_op jit(solution)/shard_map/ppermute | solution.py:308
  77.3 28.1 %collective-permute-start.1 = (bf16[320,512]{1,0:T(8,128)(2,1)S(1)}, bf16[320,512]{1,0:T(8,128)(2,1)S(1)}, u32[]{:S(2)}, u32[]{:S(2)}) collective-permute-start(bf16[320,512]{1,0:T(8,128)(2,1)S(1)} %collective-permute-done.refs_4_), channel_id=1, source_target_pairs={{0,64},{32,96},{64,128},{96,160},{128,192},{160,224},{192,0},{224,... | collective-permute-start | bytes 983048 | tf_op jit(solution)/shard_map/ppermute | solution.py:308
  84.0 23.0 %collective-permute-start.5 = (bf16[320,512]{1,0:T(8,128)(2,1)S(1)}, bf16[320,512]{1,0:T(8,128)(2,1)}, u32[]{:S(2)}, u32[]{:S(2)}) collective-permute-start(bf16[320,512]{1,0:T(8,128)(2,1)S(1)} %collective-permute-done.4.refs_3_), channel_id=1, source_target_pairs={{0,32},{32,0},{64,96},{96,64},{128,160},{160,128},{192,224},{224,1... | collective-permute-start | bytes 983048 | tf_op jit(solution)/shard_map/ppermute | solution.py:308
  85.4 36.5 %collective-permute-start.11 = (bf16[2,192,1024]{2,1,0:T(8,128)(2,1)}, bf16[2,192,1024]{2,1,0:T(8,128)(2,1)}, u32[]{:S(2)}, u32[]{:S(2)}) collective-permute-start(bf16[2,192,1024]{2,1,0:T(8,128)(2,1)} %get-tuple-element.17), channel_id=1, source_target_pairs={{0,192},{32,224},{64,0},{96,32},{128,64},{160,96},{192,128},{224,1... | collective-permute-start | bytes 2359304 | tf_op jit(solution)/shard_map/ppermute | solution.py:308
  87.5 28.1 %collective-permute-start.15 = (bf16[192,1024]{1,0:T(8,128)(2,1)}, bf16[192,1024]{1,0:T(8,128)(2,1)}, u32[]{:S(2)}, u32[]{:S(2)}) collective-permute-start(bf16[192,1024]{1,0:T(8,128)(2,1)} %collective-permute-done.14), channel_id=1, source_target_pairs={{0,192},{32,224},{64,0},{96,32},{128,64},{160,96},{192,128},{224,1... | collective-permute-start | bytes 1179656 | tf_op jit(solution)/shard_map/ppermute | solution.py:308
  106.2 25.9 %collective-permute-start.17 = (bf16[320,512]{1,0:T(8,128)(2,1)S(1)}, bf16[320,512]{1,0:T(8,128)(2,1)S(1)}, u32[]{:S(2)}, u32[]{:S(2)}) collective-permute-start(bf16[320,512]{1,0:T(8,128)(2,1)S(1)} %shard_map.100.refs_1_), channel_id=1, source_target_pairs={{0,32},{32,0},{64,96},{96,64},{128,160},{160,128},{192,224},{224,1... | collective-permute-start | bytes 983048 | tf_op jit(solution)/shard_map/ppermute | solution.py:308
  107.1 28.2 %collective-permute-start.21 = (bf16[320,512]{1,0:T(8,128)(2,1)S(1)}, bf16[320,512]{1,0:T(8,128)(2,1)S(1)}, u32[]{:S(2)}, u32[]{:S(2)}) collective-permute-start(bf16[320,512]{1,0:T(8,128)(2,1)S(1)} %collective-permute-done.20.refs_3_), channel_id=1, source_target_pairs={{0,192},{32,224},{64,0},{96,32},{128,64},{160,96},{192,128},{224,1... | collective-permute-start | bytes 983048 | tf_op jit(solution)/shard_map/ppermute | solution.py:308
  131.1 8.4 %collective-permute-start.16 = (bf16[320,512]{1,0:T(8,128)(2,1)}, bf16[320,512]{1,0:T(8,128)(2,1)}, u32[]{:S(2)}, u32[]{:S(2)}) collective-permute-start(bf16[320,512]{1,0:T(8,128)(2,1)} %shard_map.98), channel_id=1, source_target_pairs={{0,32},{32,0},{64,96},{96,64},{128,160},{160,128},{192,224},{224,1... | collective-permute-start | bytes 983048 | tf_op jit(solution)/shard_map/ppermute | solution.py:308
  132.1 16.7 %collective-permute-start.23 = (bf16[320,512]{1,0:T(8,128)(2,1)S(1)}, bf16[320,512]{1,0:T(8,128)(2,1)S(1)}, u32[]{:S(2)}, u32[]{:S(2)}) collective-permute-start(bf16[320,512]{1,0:T(8,128)(2,1)S(1)} %shard_map.100.refs_1_), channel_id=1, source_target_pairs={{0,64},{32,96},{64,128},{96,160},{128,192},{160,224},{192,0},{224,... | collective-permute-start | bytes 983048 | tf_op jit(solution)/shard_map/ppermute | solution.py:308
  132.1 19.9 %collective-permute-start.19 = (bf16[320,512]{1,0:T(8,128)(2,1)S(1)}, bf16[320,512]{1,0:T(8,128)(2,1)S(1)}, u32[]{:S(2)}, u32[]{:S(2)}) collective-permute-start(bf16[320,512]{1,0:T(8,128)(2,1)S(1)} %collective-permute-done.17.refs_4_), channel_id=1, source_target_pairs={{0,192},{32,224},{64,0},{96,32},{128,64},{160,96},{192,128},{224,1... | collective-permute-start | bytes 983048 | tf_op jit(solution)/shard_map/ppermute | solution.py:308
  135.3 16.7 %collective-permute-start.18 = (bf16[320,512]{1,0:T(8,128)(2,1)S(1)}, bf16[320,512]{1,0:T(8,128)(2,1)S(1)}, u32[]{:S(2)}, u32[]{:S(2)}) collective-permute-start(bf16[320,512]{1,0:T(8,128)(2,1)S(1)} %collective-permute-done.17.refs_4_), channel_id=1, source_target_pairs={{0,64},{32,96},{64,128},{96,160},{128,192},{160,224},{192,0},{224,... | collective-permute-start | bytes 983048 | tf_op jit(solution)/shard_map/ppermute | solution.py:308
  135.3 16.7 %collective-permute-start.22 = (bf16[320,512]{1,0:T(8,128)(2,1)S(1)}, bf16[320,512]{1,0:T(8,128)(2,1)S(1)}, u32[]{:S(2)}, u32[]{:S(2)}) collective-permute-start(bf16[320,512]{1,0:T(8,128)(2,1)S(1)} %collective-permute-done.21.refs_3_), channel_id=1, source_target_pairs={{0,32},{32,0},{64,96},{96,64},{128,160},{160,128},{192,224},{224,1... | collective-permute-start | bytes 983048 | tf_op jit(solution)/shard_map/ppermute | solution.py:308
  142.0 35.3 %all-to-all-start.2 = ((bf16[32,40,128]{2,1,0:T(8,128)(2,1)}), bf16[32,40,128]{2,1,0:T(8,128)(2,1)S(1)}, u32[]{:S(2)}, u32[]{:S(2)}) async-start(bf16[32,40,128]{2,1,0:T(8,128)(2,1)} %bitcast.11), calls=%async_computation.2 | async-start | bytes 655360 | tf_op jit(solution)/shard_map/all_to_all | solution.py:312
  (21 other events, 217.9 us)

commit v2 on v1

v2 whole, which is shorter than its diff:
```python
import jax
import jax.numpy as jnp
from jax import lax
from jax.experimental import pallas as pl
from jax.experimental.pallas import tpu as pltpu
from jax.sharding import PartitionSpec as P

epsilon = 1e-06

STEPS = 2
N_REP = 8
N_EP = 32
ROWS = 4
D = 4096
FR = 192
LOCAL = 2
EXPERTS = 64
CAP = 5
TOPK = 8
COLS = D // N_REP
LANES = 128
Q = COLS // LANES
SLOTS = LOCAL * CAP
CHUNK = Q * SLOTS
ALL_ROWS = N_REP * STEPS * ROWS
HALF = N_EP * CAP
GROUP = 16
GROUP_ROWS = GROUP * CHUNK
BLOCK = GROUP * CAP


SMEM = pl.BlockSpec(memory_space=pltpu.SMEM)
HBM = pl.BlockSpec(memory_space=pltpu.HBM)
bf16 = jnp.bfloat16
f32 = jnp.float32


def nt(a, b):
    return lax.dot_general(a, b, (((1,), (1,)), ((), ())), preferred_element_type=f32)


def nn(a, b):
    return lax.dot_general(a, b, (((1,), (0,)), ((), ())), preferred_element_type=f32)


def small_div(value, by):
    return (value * ((1 << 20) // by + 1)) >> 20


def whole(shape):
    return pl.BlockSpec(
        shape, lambda index: (0,) * len(shape), pipeline_mode=pl.Buffered(buffer_count=1)
    )


def call(kernel, out_shapes, operands, memory=None, scratch=(), limit=12, hbm=()):
    memory = memory or {}
    many = isinstance(out_shapes, (list, tuple))
    out_specs = [whole(each.shape) for each in out_shapes] if many else whole(out_shapes.shape)
    operands = [
        pltpu.with_memory_space_constraint(each, pltpu.HBM)
        if at in hbm or memory.get(at) is HBM
        else each
        for at, each in enumerate(operands)
    ]
    return pl.pallas_call(
        kernel,
        out_shape=out_shapes,
        grid=(1,),
        in_specs=[memory.get(at, whole(each.shape)) for at, each in enumerate(operands)],
        out_specs=out_specs,
        scratch_shapes=list(scratch),
        compiler_params=pltpu.CompilerParams(vmem_limit_bytes=limit << 20),
    )(*operands)


def norm_kernel(tokens, gain, out):
    parts = []
    for step in range(STEPS):
        widened = tokens[step].astype(f32)
        mean = jnp.mean(widened * widened, axis=-1, keepdims=True)
        parts.append(widened * lax.rsqrt(mean + epsilon) * gain[...])
    both = jnp.concatenate(parts, axis=0).astype(bf16)
    for part in range(N_REP):
        out[part] = both[:, part * COLS : (part + 1) * COLS]


def positions(ids):
    chosen = ids[...]
    expert = lax.broadcasted_iota(jnp.int32, (ALL_ROWS, EXPERTS), 1)
    hits = [chosen[:, which : which + 1] == expert for which in range(TOPK)]
    member = sum(jnp.where(hit, 1.0, 0.0) for hit in hits)
    row = lax.broadcasted_iota(jnp.int32, (ALL_ROWS, ALL_ROWS), 0)
    other = lax.broadcasted_iota(jnp.int32, (ALL_ROWS, ALL_ROWS), 1)
    earlier = (other < row) & (((row >> 2) & 1) == ((other >> 2) & 1))
    position = nn(jnp.where(earlier, 1.0, 0.0).astype(bf16), member.astype(bf16))
    position = jnp.where(member > 0.5, position, 100.0).astype(bf16)
    return hits, jnp.concatenate([position] * Q, axis=0)


WIDE = 256


def split(line):
    target = small_div(line, 2 * CHUNK)
    rest = line - target * (2 * CHUNK)
    step = (rest >= CHUNK).astype(jnp.int32)
    rest = rest - step * CHUNK
    part = small_div(rest, SLOTS)
    slot = rest - part * SLOTS
    local = (slot >= CAP).astype(jnp.int32)
    return target * LOCAL + local, part * 2 + step, (slot - local * CAP).astype(f32)


def send_table_kernel(ids, send):
    _, position = positions(ids)
    column = lax.broadcasted_iota(jnp.int32, (1, Q * ALL_ROWS), 1)
    column = (column >> 6) * 2 + ((column >> 2) & 1)

    def block(index, carry):
        at = pl.multiple_of(index * WIDE, WIDE)
        bucket, piece, place = split(lax.broadcasted_iota(jnp.int32, (WIDE, 1), 0) + at)
        pick = lax.broadcasted_iota(jnp.int32, (WIDE, EXPERTS), 1) == bucket
        found = nt(jnp.where(pick, 1.0, 0.0).astype(bf16), position)
        right = (found == place) & (column == piece)
        send[pl.ds(at, WIDE), :] = jnp.where(right, 1.0, 0.0).astype(bf16)
        return carry

    lax.fori_loop(0, STEPS * N_EP * CHUNK // WIDE, block, 0)


def tables_kernel(ids, weights, keep_hi, keep_lo, sort, unsort):
    hits, position = positions(ids)
    shares = weights[...] / jnp.sum(weights[...], axis=-1, keepdims=True)
    share = sum(
        jnp.where(hit, shares[:, which : which + 1], 0.0) for which, hit in enumerate(hits)
    )
    share_hi = share.astype(bf16)
    share_lo = (share - share_hi.astype(f32)).astype(bf16)
    share_hi = jnp.concatenate([share_hi] * Q, axis=0)
    share_lo = jnp.concatenate([share_lo] * Q, axis=0)

    row = lax.broadcasted_iota(jnp.int32, (Q * ALL_ROWS, 1), 0)
    row = (row >> 6) * 2 + ((row >> 2) & 1)

    def keep_block(index, carry):
        at = pl.multiple_of(index * WIDE, WIDE)
        bucket, piece, place = split(lax.broadcasted_iota(jnp.int32, (1, WIDE), 1) + at)
        pick = lax.broadcasted_iota(jnp.int32, (EXPERTS, WIDE), 0) == bucket
        pick = jnp.where(pick, 1.0, 0.0).astype(bf16)
        right = (nn(position, pick) == place) & (row == piece)
        keep_hi[:, pl.ds(at, WIDE)] = jnp.where(right, nn(share_hi, pick), 0.0).astype(bf16)
        keep_lo[:, pl.ds(at, WIDE)] = jnp.where(right, nn(share_lo, pick), 0.0).astype(bf16)
        return carry

    lax.fori_loop(0, STEPS * N_EP * CHUNK // WIDE, keep_block, 0)

    def stacked_from(line):
        part = small_div(line, 2 * BLOCK)
        rest = line - part * (2 * BLOCK)
        local = (rest >= BLOCK).astype(jnp.int32)
        rest = rest - local * BLOCK
        source = small_div(rest, CAP)
        place = rest - source * CAP
        return source * CHUNK + part * SLOTS + local * CAP + place

    across = stacked_from(lax.broadcasted_iota(jnp.int32, (1, GROUP_ROWS), 1))

    def sort_block(index, carry):
        at = pl.multiple_of(index * LANES, LANES)
        line = lax.broadcasted_iota(jnp.int32, (LANES, 1), 0) + at
        match = lax.broadcasted_iota(jnp.int32, (LANES, GROUP_ROWS), 1) == stacked_from(line)
        sort[pl.ds(at, LANES), :] = jnp.where(match, 1.0, 0.0).astype(bf16)
        unsort[pl.ds(at, LANES), :] = jnp.where(across == line, 1.0, 0.0).astype(bf16)
        return carry

    lax.fori_loop(0, GROUP_ROWS // LANES, sort_block, 0)


def send_kernel(rows, table, out):
    own = rows[...].reshape(ALL_ROWS, COLS)
    stacked = jnp.concatenate(
        [own[:, part * LANES : (part + 1) * LANES] for part in range(Q)], axis=0
    )
    out[...] = nn(table[...], stacked).astype(bf16)


def cut_kernel(places, weights, far_first, far_second, near_next, near_before, sems):
    def source(which):
        return pl.ds(pl.multiple_of(places[which], 2 * COLS), 2 * COLS)

    copies = [
        pltpu.make_async_copy(weights.at[0, :, source(0)], far_first, sems.at[0]),
        pltpu.make_async_copy(weights.at[1, :, source(0)], far_second, sems.at[1]),
        pltpu.make_async_copy(weights.at[:, :, source(1)], near_next, sems.at[2]),
        pltpu.make_async_copy(weights.at[:, :, source(2)], near_before, sems.at[3]),
    ]
    for copy in copies:
        copy.start()
    for copy in copies:
        copy.wait()


def receive_kernel(arrived, table, *outs):
    for step in range(STEPS):
        for group in range(N_EP // GROUP):
            part = arrived[
                group * GROUP : (group + 1) * GROUP, step * CHUNK : (step + 1) * CHUNK, :
            ]
            part = part.astype(f32).reshape(GROUP_ROWS, LANES).astype(bf16)
            sorted_rows = nn(table[...], part).astype(bf16)
            for piece in range(Q):
                for local in range(LOCAL):
                    at = (piece * LOCAL + local) * BLOCK
                    to = local * HALF + group * BLOCK
                    for out, shift in ((outs[step], 0), (outs[2], step * LOCAL * HALF)):
                        out[
                            shift + to : shift + to + BLOCK, piece * LANES : (piece + 1) * LANES
                        ] = sorted_rows[at : at + BLOCK]


def rows_of(refs, local):
    both = []
    for step in range(STEPS):
        if len(refs) == STEPS:
            both.append(refs[step][local * HALF : (local + 1) * HALF, :])
        else:
            at = (step * LOCAL + local) * HALF
            both.append(refs[0][at : at + HALF, :])
    return jnp.concatenate(both, axis=0)


def hidden_kernel(first, sizes, order, *refs):
    count = len(sizes)
    chunks = []
    for size in sizes:
        chunks.append(refs[:size])
        refs = refs[size:]
    before = None
    if first > 0:
        before, refs = refs[0], refs[1:]
    gate_all, up_all = refs[:2]
    outs = refs[2:-3]
    gate, up, sems = refs[-3:]

    def copies(index):
        at = pl.ds(pl.multiple_of(order[first + index] * COLS, COLS), COLS)
        return (
            pltpu.make_async_copy(gate_all.at[:, :, at], gate.at[index], sems.at[0, index]),
            pltpu.make_async_copy(up_all.at[:, :, at], up.at[index], sems.at[1, index]),
        )

    for index in range(count):
        for copy in copies(index):
            copy.start()
    sums = [None] * (2 * LOCAL)
    if before is not None:
        sums = [before[at] for at in range(2 * LOCAL)]
    for index in range(count):
        for copy in copies(index):
            copy.wait()
        for local in range(LOCAL):
            rows = rows_of(chunks[index], local)
            for which, weights in enumerate((gate, up)):
                at = 2 * local + which
                product = nt(rows, weights[index, local])
                sums[at] = product if sums[at] is None else sums[at] + product
    if before is None:
        for at in range(2 * LOCAL):
            outs[0][at] = sums[at]
        return
    for local in range(LOCAL):
        value = (jax.nn.silu(sums[2 * local]) * sums[2 * local + 1]).astype(bf16)
        for step in range(STEPS):
            outs[step][:, local * FR : (local + 1) * FR] = value[step * HALF : (step + 1) * HALF]


def down_kernel(place, *refs):
    units = [refs[2 * index : 2 * index + 2] for index in range(4)]
    all_own, from_before, from_next, far_first, far_second, out, buffer, sems = refs[8:]
    mine = pl.ds(pl.multiple_of(place[0], COLS), COLS)
    inside = pl.ds(pl.multiple_of(place[1], COLS), COLS)
    copies = [
        pltpu.make_async_copy(all_own.at[:, :, mine], buffer.at[0], sems.at[0]),
        pltpu.make_async_copy(from_before.at[:, :, inside], buffer.at[1], sems.at[1]),
        pltpu.make_async_copy(from_next.at[:, :, inside], buffer.at[2], sems.at[2]),
        pltpu.make_async_copy(far_first.at[:, inside], buffer.at[3, 0], sems.at[3]),
        pltpu.make_async_copy(far_second.at[:, inside], buffer.at[3, 1], sems.at[4]),
    ]
    for copy in copies:
        copy.start()
    sums = [None] * LOCAL
    for index in range(4):
        copies[index].wait()
        if index == 3:
            copies[4].wait()
        both = jnp.concatenate([units[index][step][...] for step in range(STEPS)], axis=0)
        for local in range(LOCAL):
            product = nn(both[:, local * FR : (local + 1) * FR], buffer[index, local])
            sums[local] = product if sums[local] is None else sums[local] + product
    for local in range(LOCAL):
        for step in range(STEPS):
            at = (step * LOCAL + local) * HALF
            out[at : at + HALF, :] = sums[local][step * HALF : (step + 1) * HALF].astype(out.dtype)


def return_kernel(mine, other, table, out):
    for step in range(STEPS):
        for group in range(N_EP // GROUP):
            pieces = []
            for piece in range(Q):
                for local in range(LOCAL):
                    at = (step * LOCAL + local) * HALF + group * BLOCK
                    span = (slice(at, at + BLOCK), slice(piece * LANES, (piece + 1) * LANES))
                    pieces.append((mine[span] + other[span].astype(f32)).astype(bf16))
            stacked = jnp.concatenate(pieces, axis=0)
            result = nn(table[...], stacked).reshape(GROUP, CHUNK, LANES).astype(bf16)
            out[group * GROUP : (group + 1) * GROUP, step * CHUNK : (step + 1) * CHUNK, :] = result


def mix_kernel(back, high, low, out):
    rows = back[...]
    total = (nn(high[...], rows) + nn(low[...], rows)).astype(bf16)
    for part in range(Q):
        piece = total[part * ALL_ROWS : (part + 1) * ALL_ROWS]
        out[:, part * LANES : (part + 1) * LANES] = piece


def final_kernel(arrived, out):
    for part in range(N_REP):
        rows = arrived[part].astype(f32)
        for step in range(STEPS):
            out[step, :, part * COLS : (part + 1) * COLS] = rows[
                step * ROWS : (step + 1) * ROWS
            ].astype(bf16)


def rep_index(x, y):
    return (x % 4) * 2 + y % 2


NEXT = [(rep_index(x, y), rep_index(x + 1, y)) for x in range(4) for y in range(2)]
BEFORE = [(rep_index(x, y), rep_index(x - 1, y)) for x in range(4) for y in range(2)]
BESIDE = [(rep_index(x, y), rep_index(x, y + 1)) for x in range(4) for y in range(2)]


def go(value, pairs):
    return lax.ppermute(value, "rep", pairs)


def swap(value, axis):
    return lax.all_to_all(value, axis, split_axis=0, concat_axis=0, tiled=True)


def gathered(own0, own1, both):
    c = go(both, BESIDE)
    a0 = go(own0, NEXT)
    b1 = go(own1, BEFORE)
    a1 = go(own1, NEXT)
    b0 = go(own0, BEFORE)
    f0 = go(a0, NEXT)
    f1 = go(b1, BEFORE)
    d = go(c, NEXT)
    e = go(c, BEFORE)
    k0 = go(f0, BESIDE)
    k1 = go(f1, BESIDE)
    return ((own0, own1), (a0, a1), (b0, b1), (c,)), ((d,), (e,), (f0, f1), (k0, k1))


def on_device(tokens, norm_gain, expert_ids, route_weights, w_gate, w_up, w_down):
    sds = jax.ShapeDtypeStruct
    me = lax.axis_index("rep")
    my_x = me // 2
    my_y = me % 2
    offset_x = jnp.array([0, 3, 1, 0, 3, 1, 2, 2], jnp.int32)
    offset_y = jnp.array([0, 0, 0, 1, 1, 1, 0, 1], jnp.int32)
    order = ((my_x + offset_x) % 4) * 2 + (my_y + offset_y) % 2
    here = jnp.arange(2, dtype=jnp.int32)
    place_mine = me * COLS * (1 - here) + my_y * COLS * here
    place_other = (me + 1 - 2 * my_y) * COLS * (1 - here) + (1 - my_y) * COLS * here

    normed = call(
        norm_kernel,
        sds((N_REP, STEPS * ROWS, COLS), bf16),
        (tokens.reshape(STEPS, ROWS, D), norm_gain.reshape(1, D)),
        hbm=(0, 1),
    )
    own = swap(normed, "rep")

    steps_ahead = jnp.array([2, 1, 3], jnp.int32)
    places = ((my_x + steps_ahead) % 4) * (2 * COLS)
    far_shape, near_shape = sds((FR, 2 * COLS), bf16), sds((LOCAL, FR, 2 * COLS), bf16)
    far_first, far_second, near_next, near_before = call(
        cut_kernel,
        [far_shape, far_shape, near_shape, near_shape],
        (places, w_down),
        memory={0: SMEM, 1: HBM},
        scratch=[pltpu.SemaphoreType.DMA((4,))],
    )
    far_first = go(far_first, NEXT)
    far_second = go(far_second, BEFORE)
    from_before = go(near_next, NEXT)
    from_next = go(near_before, BEFORE)
    far_first = go(far_first, NEXT)
    far_second = go(far_second, BEFORE)

    ids = expert_ids.reshape(STEPS, N_REP, ROWS, TOPK).swapaxes(0, 1).reshape(ALL_ROWS, TOPK)
    weights = route_weights.reshape(STEPS, N_REP, ROWS, TOPK).swapaxes(0, 1)
    weights = weights.reshape(ALL_ROWS, TOPK)
    slots = STEPS * N_EP * CHUNK
    send = call(send_table_kernel, sds((slots, Q * ALL_ROWS), bf16), (ids,))
    keep_hi, keep_lo, sort, unsort = call(
        tables_kernel,
        [
            sds((Q * ALL_ROWS, slots), bf16),
            sds((Q * ALL_ROWS, slots), bf16),
            sds((GROUP_ROWS, GROUP_ROWS), bf16),
            sds((GROUP_ROWS, GROUP_ROWS), bf16),
        ],
        (ids, weights),
    )

    outgoing = call(send_kernel, sds((slots, LANES), bf16), (own, send))
    arrived = swap(outgoing.reshape(N_EP, STEPS * CHUNK, LANES), "ep")

    one, two = sds((LOCAL * HALF, COLS), bf16), sds((STEPS * LOCAL * HALF, COLS), bf16)
    rows = call(receive_kernel, [one, one, two], (arrived, sort))
    sums = ()
    for first, parts in zip((0, 4), gathered(*rows)):
        sizes = tuple(len(part) for part in parts)
        chunks = tuple(each for part in parts for each in part)
        operands = (order, *chunks, *sums, w_gate, w_up)
        shapes = [sds((2 * LOCAL, STEPS * HALF, FR), f32)]
        if first > 0:
            shapes = [sds((HALF, LOCAL * FR), bf16)] * STEPS
        sums = call(
            lambda *refs, first=first, sizes=sizes: hidden_kernel(first, sizes, *refs),
            shapes,
            operands,
            memory={0: SMEM, len(operands) - 2: HBM, len(operands) - 1: HBM},
            scratch=[
                pltpu.VMEM((4, LOCAL, FR, COLS), bf16),
                pltpu.VMEM((4, LOCAL, FR, COLS), bf16),
                pltpu.SemaphoreType.DMA((2, 4)),
            ],
            limit=20,
        )
    hidden0, hidden1 = sums
    a0, b1 = go(hidden0, NEXT), go(hidden1, BEFORE)
    a1, b0 = go(hidden1, NEXT), go(hidden0, BEFORE)
    c0, c1 = go(a0, NEXT), go(b1, BEFORE)
    units = (hidden0, hidden1, a0, a1, b0, b1, c0, c1)

    def down(place, dtype):
        operands = (place, *units, w_down, from_before, from_next, far_first, far_second)
        return call(
            down_kernel,
            sds((STEPS * LOCAL * HALF, COLS), dtype),
            operands,
            memory={0: SMEM, **{at: HBM for at in range(9, 14)}},
            scratch=[
                pltpu.VMEM((4, LOCAL, FR, COLS), bf16),
                pltpu.SemaphoreType.DMA((5,)),
            ],
        )

    other = go(down(place_other, bf16), BESIDE)
    mine = down(place_mine, f32)
    back = call(return_kernel, sds((N_EP, STEPS * CHUNK, LANES), bf16), (mine, other, unsort))
    back = swap(back, "ep").reshape(slots, LANES)
    mixed = call(mix_kernel, sds((ALL_ROWS, COLS), bf16), (back, keep_hi, keep_lo), hbm=(1, 2))
    mixed = swap(mixed.reshape(N_REP, STEPS * ROWS, COLS), "rep")
    out = call(final_kernel, sds((STEPS, ROWS, D), bf16), (mixed,))
    return out[:, None, None]


def solution(mesh):
    return jax.shard_map(
        on_device,
        mesh=mesh,
        in_specs=(
            P(None, "ep", "rep", None, None),
            P(),
            P(None, "ep", None, None, None),
            P(None, "ep", None, None, None),
            P("ep", "rep", None),
            P("ep", "rep", None),
            P("ep", "rep", None),
        ),
        out_specs=P(None, "ep", "rep", None, None),
        check_vma=False,
    )
```

time: 218 us -> 198 us (0.908)
  starting transfers between devices: 57.7 us -> 44.5 us
  Pallas kernels: 42 us -> 30 us
  blocking collectives: 36.2 us -> 40.2 us
    pallas_call x17 -> x13, Pallas kernels: 42 us -> 30 us  [call(): pl.pallas_call(kernel, out_shape=out_shapes, grid=(1,), in_specs=[memory....]
    ppermute x28 -> x24, starting transfers between devices: 34.6 us -> 28 us  [go(): return lax.ppermute(value, 'rep', pairs)]
    all_to_all x3 -> x2, starting transfers between devices: 23 us -> 16.5 us  [swap(): return lax.all_to_all(value, axis, split_axis=0, concat_axis=0, tiled=True)]
    unnamed x28 -> x48, local copies, waits for them, and re-layouts: 8.13 us -> 13 us
    all_to_all x2, blocking collectives: 36.2 us -> 40.2 us  [swap(): return lax.all_to_all(value, axis, split_axis=0, concat_axis=0, tiled=True)]
    all_to_all x3 -> x2, waiting for transfers between devices: 15.1 us -> 18.3 us  [swap(): return lax.all_to_all(value, axis, split_axis=0, concat_axis=0, tiled=True)]
    dynamic_slice x1 -> x0, local copies, waits for them, and re-layouts: 2.69 us -> none  [slab(): return lax.dynamic_slice(w_down, (start, 0, at), (count, FR, 2 * COLS))]
    ppermute x28 -> x24, waiting for transfers between devices: 51.9 us -> 49.7 us  [go(): return lax.ppermute(value, 'rep', pairs)]
  transfers between devices with their start and end apart: 31 -> 26, of which waited for: 11 -> 12; matrix products, arithmetic and copies ran while one was open for 2% -> 0% of each run, Pallas kernels for 16% -> 10%
where the time goes in v2:
time: 198 us; the launch traced here: 197 us
  waiting for transfers between devices  68.1 us (34%)
  starting transfers between devices  44.5 us (22%)
  blocking collectives  40.2 us (20%)
  Pallas kernels  30 us (15%)
  local copies, waits for them, and re-layouts  13.7 us (7%)
    ppermute x24, waiting for transfers between devices, go(): return lax.ppermute(value, 'rep', pairs)  49.7 us
    all_to_all x2, blocking collectives, swap(): return lax.all_to_all(value, axis, split_axis=0, concat_axis=0, tiled=True)  40.2 us
    pallas_call x13, Pallas kernels, call(): pl.pallas_call(kernel, out_shape=out_shapes, grid=(1,), in_specs=[memory....  30 us
    ppermute x24, starting transfers between devices, go(): return lax.ppermute(value, 'rep', pairs)  28 us
    all_to_all x2, waiting for transfers between devices, swap(): return lax.all_to_all(value, axis, split_axis=0, concat_axis=0, tiled=True)  18.3 us
    all_to_all x2, starting transfers between devices, swap(): return lax.all_to_all(value, axis, split_axis=0, concat_axis=0, tiled=True)  16.5 us
    unnamed x48, local copies, waits for them, and re-layouts  13 us
  transfers between devices with their start and end apart: 26, of which 12 were waited for; matrix products, arithmetic and copies ran while one was open for 0% of the time, Pallas kernels for 10%

profile of v2, /device:TPU:8, one launch (start us, length us, event | category | flops | bytes accessed | tf_op | source)
XLA Modules:
  0.0 196.7 jit_solution(15246559142728834826)
XLA Ops:
  1.6 5.8 %all-to-all-start = ((bf16[8,8,512]{2,1,0:T(8,128)(2,1)}), bf16[8,8,512]{2,1,0:T(8,128)(2,1)S(1)}, u32[]{:S(2)}, u32[]{:S(2)}) async-start(bf16[8,8,512]{2,1,0:T(8,128)(2,1)} %shard_map.100), calls=%async_computation | async-start | bytes 131072 | tf_op jit(solution)/shard_map/all_to_all | solution.py:352
  8.1 2.6 %shard_map.101.table = bf16[2560,256]{1,0:T(8,128)(2,1)S(1)} custom-call(s32[64,8]{1,0:T(8,128)S(1)} %bitcast.17), custom_call_target="tpu_custom_call" | custom-call | tf_op jit(solution)/shard_map/pallas_call | solution.py:66
  13.8 10.7 %all-to-all-start.1 = ((bf16[32,80,128]{2,1,0:T(8,128)(2,1)}), bf16[32,80,128]{2,1,0:T(8,128)(2,1)S(1)}, u32[]{:S(2)}, u32[]{:S(2)}) async-start(bf16[32,80,128]{2,1,0:T(8,128)(2,1)} %bitcast.5), calls=%async_computation.1 | async-start | bytes 1310720 | tf_op jit(solution)/shard_map/all_to_all | solution.py:352
  24.6 3.4 %shard_map.103 = (bf16[256,2560]{1,0:T(8,128)(2,1)S(1)}, bf16[256,2560]{1,0:T(8,128)(2,1)S(1)}, bf16[640,640]{1,0:T(8,128)(2,1)S(1)}, bf16[640,640]{1,0:T(8,128)(2,1)S(1)}) custom-call(s32[64,8]{1,0:T(8,128)S(1)} %bitcast.18, f32[64,8]{1,0:T(8,128)S(1)} %bitcast.20), custom_call_target="tpu_custom_call" | custom-call | tf_op jit(solution)/shard_map/pallas_call | solution.py:66
  30.2 16.6 %all-to-all-done.1.arrived = bf16[32,80,128]{2,1,0:T(8,128)(2,1)S(1)} async-done(((bf16[32,80,128]{2,1,0:T(8,128)(2,1)}), bf16[32,80,128]{2,1,0:T(8,128)(2,1)S(1)}, u32[]{:S(2)}, u32[]{:S(2)}) %all-to-all-start.1) | async-done | bytes 655392 | tf_op jit(solution)/shard_map/all_to_all | solution.py:352
  50.3 3.4 %shard_map.107 = (bf16[192,1024]{1,0:T(8,128)(2,1)S(1)}, bf16[192,1024]{1,0:T(8,128)(2,1)S(1)}, bf16[2,192,1024]{2,1,0:T(8,128)(2,1)}, bf16[2,192,1024]{2,1,0:T(8,128)(2,1)}) custom-call(s32[3]{0:T(128)S(1)} %fusion.5.places, bf16[2,192,4096]{2,1,0:T(8,128)(2,1)} %refs_8_.7), custom_call_target="tpu_custom_call" | custom-call | tf_op jit(solution)/shard_map/pallas_call | solution.py:66
  54.5 2.5 %collective-permute-start.21 = (bf16[192,1024]{1,0:T(8,128)(2,1)S(1)}, bf16[192,1024]{1,0:T(8,128)(2,1)}, u32[]{:S(2)}, u32[]{:S(2)}) collective-permute-start(bf16[192,1024]{1,0:T(8,128)(2,1)S(1)} %get-tuple-element.27), channel_id=1, source_target_pairs={{0,192},{32,224},{64,0},{96,32},{128,64},{160,96},{192,128},{224,1... | collective-permute-start | bytes 1179656 | tf_op jit(solution)/shard_map/ppermute | solution.py:348
  59.8 10.9 %collective-permute-done.5.refs_6_ = bf16[320,512]{1,0:T(8,128)(2,1)S(1)} collective-permute-done((bf16[320,512]{1,0:T(8,128)(2,1)S(1)}, bf16[320,512]{1,0:T(8,128)(2,1)S(1)}, u32[]{:S(2)}, u32[]{:S(2)}) %collective-permute-start.5) | collective-permute-done | bytes 327712 | tf_op jit(solution)/shard_map/ppermute | solution.py:348
  70.6 3.2 %collective-permute-start.6 = (bf16[320,512]{1,0:T(8,128)(2,1)S(1)}, bf16[320,512]{1,0:T(8,128)(2,1)S(1)}, u32[]{:S(2)}, u32[]{:S(2)}) collective-permute-start(bf16[320,512]{1,0:T(8,128)(2,1)S(1)} %collective-permute-done.5.refs_6_), channel_id=1, source_target_pairs={{0,192},{32,224},{64,0},{96,32},{128,64},{160,96},{192,128},{224,1... | collective-permute-start | bytes 983048 | tf_op jit(solution)/shard_map/ppermute | solution.py:348
  77.7 3.5 %collective-permute-done.6.refs_4_ = bf16[320,512]{1,0:T(8,128)(2,1)S(1)} collective-permute-done((bf16[320,512]{1,0:T(8,128)(2,1)S(1)}, bf16[320,512]{1,0:T(8,128)(2,1)S(1)}, u32[]{:S(2)}, u32[]{:S(2)}) %collective-permute-start.6) | collective-permute-done | bytes 327712 | tf_op jit(solution)/shard_map/ppermute | solution.py:348
  82.4 2.4 %collective-permute-done.10.refs_5_ = bf16[320,512]{1,0:T(8,128)(2,1)S(1)} collective-permute-done((bf16[320,512]{1,0:T(8,128)(2,1)S(1)}, bf16[320,512]{1,0:T(8,128)(2,1)S(1)}, u32[]{:S(2)}, u32[]{:S(2)}) %collective-permute-start.10) | collective-permute-done | bytes 327712 | tf_op jit(solution)/shard_map/ppermute | solution.py:348
  93.5 7.8 %collective-permute-done.1.refs_1_ = bf16[640,512]{1,0:T(8,128)(2,1)S(1)} collective-permute-done((bf16[640,512]{1,0:T(8,128)(2,1)S(1)}, bf16[640,512]{1,0:T(8,128)(2,1)S(1)}, u32[]{:S(2)}, u32[]{:S(2)}) %collective-permute-start.1) | collective-permute-done | bytes 655392 | tf_op jit(solution)/shard_map/ppermute | solution.py:348
  106.2 3.6 %shard_map.105.refs_7_ = f32[4,320,192]{2,1,0:T(8,128)S(1)} custom-call(s32[8]{0:T(128)S(1)} %fusion.refs_0_, bf16[320,512]{1,0:T(8,128)(2,1)S(1)} %get-tuple-element.20.refs_1_, bf16[320,512]{1,0:T(8,128)(2,1)S(1)} %copy-done.3, bf16[320,512]{1,0:T(8,128)(2,1)S(1)} %copy-done.5, bf16[320,512]{1,0:T(8,128)(2,1)S(1)} %copy-done.15, ...), custom_call_target="tpu_custom_call" | custom-call | tf_op jit(solution)/shard_map/pallas_call | solution.py:66
  109.9 3.6 %shard_map.106 = (bf16[160,384]{1,0:T(8,128)(2,1)S(1)}, bf16[160,384]{1,0:T(8,128)(2,1)S(1)}) custom-call(s32[8]{0:T(128)S(1)} %fusion.refs_0_, bf16[640,512]{1,0:T(8,128)(2,1)S(1)} %collective-permute-done.1.refs_1_, bf16[640,512]{1,0:T(8,128)(2,1)S(1)} %collective-permute-done.2.refs_2_, bf16[320,512]{1,0:T(8,128)(2,1)S(1)} %copy-done.7, ...), custom_call_target="tpu_custom_call" | custom-call | tf_op jit(solution)/shard_map/pallas_call | solution.py:66
  115.6 7.2 %collective-permute-done.20.refs_11_ = bf16[192,1024]{1,0:T(8,128)(2,1)} collective-permute-done((bf16[192,1024]{1,0:T(8,128)(2,1)}, bf16[192,1024]{1,0:T(8,128)(2,1)}, u32[]{:S(2)}, u32[]{:S(2)}) %collective-permute-start.20) | collective-permute-done | bytes 393248 | tf_op jit(solution)/shard_map/ppermute | solution.py:348
  122.7 6.3 %collective-permute-done.22.refs_12_ = bf16[192,1024]{1,0:T(8,128)(2,1)} collective-permute-done((bf16[192,1024]{1,0:T(8,128)(2,1)}, bf16[192,1024]{1,0:T(8,128)(2,1)}, u32[]{:S(2)}, u32[]{:S(2)}) %collective-permute-start.22) | collective-permute-done | bytes 393248 | tf_op jit(solution)/shard_map/ppermute | solution.py:348
  133.0 3.0 %collective-permute-start.16 = (bf16[160,384]{1,0:T(8,128)(2,1)S(1)}, bf16[160,384]{1,0:T(8,128)(2,1)S(1)}, u32[]{:S(2)}, u32[]{:S(2)}) collective-permute-start(bf16[160,384]{1,0:T(8,128)(2,1)S(1)} %collective-permute-done.14.refs_5_), channel_id=1, source_target_pairs={{0,192},{32,224},{64,0},{96,32},{128,64},{160,96},{192,128},{224,1... | collective-permute-start | bytes 368648 | tf_op jit(solution)/shard_map/ppermute | solution.py:348
  136.0 2.8 %collective-permute-done.15.refs_6_ = bf16[160,384]{1,0:T(8,128)(2,1)S(1)} collective-permute-done((bf16[160,384]{1,0:T(8,128)(2,1)S(1)}, bf16[160,384]{1,0:T(8,128)(2,1)S(1)}, u32[]{:S(2)}, u32[]{:S(2)}) %collective-permute-start.15) | collective-permute-done | bytes 122912 | tf_op jit(solution)/shard_map/ppermute | solution.py:348
  138.8 2.6 %shard_map.109 = bf16[640,512]{1,0:T(8,128)(2,1)S(1)} custom-call(s32[2]{0:T(128)S(1)} %multiply_add_fusion.place, bf16[160,384]{1,0:T(8,128)(2,1)S(1)} %get-tuple-element.22.refs_0_, bf16[160,384]{1,0:T(8,128)(2,1)S(1)} %get-tuple-element.23.refs_1_, bf16[160,384]{1,0:T(8,128)(2,1)S(1)} %collective-permute-done.11.refs_2_, ...), custom_call_target="tpu_custom_call" | custom-call | tf_op jit(solution)/shard_map/pallas_call | solution.py:66
  142.1 2.6 %shard_map.108.mine = f32[640,512]{1,0:T(8,128)S(1)} custom-call(s32[2]{0:T(128)S(1)} %multiply_add_fusion.1.place, bf16[160,384]{1,0:T(8,128)(2,1)S(1)} %get-tuple-element.22.refs_0_, bf16[160,384]{1,0:T(8,128)(2,1)S(1)} %get-tuple-element.23.refs_1_, bf16[160,384]{1,0:T(8,128)(2,1)S(1)} %collective-permute-done.11.refs_2_, ...), custom_call_target="tpu_custom_call" | custom-call | tf_op jit(solution)/shard_map/pallas_call | solution.py:66
  144.8 7.6 %collective-permute-done.23.other = bf16[640,512]{1,0:T(8,128)(2,1)S(1)} collective-permute-done((bf16[640,512]{1,0:T(8,128)(2,1)S(1)}, bf16[640,512]{1,0:T(8,128)(2,1)S(1)}, u32[]{:S(2)}, u32[]{:S(2)}) %collective-permute-start.23) | collective-permute-done | bytes 655392 | tf_op jit(solution)/shard_map/ppermute | solution.py:348
  153.4 29.4 %all_to_all.20 = bf16[32,80,128]{2,1,0:T(8,128)(2,1)S(1)} all-to-all(bf16[32,80,128]{2,1,0:T(8,128)(2,1)S(1)} %shard_map.110), channel_id=1, replica_groups=mesh['rep'=8,'ep'=32] {'ep'}, dimensions={0} | all-to-all | bytes 1310720 | tf_op jit(solution)/shard_map/all_to_all | solution.py:352
  182.7 2.5 %shard_map.111 = bf16[64,512]{1,0:T(8,128)(2,1)S(1)} custom-call(bf16[2560,128]{1,0:T(8,128)(2,1)S(1)} %bitcast.16, bf16[256,2560]{1,0:T(8,128)(2,1)} %copy-done, bf16[256,2560]{1,0:T(8,128)(2,1)} %copy-done.1), custom_call_target="tpu_custom_call" | custom-call | tf_op jit(solution)/shard_map/pallas_call | solution.py:66
  185.3 10.8 %all_to_all.21.arrived = bf16[8,8,512]{2,1,0:T(8,128)(2,1)S(1)} all-to-all(bf16[8,8,512]{2,1,0:T(8,128)(2,1)S(1)} %bitcast.19), channel_id=1, replica_groups=mesh['rep'=8,'ep'=32] {'rep'}, dimensions={0} | all-to-all | bytes 131072 | tf_op jit(solution)/shard_map/all_to_all | solution.py:352
  (97 shorter events, 41.6 us)
Async XLA Ops:
  1.6 10.8 %all-to-all-start = ((bf16[8,8,512]{2,1,0:T(8,128)(2,1)}), bf16[8,8,512]{2,1,0:T(8,128)(2,1)S(1)}, u32[]{:S(2)}, u32[]{:S(2)}) async-start(bf16[8,8,512]{2,1,0:T(8,128)(2,1)} %shard_map.100), calls=%async_computation | async-start | bytes 131072 | tf_op jit(solution)/shard_map/all_to_all | solution.py:352
  13.8 33.0 %all-to-all-start.1 = ((bf16[32,80,128]{2,1,0:T(8,128)(2,1)}), bf16[32,80,128]{2,1,0:T(8,128)(2,1)S(1)}, u32[]{:S(2)}, u32[]{:S(2)}) async-start(bf16[32,80,128]{2,1,0:T(8,128)(2,1)} %bitcast.5), calls=%async_computation.1 | async-start | bytes 1310720 | tf_op jit(solution)/shard_map/all_to_all | solution.py:352
  47.8 11.1 %collective-permute-start.3 = (bf16[320,512]{1,0:T(8,128)(2,1)S(1)}, bf16[320,512]{1,0:T(8,128)(2,1)S(1)}, u32[]{:S(2)}, u32[]{:S(2)}) collective-permute-start(bf16[320,512]{1,0:T(8,128)(2,1)S(1)} %get-tuple-element.20.refs_1_), channel_id=1, source_target_pairs={{0,64},{32,96},{64,128},{96,160},{128,192},{160,224},{192,0},{224,... | collective-permute-start | bytes 983048 | tf_op jit(solution)/shard_map/ppermute | solution.py:348
  48.4 28.2 %collective-permute-start = (bf16[640,512]{1,0:T(8,128)(2,1)S(1)}, bf16[640,512]{1,0:T(8,128)(2,1)S(1)}, u32[]{:S(2)}, u32[]{:S(2)}) collective-permute-start(bf16[640,512]{1,0:T(8,128)(2,1)S(1)} %get-tuple-element.19), channel_id=1, source_target_pairs={{0,32},{32,0},{64,96},{96,64},{128,160},{160,128},{192,224},{224,1... | collective-permute-start | bytes 1966088 | tf_op jit(solution)/shard_map/ppermute | solution.py:348
  53.6 20.9 %collective-permute-start.19 = (bf16[192,1024]{1,0:T(8,128)(2,1)S(1)}, bf16[192,1024]{1,0:T(8,128)(2,1)}, u32[]{:S(2)}, u32[]{:S(2)}) collective-permute-start(bf16[192,1024]{1,0:T(8,128)(2,1)S(1)} %get-tuple-element.26), channel_id=1, source_target_pairs={{0,64},{32,96},{64,128},{96,160},{128,192},{160,224},{192,0},{224,... | collective-permute-start | bytes 1179656 | tf_op jit(solution)/shard_map/ppermute | solution.py:348
  54.5 21.0 %collective-permute-start.21 = (bf16[192,1024]{1,0:T(8,128)(2,1)S(1)}, bf16[192,1024]{1,0:T(8,128)(2,1)}, u32[]{:S(2)}, u32[]{:S(2)}) collective-permute-start(bf16[192,1024]{1,0:T(8,128)(2,1)S(1)} %get-tuple-element.27), channel_id=1, source_target_pairs={{0,192},{32,224},{64,0},{96,32},{128,64},{160,96},{192,128},{224,1... | collective-permute-start | bytes 1179656 | tf_op jit(solution)/shard_map/ppermute | solution.py:348
  57.0 13.6 %collective-permute-start.5 = (bf16[320,512]{1,0:T(8,128)(2,1)S(1)}, bf16[320,512]{1,0:T(8,128)(2,1)S(1)}, u32[]{:S(2)}, u32[]{:S(2)}) collective-permute-start(bf16[320,512]{1,0:T(8,128)(2,1)S(1)} %get-tuple-element.21.refs_2_), channel_id=1, source_target_pairs={{0,192},{32,224},{64,0},{96,32},{128,64},{160,96},{192,128},{224,1... | collective-permute-start | bytes 983048 | tf_op jit(solution)/shard_map/ppermute | solution.py:348
  58.9 17.8 %collective-permute-start.4 = (bf16[320,512]{1,0:T(8,128)(2,1)S(1)}, bf16[320,512]{1,0:T(8,128)(2,1)S(1)}, u32[]{:S(2)}, u32[]{:S(2)}) collective-permute-start(bf16[320,512]{1,0:T(8,128)(2,1)S(1)} %collective-permute-done.3.refs_3_), channel_id=1, source_target_pairs={{0,64},{32,96},{64,128},{96,160},{128,192},{160,224},{192,0},{224,... | collective-permute-start | bytes 983048 | tf_op jit(solution)/shard_map/ppermute | solution.py:348
  70.6 10.7 %collective-permute-start.6 = (bf16[320,512]{1,0:T(8,128)(2,1)S(1)}, bf16[320,512]{1,0:T(8,128)(2,1)S(1)}, u32[]{:S(2)}, u32[]{:S(2)}) collective-permute-start(bf16[320,512]{1,0:T(8,128)(2,1)S(1)} %collective-permute-done.5.refs_6_), channel_id=1, source_target_pairs={{0,192},{32,224},{64,0},{96,32},{128,64},{160,96},{192,128},{224,1... | collective-permute-start | bytes 983048 | tf_op jit(solution)/shard_map/ppermute | solution.py:348
  74.6 10.2 %collective-permute-start.10 = (bf16[320,512]{1,0:T(8,128)(2,1)S(1)}, bf16[320,512]{1,0:T(8,128)(2,1)S(1)}, u32[]{:S(2)}, u32[]{:S(2)}) collective-permute-start(bf16[320,512]{1,0:T(8,128)(2,1)S(1)} %get-tuple-element.20.refs_1_), channel_id=1, source_target_pairs={{0,192},{32,224},{64,0},{96,32},{128,64},{160,96},{192,128},{224,1... | collective-permute-start | bytes 983048 | tf_op jit(solution)/shard_map/ppermute | solution.py:348
  75.4 11.8 %collective-permute-start.9 = (bf16[320,512]{1,0:T(8,128)(2,1)S(1)}, bf16[320,512]{1,0:T(8,128)(2,1)S(1)}, u32[]{:S(2)}, u32[]{:S(2)}) collective-permute-start(bf16[320,512]{1,0:T(8,128)(2,1)S(1)} %get-tuple-element.21.refs_2_), channel_id=1, source_target_pairs={{0,64},{32,96},{64,128},{96,160},{128,192},{160,224},{192,0},{224,... | collective-permute-start | bytes 983048 | tf_op jit(solution)/shard_map/ppermute | solution.py:348
  76.6 24.7 %collective-permute-start.1 = (bf16[640,512]{1,0:T(8,128)(2,1)S(1)}, bf16[640,512]{1,0:T(8,128)(2,1)S(1)}, u32[]{:S(2)}, u32[]{:S(2)}) collective-permute-start(bf16[640,512]{1,0:T(8,128)(2,1)S(1)} %collective-permute-done.refs_7_), channel_id=1, source_target_pairs={{0,64},{32,96},{64,128},{96,160},{128,192},{160,224},{192,0},{224,... | collective-permute-start | bytes 1966088 | tf_op jit(solution)/shard_map/ppermute | solution.py:348
  76.7 13.3 %collective-permute-start.7 = (bf16[320,512]{1,0:T(8,128)(2,1)S(1)}, bf16[320,512]{1,0:T(8,128)(2,1)S(1)}, u32[]{:S(2)}, u32[]{:S(2)}) collective-permute-start(bf16[320,512]{1,0:T(8,128)(2,1)S(1)} %collective-permute-done.4.refs_3_), channel_id=1, source_target_pairs={{0,32},{32,0},{64,96},{96,64},{128,160},{160,128},{192,224},{224,1... | collective-permute-start | bytes 983048 | tf_op jit(solution)/shard_map/ppermute | solution.py:348
  81.3 11.5 %collective-permute-start.8 = (bf16[320,512]{1,0:T(8,128)(2,1)S(1)}, bf16[320,512]{1,0:T(8,128)(2,1)S(1)}, u32[]{:S(2)}, u32[]{:S(2)}) collective-permute-start(bf16[320,512]{1,0:T(8,128)(2,1)S(1)} %collective-permute-done.6.refs_4_), channel_id=1, source_target_pairs={{0,32},{32,0},{64,96},{96,64},{128,160},{160,128},{192,224},{224,1... | collective-permute-start | bytes 983048 | tf_op jit(solution)/shard_map/ppermute | solution.py:348
  85.5 45.4 %collective-permute-start.17 = (bf16[2,192,1024]{2,1,0:T(8,128)(2,1)}, bf16[2,192,1024]{2,1,0:T(8,128)(2,1)}, u32[]{:S(2)}, u32[]{:S(2)}) collective-permute-start(bf16[2,192,1024]{2,1,0:T(8,128)(2,1)} %get-tuple-element.24), channel_id=1, source_target_pairs={{0,64},{32,96},{64,128},{96,160},{128,192},{160,224},{192,0},{224,... | collective-permute-start | bytes 2359304 | tf_op jit(solution)/shard_map/ppermute | solution.py:348
  88.0 21.9 %collective-permute-start.2 = (bf16[640,512]{1,0:T(8,128)(2,1)S(1)}, bf16[640,512]{1,0:T(8,128)(2,1)S(1)}, u32[]{:S(2)}, u32[]{:S(2)}) collective-permute-start(bf16[640,512]{1,0:T(8,128)(2,1)S(1)} %collective-permute-done.refs_7_), channel_id=1, source_target_pairs={{0,192},{32,224},{64,0},{96,32},{128,64},{160,96},{192,128},{224,1... | collective-permute-start | bytes 1966088 | tf_op jit(solution)/shard_map/ppermute | solution.py:348
  90.7 45.3 %collective-permute-start.18 = (bf16[2,192,1024]{2,1,0:T(8,128)(2,1)}, bf16[2,192,1024]{2,1,0:T(8,128)(2,1)}, u32[]{:S(2)}, u32[]{:S(2)}) collective-permute-start(bf16[2,192,1024]{2,1,0:T(8,128)(2,1)} %get-tuple-element.25), channel_id=1, source_target_pairs={{0,192},{32,224},{64,0},{96,32},{128,64},{160,96},{192,128},{224,1... | collective-permute-start | bytes 2359304 | tf_op jit(solution)/shard_map/ppermute | solution.py:348
  93.5 29.3 %collective-permute-start.20 = (bf16[192,1024]{1,0:T(8,128)(2,1)}, bf16[192,1024]{1,0:T(8,128)(2,1)}, u32[]{:S(2)}, u32[]{:S(2)}) collective-permute-start(bf16[192,1024]{1,0:T(8,128)(2,1)} %collective-permute-done.19), channel_id=1, source_target_pairs={{0,64},{32,96},{64,128},{96,160},{128,192},{160,224},{192,0},{224,... | collective-permute-start | bytes 1179656 | tf_op jit(solution)/shard_map/ppermute | solution.py:348
  101.3 27.7 %collective-permute-start.22 = (bf16[192,1024]{1,0:T(8,128)(2,1)}, bf16[192,1024]{1,0:T(8,128)(2,1)}, u32[]{:S(2)}, u32[]{:S(2)}) collective-permute-start(bf16[192,1024]{1,0:T(8,128)(2,1)} %collective-permute-done.21), channel_id=1, source_target_pairs={{0,192},{32,224},{64,0},{96,32},{128,64},{160,96},{192,128},{224,1... | collective-permute-start | bytes 1179656 | tf_op jit(solution)/shard_map/ppermute | solution.py:348
  113.5 19.3 %collective-permute-start.11 = (bf16[160,384]{1,0:T(8,128)(2,1)S(1)}, bf16[160,384]{1,0:T(8,128)(2,1)S(1)}, u32[]{:S(2)}, u32[]{:S(2)}) collective-permute-start(bf16[160,384]{1,0:T(8,128)(2,1)S(1)} %get-tuple-element.22.refs_0_), channel_id=1, source_target_pairs={{0,64},{32,96},{64,128},{96,160},{128,192},{160,224},{192,0},{224,... | collective-permute-start | bytes 368648 | tf_op jit(solution)/shard_map/ppermute | solution.py:348
  122.7 10.2 %collective-permute-start.14 = (bf16[160,384]{1,0:T(8,128)(2,1)S(1)}, bf16[160,384]{1,0:T(8,128)(2,1)S(1)}, u32[]{:S(2)}, u32[]{:S(2)}) collective-permute-start(bf16[160,384]{1,0:T(8,128)(2,1)S(1)} %get-tuple-element.23.refs_1_), channel_id=1, source_target_pairs={{0,192},{32,224},{64,0},{96,32},{128,64},{160,96},{192,128},{224,1... | collective-permute-start | bytes 368648 | tf_op jit(solution)/shard_map/ppermute | solution.py:348
  129.0 7.0 %collective-permute-start.12 = (bf16[160,384]{1,0:T(8,128)(2,1)S(1)}, bf16[160,384]{1,0:T(8,128)(2,1)S(1)}, u32[]{:S(2)}, u32[]{:S(2)}) collective-permute-start(bf16[160,384]{1,0:T(8,128)(2,1)S(1)} %get-tuple-element.23.refs_1_), channel_id=1, source_target_pairs={{0,64},{32,96},{64,128},{96,160},{128,192},{160,224},{192,0},{224,... | collective-permute-start | bytes 368648 | tf_op jit(solution)/shard_map/ppermute | solution.py:348
  132.7 6.1 %collective-permute-start.15 = (bf16[160,384]{1,0:T(8,128)(2,1)S(1)}, bf16[160,384]{1,0:T(8,128)(2,1)S(1)}, u32[]{:S(2)}, u32[]{:S(2)}) collective-permute-start(bf16[160,384]{1,0:T(8,128)(2,1)S(1)} %collective-permute-done.11.refs_2_), channel_id=1, source_target_pairs={{0,64},{32,96},{64,128},{96,160},{128,192},{160,224},{192,0},{224,... | collective-permute-start | bytes 368648 | tf_op jit(solution)/shard_map/ppermute | solution.py:348
  141.5 10.9 %collective-permute-start.23 = (bf16[640,512]{1,0:T(8,128)(2,1)S(1)}, bf16[640,512]{1,0:T(8,128)(2,1)S(1)}, u32[]{:S(2)}, u32[]{:S(2)}) collective-permute-start(bf16[640,512]{1,0:T(8,128)(2,1)S(1)} %shard_map.109), channel_id=1, source_target_pairs={{0,32},{32,0},{64,96},{96,64},{128,160},{160,128},{192,224},{224,1... | collective-permute-start | bytes 1966088 | tf_op jit(solution)/shard_map/ppermute | solution.py:348
  (26 other events, 218.6 us)

commit v3 on v2

--- a/solution.py
+++ b/solution.py
@@ -1,3 +1,5 @@
+from functools import partial
+
 import jax
 import jax.numpy as jnp
 from jax import lax
@@ -29,8 +31,8 @@
 BLOCK = GROUP * CAP
 
 
-SMEM = pl.BlockSpec(memory_space=pltpu.SMEM)
 HBM = pl.BlockSpec(memory_space=pltpu.HBM)
+VMEM = pl.BlockSpec(memory_space=pltpu.VMEM)
 bf16 = jnp.bfloat16
 f32 = jnp.float32
 
@@ -53,10 +55,12 @@
     )
 
 
-def call(kernel, out_shapes, operands, memory=None, scratch=(), limit=12, hbm=()):
+def call(kernel, out_shapes, operands, memory=None, scratch=(), limit=12, hbm=(), out=None):
     memory = memory or {}
     many = isinstance(out_shapes, (list, tuple))
     out_specs = [whole(each.shape) for each in out_shapes] if many else whole(out_shapes.shape)
+    if out is not None:
+        out_specs = [out] * len(out_shapes)
     operands = [
         pltpu.with_memory_space_constraint(each, pltpu.HBM)
         if at in hbm or memory.get(at) is HBM
@@ -126,20 +130,16 @@
         send[pl.ds(at, WIDE), :] = jnp.where(right, 1.0, 0.0).astype(bf16)
         return carry
 
-    lax.fori_loop(0, STEPS * N_EP * CHUNK // WIDE, block, 0)
-
-
-def tables_kernel(ids, weights, keep_hi, keep_lo, sort, unsort):
+    lax.fori_loop(0, STEPS * N_EP * CHUNK // WIDE, block, 0, unroll=5)
+
+
+def tables_kernel(ids, weights, keep, sort, unsort):
     hits, position = positions(ids)
     shares = weights[...] / jnp.sum(weights[...], axis=-1, keepdims=True)
     share = sum(
         jnp.where(hit, shares[:, which : which + 1], 0.0) for which, hit in enumerate(hits)
     )
-    share_hi = share.astype(bf16)
-    share_lo = (share - share_hi.astype(f32)).astype(bf16)
-    share_hi = jnp.concatenate([share_hi] * Q, axis=0)
-    share_lo = jnp.concatenate([share_lo] * Q, axis=0)
-
+    share = jnp.concatenate([share.astype(bf16)] * Q, axis=0)
     row = lax.broadcasted_iota(jnp.int32, (Q * ALL_ROWS, 1), 0)
     row = (row >> 6) * 2 + ((row >> 2) & 1)
 
@@ -149,8 +149,7 @@
         pick = lax.broadcasted_iota(jnp.int32, (EXPERTS, WIDE), 0) == bucket
         pick = jnp.where(pick, 1.0, 0.0).astype(bf16)
         right = (nn(position, pick) == place) & (row == piece)
-        keep_hi[:, pl.ds(at, WIDE)] = jnp.where(right, nn(share_hi, pick), 0.0).astype(bf16)
-        keep_lo[:, pl.ds(at, WIDE)] = jnp.where(right, nn(share_lo, pick), 0.0).astype(bf16)
+        keep[:, pl.ds(at, WIDE)] = jnp.where(right, nn(share, pick), 0.0).astype(bf16)
         return carry
 
     lax.fori_loop(0, STEPS * N_EP * CHUNK // WIDE, keep_block, 0)
@@ -185,20 +184,42 @@
     out[...] = nn(table[...], stacked).astype(bf16)
 
 
-def cut_kernel(places, weights, far_first, far_second, near_next, near_before, sems):
-    def source(which):
-        return pl.ds(pl.multiple_of(places[which], 2 * COLS), 2 * COLS)
-
-    copies = [
-        pltpu.make_async_copy(weights.at[0, :, source(0)], far_first, sems.at[0]),
-        pltpu.make_async_copy(weights.at[1, :, source(0)], far_second, sems.at[1]),
-        pltpu.make_async_copy(weights.at[:, :, source(1)], near_next, sems.at[2]),
-        pltpu.make_async_copy(weights.at[:, :, source(2)], near_before, sems.at[3]),
-    ]
+def my_place():
+    me = lax.axis_index("rep")
+    return me >> 1, me & 1
+
+
+OFFSETS = ((0, 0), (3, 0), (1, 0), (0, 1), (3, 1), (1, 1), (2, 0), (2, 1))
+
+
+def slab(ahead):
+    x, _ = my_place()
+    return pl.ds(pl.multiple_of(((x + ahead) & 3) * (2 * COLS), 2 * COLS), 2 * COLS)
+
+
+def run_all(copies):
     for copy in copies:
         copy.start()
     for copy in copies:
         copy.wait()
+
+
+def near_kernel(weights, near_next, near_before, sems):
+    run_all(
+        [
+            pltpu.make_async_copy(weights.at[:, :, slab(1)], near_next, sems.at[0]),
+            pltpu.make_async_copy(weights.at[:, :, slab(3)], near_before, sems.at[1]),
+        ]
+    )
+
+
+def far_kernel(weights, far_first, far_second, sems):
+    run_all(
+        [
+            pltpu.make_async_copy(weights.at[0, :, slab(2)], far_first, sems.at[0]),
+            pltpu.make_async_copy(weights.at[1, :, slab(2)], far_second, sems.at[1]),
+        ]
+    )
 
 
 def receive_kernel(arrived, table, *outs):
@@ -230,21 +251,24 @@
     return jnp.concatenate(both, axis=0)
 
 
-def hidden_kernel(first, sizes, order, *refs):
+def hidden_kernel(which_chunks, last, sizes, *refs):
     count = len(sizes)
     chunks = []
     for size in sizes:
         chunks.append(refs[:size])
         refs = refs[size:]
     before = None
-    if first > 0:
+    if which_chunks[0] > 0:
         before, refs = refs[0], refs[1:]
     gate_all, up_all = refs[:2]
     outs = refs[2:-3]
     gate, up, sems = refs[-3:]
 
     def copies(index):
-        at = pl.ds(pl.multiple_of(order[first + index] * COLS, COLS), COLS)
+        ahead, aside = OFFSETS[which_chunks[index]]
+        x, y = my_place()
+        chunk = ((x + ahead) & 3) * 2 + (y ^ aside)
+        at = pl.ds(pl.multiple_of(chunk * COLS, COLS), COLS)
         return (
             pltpu.make_async_copy(gate_all.at[:, :, at], gate.at[index], sems.at[0, index]),
             pltpu.make_async_copy(up_all.at[:, :, at], up.at[index], sems.at[1, index]),
@@ -265,7 +289,7 @@
                 at = 2 * local + which
                 product = nt(rows, weights[index, local])
                 sums[at] = product if sums[at] is None else sums[at] + product
-    if before is None:
+    if not last:
         for at in range(2 * LOCAL):
             outs[0][at] = sums[at]
         return
@@ -275,11 +299,12 @@
             outs[step][:, local * FR : (local + 1) * FR] = value[step * HALF : (step + 1) * HALF]
 
 
-def down_kernel(place, *refs):
+def down_kernel(aside, *refs):
     units = [refs[2 * index : 2 * index + 2] for index in range(4)]
     all_own, from_before, from_next, far_first, far_second, out, buffer, sems = refs[8:]
-    mine = pl.ds(pl.multiple_of(place[0], COLS), COLS)
-    inside = pl.ds(pl.multiple_of(place[1], COLS), COLS)
+    x, y = my_place()
+    mine = pl.ds(pl.multiple_of((x * 2 + (y ^ aside)) * COLS, COLS), COLS)
+    inside = pl.ds(pl.multiple_of((y ^ aside) * COLS, COLS), COLS)
     copies = [
         pltpu.make_async_copy(all_own.at[:, :, mine], buffer.at[0], sems.at[0]),
         pltpu.make_async_copy(from_before.at[:, :, inside], buffer.at[1], sems.at[1]),
@@ -318,9 +343,8 @@
             out[group * GROUP : (group + 1) * GROUP, step * CHUNK : (step + 1) * CHUNK, :] = result
 
 
-def mix_kernel(back, high, low, out):
-    rows = back[...]
-    total = (nn(high[...], rows) + nn(low[...], rows)).astype(bf16)
+def mix_kernel(back, keep, out):
+    total = nn(keep[...], back[...]).astype(bf16)
     for part in range(Q):
         piece = total[part * ALL_ROWS : (part + 1) * ALL_ROWS]
         out[:, part * LANES : (part + 1) * LANES] = piece
@@ -369,16 +393,6 @@
 
 def on_device(tokens, norm_gain, expert_ids, route_weights, w_gate, w_up, w_down):
     sds = jax.ShapeDtypeStruct
-    me = lax.axis_index("rep")
-    my_x = me // 2
-    my_y = me % 2
-    offset_x = jnp.array([0, 3, 1, 0, 3, 1, 2, 2], jnp.int32)
-    offset_y = jnp.array([0, 0, 0, 1, 1, 1, 0, 1], jnp.int32)
-    order = ((my_x + offset_x) % 4) * 2 + (my_y + offset_y) % 2
-    here = jnp.arange(2, dtype=jnp.int32)
-    place_mine = me * COLS * (1 - here) + my_y * COLS * here
-    place_other = (me + 1 - 2 * my_y) * COLS * (1 - here) + (1 - my_y) * COLS * here
-
     normed = call(
         norm_kernel,
         sds((N_REP, STEPS * ROWS, COLS), bf16),
@@ -387,20 +401,18 @@
     )
     own = swap(normed, "rep")
 
-    steps_ahead = jnp.array([2, 1, 3], jnp.int32)
-    places = ((my_x + steps_ahead) % 4) * (2 * COLS)
     far_shape, near_shape = sds((FR, 2 * COLS), bf16), sds((LOCAL, FR, 2 * COLS), bf16)
-    far_first, far_second, near_next, near_before = call(
-        cut_kernel,
-        [far_shape, far_shape, near_shape, near_shape],
-        (places, w_down),
-        memory={0: SMEM, 1: HBM},
-        scratch=[pltpu.SemaphoreType.DMA((4,))],
-    )
+
+    def cut(kernel, shape):
+        scratch = [pltpu.SemaphoreType.DMA((2,))]
+        return call(kernel, [shape] * 2, (w_down,), memory={0: HBM}, scratch=scratch, out=VMEM)
+
+    near_next, near_before = cut(near_kernel, near_shape)
+    far_first, far_second = cut(far_kernel, far_shape)
+    from_before = go(near_next, NEXT)
+    from_next = go(near_before, BEFORE)
     far_first = go(far_first, NEXT)
     far_second = go(far_second, BEFORE)
-    from_before = go(near_next, NEXT)
-    from_next = go(near_before, BEFORE)
     far_first = go(far_first, NEXT)
     far_second = go(far_second, BEFORE)
 
@@ -409,10 +421,9 @@
     weights = weights.reshape(ALL_ROWS, TOPK)
     slots = STEPS * N_EP * CHUNK
     send = call(send_table_kernel, sds((slots, Q * ALL_ROWS), bf16), (ids,))
-    keep_hi, keep_lo, sort, unsort = call(
+    keep, sort, unsort = call(
         tables_kernel,
         [
-            sds((Q * ALL_ROWS, slots), bf16),
             sds((Q * ALL_ROWS, slots), bf16),
             sds((GROUP_ROWS, GROUP_ROWS), bf16),
             sds((GROUP_ROWS, GROUP_ROWS), bf16),
@@ -426,22 +437,27 @@
     one, two = sds((LOCAL * HALF, COLS), bf16), sds((STEPS * LOCAL * HALF, COLS), bf16)
     rows = call(receive_kernel, [one, one, two], (arrived, sort))
     sums = ()
-    for first, parts in zip((0, 4), gathered(*rows)):
+    early, late = gathered(*rows)
+    every = (*early, *late)
+    for name, which in (("early", (0, 1, 2, 3)), ("middle", (6,)), ("late", (4, 5, 7))):
+        parts = [every[index] for index in which]
         sizes = tuple(len(part) for part in parts)
+        count = len(sizes)
+        last = name == "late"
         chunks = tuple(each for part in parts for each in part)
-        operands = (order, *chunks, *sums, w_gate, w_up)
+        operands = (*chunks, *sums, w_gate, w_up)
         shapes = [sds((2 * LOCAL, STEPS * HALF, FR), f32)]
-        if first > 0:
+        if last:
             shapes = [sds((HALF, LOCAL * FR), bf16)] * STEPS
         sums = call(
-            lambda *refs, first=first, sizes=sizes: hidden_kernel(first, sizes, *refs),
+            partial(hidden_kernel, which, last, sizes),
             shapes,
             operands,
-            memory={0: SMEM, len(operands) - 2: HBM, len(operands) - 1: HBM},
+            memory={len(operands) - 2: HBM, len(operands) - 1: HBM},
             scratch=[
-                pltpu.VMEM((4, LOCAL, FR, COLS), bf16),
-                pltpu.VMEM((4, LOCAL, FR, COLS), bf16),
-                pltpu.SemaphoreType.DMA((2, 4)),
+                pltpu.VMEM((count, LOCAL, FR, COLS), bf16),
+                pltpu.VMEM((count, LOCAL, FR, COLS), bf16),
+                pltpu.SemaphoreType.DMA((2, count)),
             ],
             limit=20,
         )
@@ -451,24 +467,24 @@
     c0, c1 = go(a0, NEXT), go(b1, BEFORE)
     units = (hidden0, hidden1, a0, a1, b0, b1, c0, c1)
 
-    def down(place, dtype):
-        operands = (place, *units, w_down, from_before, from_next, far_first, far_second)
+    def down(aside, dtype):
+        operands = (*units, w_down, from_before, from_next, far_first, far_second)
         return call(
-            down_kernel,
+            partial(down_kernel, aside),
             sds((STEPS * LOCAL * HALF, COLS), dtype),
             operands,
-            memory={0: SMEM, **{at: HBM for at in range(9, 14)}},
+            memory={at: HBM for at in range(8, 13)},
             scratch=[
                 pltpu.VMEM((4, LOCAL, FR, COLS), bf16),
                 pltpu.SemaphoreType.DMA((5,)),
             ],
         )
 
-    other = go(down(place_other, bf16), BESIDE)
-    mine = down(place_mine, f32)
+    other = go(down(1, bf16), BESIDE)
+    mine = down(0, f32)
     back = call(return_kernel, sds((N_EP, STEPS * CHUNK, LANES), bf16), (mine, other, unsort))
     back = swap(back, "ep").reshape(slots, LANES)
-    mixed = call(mix_kernel, sds((ALL_ROWS, COLS), bf16), (back, keep_hi, keep_lo), hbm=(1, 2))
+    mixed = call(mix_kernel, sds((ALL_ROWS, COLS), bf16), (back, keep), hbm=(1,))
     mixed = swap(mixed.reshape(N_REP, STEPS * ROWS, COLS), "rep")
     out = call(final_kernel, sds((STEPS, ROWS, D), bf16), (mixed,))
     return out[:, None, None]

time: 198 us -> 190 us (0.960)
  local copies, waits for them, and re-layouts: 13.7 us -> 1.86 us
  starting transfers between devices: 44.5 us -> 50.6 us
  Pallas kernels: 30 us -> 26.4 us
    unnamed x48 -> x12, local copies, waits for them, and re-layouts: 13 us -> 1.08 us
    ppermute x24, starting transfers between devices: 28 us -> 34.2 us  [go(): return lax.ppermute(value, 'rep', pairs)]
    pallas_call x13 -> x15, Pallas kernels: 30 us -> 26.4 us  [call(): pl.pallas_call(kernel, out_shape=out_shapes, grid=(1,), in_specs=[memory....]
    all_to_all x2, waiting for transfers between devices: 18.3 us -> 20.5 us  [swap(): return lax.all_to_all(value, axis, split_axis=0, concat_axis=0, tiled=True)]
  transfers between devices with their start and end apart: 26 -> 26, of which waited for: 12 -> 16; matrix products, arithmetic and copies ran while one was open for 0% -> 0% of each run, Pallas kernels for 10% -> 9%
where the time goes in v3:
time: 190 us; the launch traced here: 189 us
  waiting for transfers between devices  70 us (37%)
  starting transfers between devices  50.6 us (27%)
  blocking collectives  39.8 us (21%)
  Pallas kernels  26.4 us (14%)
    ppermute x24, waiting for transfers between devices, go(): return lax.ppermute(value, 'rep', pairs)  49.5 us
    all_to_all x2, blocking collectives, swap(): return lax.all_to_all(value, axis, split_axis=0, concat_axis=0, tiled=True)  39.8 us
    ppermute x24, starting transfers between devices, go(): return lax.ppermute(value, 'rep', pairs)  34.2 us
    pallas_call x15, Pallas kernels, call(): pl.pallas_call(kernel, out_shape=out_shapes, grid=(1,), in_specs=[memory....  26.4 us
    all_to_all x2, waiting for transfers between devices, swap(): return lax.all_to_all(value, axis, split_axis=0, concat_axis=0, tiled=True)  20.5 us
    all_to_all x2, starting transfers between devices, swap(): return lax.all_to_all(value, axis, split_axis=0, concat_axis=0, tiled=True)  16.4 us
  transfers between devices with their start and end apart: 26, of which 16 were waited for; matrix products, arithmetic and copies ran while one was open for 0% of the time, Pallas kernels for 9%

profile of v3, /device:TPU:8, one launch (start us, length us, event | category | flops | bytes accessed | tf_op | source)
XLA Modules:
  0.0 188.8 jit_solution(16461740299992583796)
XLA Ops:
  1.6 5.8 %all-to-all-start = ((bf16[8,8,512]{2,1,0:T(8,128)(2,1)}), bf16[8,8,512]{2,1,0:T(8,128)(2,1)S(1)}, u32[]{:S(2)}, u32[]{:S(2)}) async-start(bf16[8,8,512]{2,1,0:T(8,128)(2,1)} %shard_map.73), calls=%async_computation | async-start | bytes 131072 | tf_op jit(solution)/shard_map/all_to_all | solution.py:376
  10.0 2.4 %all-to-all-done.rows = bf16[8,8,512]{2,1,0:T(8,128)(2,1)S(1)} async-done(((bf16[8,8,512]{2,1,0:T(8,128)(2,1)}), bf16[8,8,512]{2,1,0:T(8,128)(2,1)S(1)}, u32[]{:S(2)}, u32[]{:S(2)}) %all-to-all-start) | async-done | bytes 65568 | tf_op jit(solution)/shard_map/all_to_all | solution.py:376
  13.8 10.6 %all-to-all-start.1 = ((bf16[32,80,128]{2,1,0:T(8,128)(2,1)}), bf16[32,80,128]{2,1,0:T(8,128)(2,1)S(1)}, u32[]{:S(2)}, u32[]{:S(2)}) async-start(bf16[32,80,128]{2,1,0:T(8,128)(2,1)} %bitcast.5), calls=%async_computation.1 | async-start | bytes 1310720 | tf_op jit(solution)/shard_map/all_to_all | solution.py:376
  24.4 3.1 %shard_map.76 = (bf16[256,2560]{1,0:T(8,128)(2,1)S(1)}, bf16[640,640]{1,0:T(8,128)(2,1)S(1)}, bf16[640,640]{1,0:T(8,128)(2,1)S(1)}) custom-call(s32[64,8]{1,0:T(8,128)S(1)} %bitcast.18, f32[64,8]{1,0:T(8,128)S(1)} %bitcast.20), custom_call_target="tpu_custom_call" | custom-call | tf_op jit(solution)/shard_map/pallas_call | solution.py:70
  28.6 18.1 %all-to-all-done.1.arrived = bf16[32,80,128]{2,1,0:T(8,128)(2,1)S(1)} async-done(((bf16[32,80,128]{2,1,0:T(8,128)(2,1)}), bf16[32,80,128]{2,1,0:T(8,128)(2,1)S(1)}, u32[]{:S(2)}, u32[]{:S(2)}) %all-to-all-start.1) | async-done | bytes 655392 | tf_op jit(solution)/shard_map/all_to_all | solution.py:376
  52.0 2.5 %collective-permute-start.21 = (bf16[192,1024]{1,0:T(8,128)(2,1)S(1)}, bf16[192,1024]{1,0:T(8,128)(2,1)S(1)}, u32[]{:S(2)}, u32[]{:S(2)}) collective-permute-start(bf16[192,1024]{1,0:T(8,128)(2,1)S(1)} %get-tuple-element.26), channel_id=1, source_target_pairs={{0,192},{32,224},{64,0},{96,32},{128,64},{160,96},{192,128},{224,1... | collective-permute-start | bytes 1179656 | tf_op jit(solution)/shard_map/ppermute | solution.py:372
  56.0 3.5 %collective-permute-done.3.refs_2_ = bf16[320,512]{1,0:T(8,128)(2,1)S(1)} collective-permute-done((bf16[320,512]{1,0:T(8,128)(2,1)S(1)}, bf16[320,512]{1,0:T(8,128)(2,1)S(1)}, u32[]{:S(2)}, u32[]{:S(2)}) %collective-permute-start.3) | collective-permute-done | bytes 327712 | tf_op jit(solution)/shard_map/ppermute | solution.py:372
  59.5 8.4 %collective-permute-done.19 = bf16[192,1024]{1,0:T(8,128)(2,1)S(1)} collective-permute-done((bf16[192,1024]{1,0:T(8,128)(2,1)S(1)}, bf16[192,1024]{1,0:T(8,128)(2,1)S(1)}, u32[]{:S(2)}, u32[]{:S(2)}) %collective-permute-start.19) | collective-permute-done | bytes 393248 | tf_op jit(solution)/shard_map/ppermute | solution.py:372
  71.1 3.7 %collective-permute-start.7 = (bf16[320,512]{1,0:T(8,128)(2,1)S(1)}, bf16[320,512]{1,0:T(8,128)(2,1)S(1)}, u32[]{:S(2)}, u32[]{:S(2)}) collective-permute-start(bf16[320,512]{1,0:T(8,128)(2,1)S(1)} %collective-permute-done.6.refs_5_), channel_id=1, source_target_pairs={{0,192},{32,224},{64,0},{96,32},{128,64},{160,96},{192,128},{224,1... | collective-permute-start | bytes 983048 | tf_op jit(solution)/shard_map/ppermute | solution.py:372
  79.4 2.6 %collective-permute-done.9.refs_3_ = bf16[320,512]{1,0:T(8,128)(2,1)S(1)} collective-permute-done((bf16[320,512]{1,0:T(8,128)(2,1)S(1)}, bf16[320,512]{1,0:T(8,128)(2,1)S(1)}, u32[]{:S(2)}, u32[]{:S(2)}) %collective-permute-start.9) | collective-permute-done | bytes 327712 | tf_op jit(solution)/shard_map/ppermute | solution.py:372
  82.0 3.1 %collective-permute-done.7.refs_1_ = bf16[320,512]{1,0:T(8,128)(2,1)S(1)} collective-permute-done((bf16[320,512]{1,0:T(8,128)(2,1)S(1)}, bf16[320,512]{1,0:T(8,128)(2,1)S(1)}, u32[]{:S(2)}, u32[]{:S(2)}) %collective-permute-start.7) | collective-permute-done | bytes 327712 | tf_op jit(solution)/shard_map/ppermute | solution.py:372
  85.1 3.7 %collective-permute-start.2 = (bf16[640,512]{1,0:T(8,128)(2,1)S(1)}, bf16[640,512]{1,0:T(8,128)(2,1)S(1)}, u32[]{:S(2)}, u32[]{:S(2)}) collective-permute-start(bf16[640,512]{1,0:T(8,128)(2,1)S(1)} %collective-permute-done.refs_6_), channel_id=1, source_target_pairs={{0,192},{32,224},{64,0},{96,32},{128,64},{160,96},{192,128},{224,1... | collective-permute-start | bytes 1966088 | tf_op jit(solution)/shard_map/ppermute | solution.py:372
  88.8 7.1 %collective-permute-done.8.refs_3_ = bf16[320,512]{1,0:T(8,128)(2,1)S(1)} collective-permute-done((bf16[320,512]{1,0:T(8,128)(2,1)S(1)}, bf16[320,512]{1,0:T(8,128)(2,1)S(1)}, u32[]{:S(2)}, u32[]{:S(2)}) %collective-permute-start.8) | collective-permute-done | bytes 327712 | tf_op jit(solution)/shard_map/ppermute | solution.py:372
  96.0 3.1 %collective-permute-start.22 = (bf16[192,1024]{1,0:T(8,128)(2,1)S(1)}, bf16[192,1024]{1,0:T(8,128)(2,1)S(1)}, u32[]{:S(2)}, u32[]{:S(2)}) collective-permute-start(bf16[192,1024]{1,0:T(8,128)(2,1)S(1)} %collective-permute-done.21), channel_id=1, source_target_pairs={{0,192},{32,224},{64,0},{96,32},{128,64},{160,96},{192,128},{224,1... | collective-permute-start | bytes 1179656 | tf_op jit(solution)/shard_map/ppermute | solution.py:372
  99.1 3.1 %shard_map.78.refs_2_ = f32[4,320,192]{2,1,0:T(8,128)S(1)} custom-call(bf16[320,512]{1,0:T(8,128)(2,1)S(1)} %get-tuple-element.19.refs_0_, bf16[320,512]{1,0:T(8,128)(2,1)S(1)} %get-tuple-element.20.refs_1_, bf16[320,512]{1,0:T(8,128)(2,1)S(1)} %collective-permute-done.3.refs_2_, bf16[320,512]{1,0:T(8,128)(2,1)S(1)} %collective-permute-done.9.refs_3_, ...), custom_call_target="tpu_custom_call" | custom-call | tf_op jit(solution)/shard_map/pallas_call | solution.py:70
  103.9 12.5 %collective-permute-done.2.refs_1_ = bf16[640,512]{1,0:T(8,128)(2,1)S(1)} collective-permute-done((bf16[640,512]{1,0:T(8,128)(2,1)S(1)}, bf16[640,512]{1,0:T(8,128)(2,1)S(1)}, u32[]{:S(2)}, u32[]{:S(2)}) %collective-permute-start.2) | collective-permute-done | bytes 655392 | tf_op jit(solution)/shard_map/ppermute | solution.py:372
  116.4 2.6 %shard_map.80 = (bf16[160,384]{1,0:T(8,128)(2,1)S(1)}, bf16[160,384]{1,0:T(8,128)(2,1)S(1)}) custom-call(bf16[640,512]{1,0:T(8,128)(2,1)S(1)} %collective-permute-done.1.refs_0_, bf16[640,512]{1,0:T(8,128)(2,1)S(1)} %collective-permute-done.2.refs_1_, bf16[320,512]{1,0:T(8,128)(2,1)S(1)} %collective-permute-done.5.refs_2_, ...), custom_call_target="tpu_custom_call" | custom-call | tf_op jit(solution)/shard_map/pallas_call | solution.py:70
  120.0 2.5 %collective-permute-start.14 = (bf16[160,384]{1,0:T(8,128)(2,1)S(1)}, bf16[160,384]{1,0:T(8,128)(2,1)S(1)}, u32[]{:S(2)}, u32[]{:S(2)}) collective-permute-start(bf16[160,384]{1,0:T(8,128)(2,1)S(1)} %get-tuple-element.22.refs_1_), channel_id=1, source_target_pairs={{0,192},{32,224},{64,0},{96,32},{128,64},{160,96},{192,128},{224,1... | collective-permute-start | bytes 368648 | tf_op jit(solution)/shard_map/ppermute | solution.py:372
  122.5 3.2 %collective-permute-start.13 = (bf16[160,384]{1,0:T(8,128)(2,1)S(1)}, bf16[160,384]{1,0:T(8,128)(2,1)S(1)}, u32[]{:S(2)}, u32[]{:S(2)}) collective-permute-start(bf16[160,384]{1,0:T(8,128)(2,1)S(1)} %get-tuple-element.21.refs_0_), channel_id=1, source_target_pairs={{0,192},{32,224},{64,0},{96,32},{128,64},{160,96},{192,128},{224,1... | collective-permute-start | bytes 368648 | tf_op jit(solution)/shard_map/ppermute | solution.py:372
  126.3 3.1 %collective-permute-start.16 = (bf16[160,384]{1,0:T(8,128)(2,1)S(1)}, bf16[160,384]{1,0:T(8,128)(2,1)S(1)}, u32[]{:S(2)}, u32[]{:S(2)}) collective-permute-start(bf16[160,384]{1,0:T(8,128)(2,1)S(1)} %collective-permute-done.14.refs_5_), channel_id=1, source_target_pairs={{0,192},{32,224},{64,0},{96,32},{128,64},{160,96},{192,128},{224,1... | collective-permute-start | bytes 368648 | tf_op jit(solution)/shard_map/ppermute | solution.py:372
  129.5 2.5 %collective-permute-done.15.refs_6_ = bf16[160,384]{1,0:T(8,128)(2,1)S(1)} collective-permute-done((bf16[160,384]{1,0:T(8,128)(2,1)S(1)}, bf16[160,384]{1,0:T(8,128)(2,1)S(1)}, u32[]{:S(2)}, u32[]{:S(2)}) %collective-permute-start.15) | collective-permute-done | bytes 122912 | tf_op jit(solution)/shard_map/ppermute | solution.py:372
  137.9 7.6 %collective-permute-done.23.other = bf16[640,512]{1,0:T(8,128)(2,1)S(1)} collective-permute-done((bf16[640,512]{1,0:T(8,128)(2,1)S(1)}, bf16[640,512]{1,0:T(8,128)(2,1)S(1)}, u32[]{:S(2)}, u32[]{:S(2)}) %collective-permute-start.23) | collective-permute-done | bytes 655392 | tf_op jit(solution)/shard_map/ppermute | solution.py:372
  146.6 28.2 %all_to_all.20 = bf16[32,80,128]{2,1,0:T(8,128)(2,1)S(1)} all-to-all(bf16[32,80,128]{2,1,0:T(8,128)(2,1)S(1)} %shard_map.85), channel_id=1, replica_groups=mesh['rep'=8,'ep'=32] {'ep'}, dimensions={0} | all-to-all | bytes 1310720 | tf_op jit(solution)/shard_map/all_to_all | solution.py:376
  176.6 11.6 %all_to_all.21.arrived = bf16[8,8,512]{2,1,0:T(8,128)(2,1)S(1)} all-to-all(bf16[8,8,512]{2,1,0:T(8,128)(2,1)S(1)} %bitcast.19), channel_id=1, replica_groups=mesh['rep'=8,'ep'=32] {'rep'}, dimensions={0} | all-to-all | bytes 131072 | tf_op jit(solution)/shard_map/all_to_all | solution.py:376
  (59 shorter events, 34.1 us)
Async XLA Ops:
  1.6 10.8 %all-to-all-start = ((bf16[8,8,512]{2,1,0:T(8,128)(2,1)}), bf16[8,8,512]{2,1,0:T(8,128)(2,1)S(1)}, u32[]{:S(2)}, u32[]{:S(2)}) async-start(bf16[8,8,512]{2,1,0:T(8,128)(2,1)} %shard_map.73), calls=%async_computation | async-start | bytes 131072 | tf_op jit(solution)/shard_map/all_to_all | solution.py:376
  13.8 32.9 %all-to-all-start.1 = ((bf16[32,80,128]{2,1,0:T(8,128)(2,1)}), bf16[32,80,128]{2,1,0:T(8,128)(2,1)S(1)}, u32[]{:S(2)}, u32[]{:S(2)}) async-start(bf16[32,80,128]{2,1,0:T(8,128)(2,1)} %bitcast.5), calls=%async_computation.1 | async-start | bytes 1310720 | tf_op jit(solution)/shard_map/all_to_all | solution.py:376
  47.6 11.9 %collective-permute-start.3 = (bf16[320,512]{1,0:T(8,128)(2,1)S(1)}, bf16[320,512]{1,0:T(8,128)(2,1)S(1)}, u32[]{:S(2)}, u32[]{:S(2)}) collective-permute-start(bf16[320,512]{1,0:T(8,128)(2,1)S(1)} %get-tuple-element.19.refs_0_), channel_id=1, source_target_pairs={{0,64},{32,96},{64,128},{96,160},{128,192},{160,224},{192,0},{224,... | collective-permute-start | bytes 983048 | tf_op jit(solution)/shard_map/ppermute | solution.py:372
  49.4 18.5 %collective-permute-start.19 = (bf16[192,1024]{1,0:T(8,128)(2,1)S(1)}, bf16[192,1024]{1,0:T(8,128)(2,1)S(1)}, u32[]{:S(2)}, u32[]{:S(2)}) collective-permute-start(bf16[192,1024]{1,0:T(8,128)(2,1)S(1)} %get-tuple-element.25), channel_id=1, source_target_pairs={{0,64},{32,96},{64,128},{96,160},{128,192},{160,224},{192,0},{224,... | collective-permute-start | bytes 1179656 | tf_op jit(solution)/shard_map/ppermute | solution.py:372
  49.9 26.9 %collective-permute-start = (bf16[640,512]{1,0:T(8,128)(2,1)S(1)}, bf16[640,512]{1,0:T(8,128)(2,1)S(1)}, u32[]{:S(2)}, u32[]{:S(2)}) collective-permute-start(bf16[640,512]{1,0:T(8,128)(2,1)S(1)} %get-tuple-element.18), channel_id=1, source_target_pairs={{0,32},{32,0},{64,96},{96,64},{128,160},{160,128},{192,224},{224,1... | collective-permute-start | bytes 1966088 | tf_op jit(solution)/shard_map/ppermute | solution.py:372
  52.0 15.9 %collective-permute-start.21 = (bf16[192,1024]{1,0:T(8,128)(2,1)S(1)}, bf16[192,1024]{1,0:T(8,128)(2,1)S(1)}, u32[]{:S(2)}, u32[]{:S(2)}) collective-permute-start(bf16[192,1024]{1,0:T(8,128)(2,1)S(1)} %get-tuple-element.26), channel_id=1, source_target_pairs={{0,192},{32,224},{64,0},{96,32},{128,64},{160,96},{192,128},{224,1... | collective-permute-start | bytes 1179656 | tf_op jit(solution)/shard_map/ppermute | solution.py:372
  54.5 16.5 %collective-permute-start.6 = (bf16[320,512]{1,0:T(8,128)(2,1)S(1)}, bf16[320,512]{1,0:T(8,128)(2,1)S(1)}, u32[]{:S(2)}, u32[]{:S(2)}) collective-permute-start(bf16[320,512]{1,0:T(8,128)(2,1)S(1)} %get-tuple-element.20.refs_1_), channel_id=1, source_target_pairs={{0,192},{32,224},{64,0},{96,32},{128,64},{160,96},{192,128},{224,1... | collective-permute-start | bytes 983048 | tf_op jit(solution)/shard_map/ppermute | solution.py:372
  59.5 15.4 %collective-permute-start.4 = (bf16[320,512]{1,0:T(8,128)(2,1)S(1)}, bf16[320,512]{1,0:T(8,128)(2,1)S(1)}, u32[]{:S(2)}, u32[]{:S(2)}) collective-permute-start(bf16[320,512]{1,0:T(8,128)(2,1)S(1)} %collective-permute-done.3.refs_2_), channel_id=1, source_target_pairs={{0,64},{32,96},{64,128},{96,160},{128,192},{160,224},{192,0},{224,... | collective-permute-start | bytes 983048 | tf_op jit(solution)/shard_map/ppermute | solution.py:372
  67.9 10.3 %collective-permute-start.10 = (bf16[320,512]{1,0:T(8,128)(2,1)S(1)}, bf16[320,512]{1,0:T(8,128)(2,1)S(1)}, u32[]{:S(2)}, u32[]{:S(2)}) collective-permute-start(bf16[320,512]{1,0:T(8,128)(2,1)S(1)} %get-tuple-element.19.refs_0_), channel_id=1, source_target_pairs={{0,192},{32,224},{64,0},{96,32},{128,64},{160,96},{192,128},{224,1... | collective-permute-start | bytes 983048 | tf_op jit(solution)/shard_map/ppermute | solution.py:372
  67.9 14.0 %collective-permute-start.9 = (bf16[320,512]{1,0:T(8,128)(2,1)S(1)}, bf16[320,512]{1,0:T(8,128)(2,1)S(1)}, u32[]{:S(2)}, u32[]{:S(2)}) collective-permute-start(bf16[320,512]{1,0:T(8,128)(2,1)S(1)} %get-tuple-element.20.refs_1_), channel_id=1, source_target_pairs={{0,64},{32,96},{64,128},{96,160},{128,192},{160,224},{192,0},{224,... | collective-permute-start | bytes 983048 | tf_op jit(solution)/shard_map/ppermute | solution.py:372
  71.1 14.0 %collective-permute-start.7 = (bf16[320,512]{1,0:T(8,128)(2,1)S(1)}, bf16[320,512]{1,0:T(8,128)(2,1)S(1)}, u32[]{:S(2)}, u32[]{:S(2)}) collective-permute-start(bf16[320,512]{1,0:T(8,128)(2,1)S(1)} %collective-permute-done.6.refs_5_), channel_id=1, source_target_pairs={{0,192},{32,224},{64,0},{96,32},{128,64},{160,96},{192,128},{224,1... | collective-permute-start | bytes 983048 | tf_op jit(solution)/shard_map/ppermute | solution.py:372
  75.0 13.8 %collective-permute-start.5 = (bf16[320,512]{1,0:T(8,128)(2,1)S(1)}, bf16[320,512]{1,0:T(8,128)(2,1)S(1)}, u32[]{:S(2)}, u32[]{:S(2)}) collective-permute-start(bf16[320,512]{1,0:T(8,128)(2,1)S(1)} %collective-permute-done.4.refs_0_), channel_id=1, source_target_pairs={{0,32},{32,0},{64,96},{96,64},{128,160},{160,128},{192,224},{224,1... | collective-permute-start | bytes 983048 | tf_op jit(solution)/shard_map/ppermute | solution.py:372
  76.8 19.3 %collective-permute-start.1 = (bf16[640,512]{1,0:T(8,128)(2,1)S(1)}, bf16[640,512]{1,0:T(8,128)(2,1)S(1)}, u32[]{:S(2)}, u32[]{:S(2)}) collective-permute-start(bf16[640,512]{1,0:T(8,128)(2,1)S(1)} %collective-permute-done.refs_6_), channel_id=1, source_target_pairs={{0,64},{32,96},{64,128},{96,160},{128,192},{160,224},{192,0},{224,... | collective-permute-start | bytes 1966088 | tf_op jit(solution)/shard_map/ppermute | solution.py:372
  78.2 41.8 %collective-permute-start.17 = (bf16[2,192,1024]{2,1,0:T(8,128)(2,1)S(1)}, bf16[2,192,1024]{2,1,0:T(8,128)(2,1)S(1)}, u32[]{:S(2)}, u32[]{:S(2)}) collective-permute-start(bf16[2,192,1024]{2,1,0:T(8,128)(2,1)S(1)} %get-tuple-element.23), channel_id=1, source_target_pairs={{0,64},{32,96},{64,128},{96,160},{128,192},{160,224},{192,0},{224,... | collective-permute-start | bytes 2359304 | tf_op jit(solution)/shard_map/ppermute | solution.py:372
  82.0 40.5 %collective-permute-start.18 = (bf16[2,192,1024]{2,1,0:T(8,128)(2,1)S(1)}, bf16[2,192,1024]{2,1,0:T(8,128)(2,1)S(1)}, u32[]{:S(2)}, u32[]{:S(2)}) collective-permute-start(bf16[2,192,1024]{2,1,0:T(8,128)(2,1)S(1)} %get-tuple-element.24), channel_id=1, source_target_pairs={{0,192},{32,224},{64,0},{96,32},{128,64},{160,96},{192,128},{224,1... | collective-permute-start | bytes 2359304 | tf_op jit(solution)/shard_map/ppermute | solution.py:372
  85.1 31.3 %collective-permute-start.2 = (bf16[640,512]{1,0:T(8,128)(2,1)S(1)}, bf16[640,512]{1,0:T(8,128)(2,1)S(1)}, u32[]{:S(2)}, u32[]{:S(2)}) collective-permute-start(bf16[640,512]{1,0:T(8,128)(2,1)S(1)} %collective-permute-done.refs_6_), channel_id=1, source_target_pairs={{0,192},{32,224},{64,0},{96,32},{128,64},{160,96},{192,128},{224,1... | collective-permute-start | bytes 1966088 | tf_op jit(solution)/shard_map/ppermute | solution.py:372
  88.8 7.1 %collective-permute-start.8 = (bf16[320,512]{1,0:T(8,128)(2,1)S(1)}, bf16[320,512]{1,0:T(8,128)(2,1)S(1)}, u32[]{:S(2)}, u32[]{:S(2)}) collective-permute-start(bf16[320,512]{1,0:T(8,128)(2,1)S(1)} %collective-permute-done.7.refs_1_), channel_id=1, source_target_pairs={{0,32},{32,0},{64,96},{96,64},{128,160},{160,128},{192,224},{224,1... | collective-permute-start | bytes 983048 | tf_op jit(solution)/shard_map/ppermute | solution.py:372
  95.9 26.6 %collective-permute-start.20 = (bf16[192,1024]{1,0:T(8,128)(2,1)S(1)}, bf16[192,1024]{1,0:T(8,128)(2,1)S(1)}, u32[]{:S(2)}, u32[]{:S(2)}) collective-permute-start(bf16[192,1024]{1,0:T(8,128)(2,1)S(1)} %collective-permute-done.19), channel_id=1, source_target_pairs={{0,64},{32,96},{64,128},{96,160},{128,192},{160,224},{192,0},{224,... | collective-permute-start | bytes 1179656 | tf_op jit(solution)/shard_map/ppermute | solution.py:372
  96.0 33.4 %collective-permute-start.22 = (bf16[192,1024]{1,0:T(8,128)(2,1)S(1)}, bf16[192,1024]{1,0:T(8,128)(2,1)S(1)}, u32[]{:S(2)}, u32[]{:S(2)}) collective-permute-start(bf16[192,1024]{1,0:T(8,128)(2,1)S(1)} %collective-permute-done.21), channel_id=1, source_target_pairs={{0,192},{32,224},{64,0},{96,32},{128,64},{160,96},{192,128},{224,1... | collective-permute-start | bytes 1179656 | tf_op jit(solution)/shard_map/ppermute | solution.py:372
  119.0 6.8 %collective-permute-start.11 = (bf16[160,384]{1,0:T(8,128)(2,1)S(1)}, bf16[160,384]{1,0:T(8,128)(2,1)S(1)}, u32[]{:S(2)}, u32[]{:S(2)}) collective-permute-start(bf16[160,384]{1,0:T(8,128)(2,1)S(1)} %get-tuple-element.21.refs_0_), channel_id=1, source_target_pairs={{0,64},{32,96},{64,128},{96,160},{128,192},{160,224},{192,0},{224,... | collective-permute-start | bytes 368648 | tf_op jit(solution)/shard_map/ppermute | solution.py:372
  120.0 6.3 %collective-permute-start.14 = (bf16[160,384]{1,0:T(8,128)(2,1)S(1)}, bf16[160,384]{1,0:T(8,128)(2,1)S(1)}, u32[]{:S(2)}, u32[]{:S(2)}) collective-permute-start(bf16[160,384]{1,0:T(8,128)(2,1)S(1)} %get-tuple-element.22.refs_1_), channel_id=1, source_target_pairs={{0,192},{32,224},{64,0},{96,32},{128,64},{160,96},{192,128},{224,1... | collective-permute-start | bytes 368648 | tf_op jit(solution)/shard_map/ppermute | solution.py:372
  122.5 7.0 %collective-permute-start.12 = (bf16[160,384]{1,0:T(8,128)(2,1)S(1)}, bf16[160,384]{1,0:T(8,128)(2,1)S(1)}, u32[]{:S(2)}, u32[]{:S(2)}) collective-permute-start(bf16[160,384]{1,0:T(8,128)(2,1)S(1)} %get-tuple-element.22.refs_1_), channel_id=1, source_target_pairs={{0,64},{32,96},{64,128},{96,160},{128,192},{160,224},{192,0},{224,... | collective-permute-start | bytes 368648 | tf_op jit(solution)/shard_map/ppermute | solution.py:372
  122.5 7.0 %collective-permute-start.13 = (bf16[160,384]{1,0:T(8,128)(2,1)S(1)}, bf16[160,384]{1,0:T(8,128)(2,1)S(1)}, u32[]{:S(2)}, u32[]{:S(2)}) collective-permute-start(bf16[160,384]{1,0:T(8,128)(2,1)S(1)} %get-tuple-element.21.refs_0_), channel_id=1, source_target_pairs={{0,192},{32,224},{64,0},{96,32},{128,64},{160,96},{192,128},{224,1... | collective-permute-start | bytes 368648 | tf_op jit(solution)/shard_map/ppermute | solution.py:372
  134.1 11.5 %collective-permute-start.23 = (bf16[640,512]{1,0:T(8,128)(2,1)S(1)}, bf16[640,512]{1,0:T(8,128)(2,1)S(1)}, u32[]{:S(2)}, u32[]{:S(2)}) collective-permute-start(bf16[640,512]{1,0:T(8,128)(2,1)S(1)} %shard_map.84), channel_id=1, source_target_pairs={{0,32},{32,0},{64,96},{96,64},{128,160},{160,128},{192,224},{224,1... | collective-permute-start | bytes 1966088 | tf_op jit(solution)/shard_map/ppermute | solution.py:372
  (8 other events, 60.5 us)

commit v4 on v3

--- a/solution.py
+++ b/solution.py
@@ -49,18 +49,10 @@
     return (value * ((1 << 20) // by + 1)) >> 20
 
 
-def whole(shape):
-    return pl.BlockSpec(
-        shape, lambda index: (0,) * len(shape), pipeline_mode=pl.Buffered(buffer_count=1)
-    )
-
-
-def call(kernel, out_shapes, operands, memory=None, scratch=(), limit=12, hbm=(), out=None):
+def call(kernel, out_shapes, operands, memory=None, scratch=(), limit=12, hbm=()):
     memory = memory or {}
     many = isinstance(out_shapes, (list, tuple))
-    out_specs = [whole(each.shape) for each in out_shapes] if many else whole(out_shapes.shape)
-    if out is not None:
-        out_specs = [out] * len(out_shapes)
+    out_specs = [VMEM] * len(out_shapes) if many else VMEM
     operands = [
         pltpu.with_memory_space_constraint(each, pltpu.HBM)
         if at in hbm or memory.get(at) is HBM
@@ -70,8 +62,7 @@
     return pl.pallas_call(
         kernel,
         out_shape=out_shapes,
-        grid=(1,),
-        in_specs=[memory.get(at, whole(each.shape)) for at, each in enumerate(operands)],
+        in_specs=[memory.get(at, VMEM) for at in range(len(operands))],
         out_specs=out_specs,
         scratch_shapes=list(scratch),
         compiler_params=pltpu.CompilerParams(vmem_limit_bytes=limit << 20),
@@ -204,22 +195,21 @@
         copy.wait()
 
 
-def near_kernel(weights, near_next, near_before, sems):
-    run_all(
-        [
-            pltpu.make_async_copy(weights.at[:, :, slab(1)], near_next, sems.at[0]),
-            pltpu.make_async_copy(weights.at[:, :, slab(3)], near_before, sems.at[1]),
-        ]
-    )
-
-
-def far_kernel(weights, far_first, far_second, sems):
-    run_all(
-        [
-            pltpu.make_async_copy(weights.at[0, :, slab(2)], far_first, sems.at[0]),
-            pltpu.make_async_copy(weights.at[1, :, slab(2)], far_second, sems.at[1]),
-        ]
-    )
+def cut_kernel(aheads, weights, *refs):
+    outs, sems = refs[:-1], refs[-1]
+    copies = []
+    for out, ahead in zip(outs, aheads):
+        for local in range(LOCAL):
+            for start in range(0, FR, FR // 4):
+                rows = pl.ds(start, FR // 4)
+                copies.append(
+                    pltpu.make_async_copy(
+                        weights.at[local, rows, slab(ahead)],
+                        out.at[local, rows, :],
+                        sems.at[len(copies)],
+                    )
+                )
+    run_all(copies)
 
 
 def receive_kernel(arrived, table, *outs):
@@ -251,93 +241,116 @@
     return jnp.concatenate(both, axis=0)
 
 
-def hidden_kernel(which_chunks, last, sizes, *refs):
-    count = len(sizes)
+def stage_kernel(all_own, from_before, from_next, from_far, out, sems):
+    sources = (all_own.at[:, :, slab(0)], from_before, from_next, from_far)
+    run_all(
+        [
+            pltpu.make_async_copy(source, out.at[index], sems.at[index])
+            for index, source in enumerate(sources)
+        ]
+    )
+
+
+def chunk_copies(which, gate_all, up_all, gate, up, sems):
+    copies = []
+    for index, chunk in enumerate(which):
+        ahead, aside = OFFSETS[chunk]
+        x, y = my_place()
+        place = ((x + ahead) & 3) * 2 + (y ^ aside)
+        at = pl.ds(pl.multiple_of(place * COLS, COLS), COLS)
+        copies.append(
+            (
+                pltpu.make_async_copy(gate_all.at[:, :, at], gate.at[index], sems.at[0, index]),
+                pltpu.make_async_copy(up_all.at[:, :, at], up.at[index], sems.at[1, index]),
+            )
+        )
+    return copies
+
+
+def add_products(sums, chunk, gate, up):
+    for local in range(LOCAL):
+        rows = rows_of(chunk, local)
+        for which, weights in enumerate((gate, up)):
+            at = 2 * local + which
+            product = nt(rows, weights[local])
+            sums[at] = product if sums[at] is None else sums[at] + product
+
+
+def take(refs, sizes):
     chunks = []
     for size in sizes:
         chunks.append(refs[:size])
         refs = refs[size:]
-    before = None
-    if which_chunks[0] > 0:
-        before, refs = refs[0], refs[1:]
-    gate_all, up_all = refs[:2]
-    outs = refs[2:-3]
+    return chunks, refs
+
+
+def hidden_kernel(which, staged, sizes, *refs):
+    chunks, refs = take(refs, sizes)
+    sums = [None] * (2 * LOCAL)
+    if which[0] > 0:
+        sums = [refs[0][at] for at in range(2 * LOCAL)]
+        refs = refs[1:]
+    gate_all, up_all, total = refs[:3]
+    later = refs[3:-3]
     gate, up, sems = refs[-3:]
-
-    def copies(index):
-        ahead, aside = OFFSETS[which_chunks[index]]
-        x, y = my_place()
-        chunk = ((x + ahead) & 3) * 2 + (y ^ aside)
-        at = pl.ds(pl.multiple_of(chunk * COLS, COLS), COLS)
-        return (
-            pltpu.make_async_copy(gate_all.at[:, :, at], gate.at[index], sems.at[0, index]),
-            pltpu.make_async_copy(up_all.at[:, :, at], up.at[index], sems.at[1, index]),
-        )
-
+    count = len(which)
+    copies = chunk_copies(which, gate_all, up_all, gate, up, sems)
+    if staged:
+        copies += chunk_copies(staged, gate_all, up_all, *later, sems.at[:, count:])
+    for pair in copies:
+        for copy in pair:
+            copy.start()
     for index in range(count):
-        for copy in copies(index):
-            copy.start()
-    sums = [None] * (2 * LOCAL)
-    if before is not None:
-        sums = [before[at] for at in range(2 * LOCAL)]
-    for index in range(count):
-        for copy in copies(index):
+        for copy in copies[index]:
             copy.wait()
-        for local in range(LOCAL):
-            rows = rows_of(chunks[index], local)
-            for which, weights in enumerate((gate, up)):
-                at = 2 * local + which
-                product = nt(rows, weights[index, local])
-                sums[at] = product if sums[at] is None else sums[at] + product
-    if not last:
-        for at in range(2 * LOCAL):
-            outs[0][at] = sums[at]
-        return
+        add_products(sums, chunks[index], gate.at[index], up.at[index])
+    for at in range(2 * LOCAL):
+        total[at] = sums[at]
+    for pair in copies[count:]:
+        for copy in pair:
+            copy.wait()
+
+
+def late_kernel(sizes, *refs):
+    chunks, refs = take(refs, sizes)
+    before, gate, up, *outs = refs
+    sums = [before[at] for at in range(2 * LOCAL)]
+    for index, chunk in enumerate(chunks):
+        add_products(sums, chunk, gate.at[index], up.at[index])
     for local in range(LOCAL):
         value = (jax.nn.silu(sums[2 * local]) * sums[2 * local + 1]).astype(bf16)
         for step in range(STEPS):
             outs[step][:, local * FR : (local + 1) * FR] = value[step * HALF : (step + 1) * HALF]
 
 
-def down_kernel(aside, *refs):
-    units = [refs[2 * index : 2 * index + 2] for index in range(4)]
-    all_own, from_before, from_next, far_first, far_second, out, buffer, sems = refs[8:]
-    x, y = my_place()
-    mine = pl.ds(pl.multiple_of((x * 2 + (y ^ aside)) * COLS, COLS), COLS)
+def down_kernel(aside, count, *refs):
+    units = [refs[count * index : count * (index + 1)] for index in range(4)]
+    staged, out = refs[4 * count :]
+    _, y = my_place()
     inside = pl.ds(pl.multiple_of((y ^ aside) * COLS, COLS), COLS)
-    copies = [
-        pltpu.make_async_copy(all_own.at[:, :, mine], buffer.at[0], sems.at[0]),
-        pltpu.make_async_copy(from_before.at[:, :, inside], buffer.at[1], sems.at[1]),
-        pltpu.make_async_copy(from_next.at[:, :, inside], buffer.at[2], sems.at[2]),
-        pltpu.make_async_copy(far_first.at[:, inside], buffer.at[3, 0], sems.at[3]),
-        pltpu.make_async_copy(far_second.at[:, inside], buffer.at[3, 1], sems.at[4]),
-    ]
-    for copy in copies:
-        copy.start()
     sums = [None] * LOCAL
     for index in range(4):
-        copies[index].wait()
-        if index == 3:
-            copies[4].wait()
-        both = jnp.concatenate([units[index][step][...] for step in range(STEPS)], axis=0)
+        both = jnp.concatenate([each[...] for each in units[index]], axis=0)
         for local in range(LOCAL):
-            product = nn(both[:, local * FR : (local + 1) * FR], buffer[index, local])
+            product = nn(both[:, local * FR : (local + 1) * FR], staged[index, local, :, inside])
             sums[local] = product if sums[local] is None else sums[local] + product
     for local in range(LOCAL):
-        for step in range(STEPS):
+        for step in range(count):
             at = (step * LOCAL + local) * HALF
             out[at : at + HALF, :] = sums[local][step * HALF : (step + 1) * HALF].astype(out.dtype)
 
 
-def return_kernel(mine, other, table, out):
+def return_kernel(mine, other0, other1, table, out):
     for step in range(STEPS):
         for group in range(N_EP // GROUP):
             pieces = []
             for piece in range(Q):
                 for local in range(LOCAL):
-                    at = (step * LOCAL + local) * HALF + group * BLOCK
-                    span = (slice(at, at + BLOCK), slice(piece * LANES, (piece + 1) * LANES))
-                    pieces.append((mine[span] + other[span].astype(f32)).astype(bf16))
+                    at = local * HALF + group * BLOCK
+                    to = step * LOCAL * HALF + at
+                    lanes = slice(piece * LANES, (piece + 1) * LANES)
+                    other = (other0, other1)[step][at : at + BLOCK, lanes].astype(f32)
+                    pieces.append((mine[to : to + BLOCK, lanes] + other).astype(bf16))
             stacked = jnp.concatenate(pieces, axis=0)
             result = nn(table[...], stacked).reshape(GROUP, CHUNK, LANES).astype(bf16)
             out[group * GROUP : (group + 1) * GROUP, step * CHUNK : (step + 1) * CHUNK, :] = result
@@ -365,6 +378,7 @@
 
 NEXT = [(rep_index(x, y), rep_index(x + 1, y)) for x in range(4) for y in range(2)]
 BEFORE = [(rep_index(x, y), rep_index(x - 1, y)) for x in range(4) for y in range(2)]
+ACROSS = [(rep_index(x, y), rep_index(x + 2, y)) for x in range(4) for y in range(2)]
 BESIDE = [(rep_index(x, y), rep_index(x, y + 1)) for x in range(4) for y in range(2)]
 
 
@@ -401,20 +415,19 @@
     )
     own = swap(normed, "rep")
 
-    far_shape, near_shape = sds((FR, 2 * COLS), bf16), sds((LOCAL, FR, 2 * COLS), bf16)
-
-    def cut(kernel, shape):
-        scratch = [pltpu.SemaphoreType.DMA((2,))]
-        return call(kernel, [shape] * 2, (w_down,), memory={0: HBM}, scratch=scratch, out=VMEM)
-
-    near_next, near_before = cut(near_kernel, near_shape)
-    far_first, far_second = cut(far_kernel, far_shape)
+    def cut(*aheads):
+        return call(
+            partial(cut_kernel, aheads),
+            [sds((LOCAL, FR, 2 * COLS), bf16)] * len(aheads),
+            (w_down,),
+            memory={0: HBM},
+            scratch=[pltpu.SemaphoreType.DMA((8 * len(aheads),))],
+        )
+
+    near_next, near_before = cut(1, 3)
     from_before = go(near_next, NEXT)
     from_next = go(near_before, BEFORE)
-    far_first = go(far_first, NEXT)
-    far_second = go(far_second, BEFORE)
-    far_first = go(far_first, NEXT)
-    far_second = go(far_second, BEFORE)
+    from_far = go(cut(2)[0], ACROSS)
 
     ids = expert_ids.reshape(STEPS, N_REP, ROWS, TOPK).swapaxes(0, 1).reshape(ALL_ROWS, TOPK)
     weights = route_weights.reshape(STEPS, N_REP, ROWS, TOPK).swapaxes(0, 1)
@@ -436,53 +449,60 @@
 
     one, two = sds((LOCAL * HALF, COLS), bf16), sds((STEPS * LOCAL * HALF, COLS), bf16)
     rows = call(receive_kernel, [one, one, two], (arrived, sort))
-    sums = ()
     early, late = gathered(*rows)
     every = (*early, *late)
-    for name, which in (("early", (0, 1, 2, 3)), ("middle", (6,)), ("late", (4, 5, 7))):
+    total = sds((2 * LOCAL, STEPS * HALF, FR), f32)
+    last = (4, 5, 7)
+    held = sds((len(last), LOCAL, FR, COLS), bf16)
+    sums = ()
+    for which, staged in (((0, 1, 2, 3), ()), ((6,), last)):
         parts = [every[index] for index in which]
-        sizes = tuple(len(part) for part in parts)
-        count = len(sizes)
-        last = name == "late"
-        chunks = tuple(each for part in parts for each in part)
-        operands = (*chunks, *sums, w_gate, w_up)
-        shapes = [sds((2 * LOCAL, STEPS * HALF, FR), f32)]
-        if last:
-            shapes = [sds((HALF, LOCAL * FR), bf16)] * STEPS
+        count = len(which)
+        operands = (*(each for part in parts for each in part), *sums[:1], w_gate, w_up)
         sums = call(
-            partial(hidden_kernel, which, last, sizes),
-            shapes,
+            partial(hidden_kernel, which, staged, tuple(len(part) for part in parts)),
+            [total] + [held] * (2 if staged else 0),
             operands,
             memory={len(operands) - 2: HBM, len(operands) - 1: HBM},
             scratch=[
                 pltpu.VMEM((count, LOCAL, FR, COLS), bf16),
                 pltpu.VMEM((count, LOCAL, FR, COLS), bf16),
-                pltpu.SemaphoreType.DMA((2, count)),
+                pltpu.SemaphoreType.DMA((2, count + len(staged))),
             ],
             limit=20,
         )
-    hidden0, hidden1 = sums
-    a0, b1 = go(hidden0, NEXT), go(hidden1, BEFORE)
-    a1, b0 = go(hidden1, NEXT), go(hidden0, BEFORE)
-    c0, c1 = go(a0, NEXT), go(b1, BEFORE)
-    units = (hidden0, hidden1, a0, a1, b0, b1, c0, c1)
-
-    def down(aside, dtype):
-        operands = (*units, w_down, from_before, from_next, far_first, far_second)
+    parts = [every[index] for index in last]
+    hidden_all = call(
+        partial(late_kernel, tuple(len(part) for part in parts)),
+        [sds((HALF, LOCAL * FR), bf16)] * STEPS,
+        (*(each for part in parts for each in part), *sums),
+    )
+    staged = call(
+        stage_kernel,
+        sds((4, LOCAL, FR, 2 * COLS), bf16),
+        (w_down, from_before, from_next, from_far),
+        memory={at: HBM for at in range(4)},
+        scratch=[pltpu.SemaphoreType.DMA((4,))],
+    )
+    units = []
+    for hidden in hidden_all:
+        c = go(hidden, ACROSS)
+        a = go(hidden, NEXT)
+        b = go(hidden, BEFORE)
+        units.append((hidden, a, b, c))
+
+    def down(aside, dtype, *steps):
+        count = len(steps)
+        chunks = [each for chunk in zip(*steps) for each in chunk]
         return call(
-            partial(down_kernel, aside),
-            sds((STEPS * LOCAL * HALF, COLS), dtype),
-            operands,
-            memory={at: HBM for at in range(8, 13)},
-            scratch=[
-                pltpu.VMEM((4, LOCAL, FR, COLS), bf16),
-                pltpu.SemaphoreType.DMA((5,)),
-            ],
+            partial(down_kernel, aside, count),
+            sds((count * LOCAL * HALF, COLS), dtype),
+            (*chunks, staged),
         )
 
-    other = go(down(1, bf16), BESIDE)
-    mine = down(0, f32)
-    back = call(return_kernel, sds((N_EP, STEPS * CHUNK, LANES), bf16), (mine, other, unsort))
+    others = [go(down(1, bf16, units[step]), BESIDE) for step in range(STEPS)]
+    mine = down(0, f32, *units)
+    back = call(return_kernel, sds((N_EP, STEPS * CHUNK, LANES), bf16), (mine, *others, unsort))
     back = swap(back, "ep").reshape(slots, LANES)
     mixed = call(mix_kernel, sds((ALL_ROWS, COLS), bf16), (back, keep), hbm=(1,))
     mixed = swap(mixed.reshape(N_REP, STEPS * ROWS, COLS), "rep")

time: 190 us -> 193 us (1.016)
  blocking collectives: 39.8 us -> 43.5 us
    all_to_all x2, blocking collectives: 39.8 us -> 43.5 us  [swap(): return lax.all_to_all(value, axis, split_axis=0, concat_axis=0, tiled=True)]
    ppermute x24 -> x22, waiting for transfers between devices: 49.5 us -> 51.1 us  [go(): return lax.ppermute(value, 'rep', pairs)]
    ppermute x24 -> x22, starting transfers between devices: 34.2 us -> 32.8 us  [go(): return lax.ppermute(value, 'rep', pairs)]
    pallas_call x15 -> x17, Pallas kernels: 26.4 us -> 25.3 us  [call(): pl.pallas_call(kernel, out_shape=out_shapes, in_specs=[memory.get(at, VME...]
  transfers between devices with their start and end apart: 26 -> 24, of which waited for: 16 -> 8; matrix products, arithmetic and copies ran while one was open for 0% -> 0% of each run, Pallas kernels for 9% -> 9%
where the time goes in v4:
time: 193 us; the launch traced here: 192 us
  waiting for transfers between devices  71.6 us (37%)
  starting transfers between devices  49.2 us (25%)
  blocking collectives  43.5 us (23%)
  Pallas kernels  25.3 us (13%)
    ppermute x22, waiting for transfers between devices, go(): return lax.ppermute(value, 'rep', pairs)  51.1 us
    all_to_all x2, blocking collectives, swap(): return lax.all_to_all(value, axis, split_axis=0, concat_axis=0, tiled=True)  43.5 us
    ppermute x22, starting transfers between devices, go(): return lax.ppermute(value, 'rep', pairs)  32.8 us
    pallas_call x17, Pallas kernels, call(): pl.pallas_call(kernel, out_shape=out_shapes, in_specs=[memory.get(at, VME...  25.3 us
    all_to_all x2, waiting for transfers between devices, swap(): return lax.all_to_all(value, axis, split_axis=0, concat_axis=0, tiled=True)  20.5 us
    all_to_all x2, starting transfers between devices, swap(): return lax.all_to_all(value, axis, split_axis=0, concat_axis=0, tiled=True)  16.4 us
  transfers between devices with their start and end apart: 24, of which 8 were waited for; matrix products, arithmetic and copies ran while one was open for 0% of the time, Pallas kernels for 9%

profile of v4, /device:TPU:8, one launch (start us, length us, event | category | flops | bytes accessed | tf_op | source)
XLA Modules:
  0.0 191.6 jit_solution(13614494253856251052)
XLA Ops:
  1.6 5.8 %all-to-all-start = ((bf16[8,8,512]{2,1,0:T(8,128)(2,1)}), bf16[8,8,512]{2,1,0:T(8,128)(2,1)S(1)}, u32[]{:S(2)}, u32[]{:S(2)}) async-start(bf16[8,8,512]{2,1,0:T(8,128)(2,1)} %shard_map.73), calls=%async_computation | async-start | bytes 131072 | tf_op jit(solution)/shard_map/all_to_all | solution.py:390
  8.1 1.8 shard_map.74.table
  10.0 2.4 %all-to-all-done.rows = bf16[8,8,512]{2,1,0:T(8,128)(2,1)S(1)} async-done(((bf16[8,8,512]{2,1,0:T(8,128)(2,1)}), bf16[8,8,512]{2,1,0:T(8,128)(2,1)S(1)}, u32[]{:S(2)}, u32[]{:S(2)}) %all-to-all-start) | async-done | bytes 65568 | tf_op jit(solution)/shard_map/all_to_all | solution.py:390
  13.8 10.6 %all-to-all-start.1 = ((bf16[32,80,128]{2,1,0:T(8,128)(2,1)}), bf16[32,80,128]{2,1,0:T(8,128)(2,1)S(1)}, u32[]{:S(2)}, u32[]{:S(2)}) async-start(bf16[32,80,128]{2,1,0:T(8,128)(2,1)} %bitcast.5), calls=%async_computation.1 | async-start | bytes 1310720 | tf_op jit(solution)/shard_map/all_to_all | solution.py:390
  24.4 3.1 %shard_map.76 = (bf16[256,2560]{1,0:T(8,128)(2,1)S(1)}, bf16[640,640]{1,0:T(8,128)(2,1)S(1)}, bf16[640,640]{1,0:T(8,128)(2,1)S(1)}) custom-call(s32[64,8]{1,0:T(8,128)S(1)} %bitcast.18, f32[64,8]{1,0:T(8,128)S(1)} %bitcast.20), custom_call_target="tpu_custom_call" | custom-call | tf_op jit(solution)/shard_map/pallas_call | solution.py:62
  28.6 18.0 %all-to-all-done.1.arrived = bf16[32,80,128]{2,1,0:T(8,128)(2,1)S(1)} async-done(((bf16[32,80,128]{2,1,0:T(8,128)(2,1)}), bf16[32,80,128]{2,1,0:T(8,128)(2,1)S(1)}, u32[]{:S(2)}, u32[]{:S(2)}) %all-to-all-start.1) | async-done | bytes 655392 | tf_op jit(solution)/shard_map/all_to_all | solution.py:390
  48.3 2.7 %collective-permute-start.6 = (bf16[320,512]{1,0:T(8,128)(2,1)S(1)}, bf16[320,512]{1,0:T(8,128)(2,1)S(1)}, u32[]{:S(2)}, u32[]{:S(2)}) collective-permute-start(bf16[320,512]{1,0:T(8,128)(2,1)S(1)} %get-tuple-element.21.refs_1_), channel_id=1, source_target_pairs={{0,192},{32,224},{64,0},{96,32},{128,64},{160,96},{192,128},{224,1... | collective-permute-start | bytes 983048 | tf_op jit(solution)/shard_map/ppermute | solution.py:386
  52.8 4.3 %collective-permute-done.3.refs_2_ = bf16[320,512]{1,0:T(8,128)(2,1)S(1)} collective-permute-done((bf16[320,512]{1,0:T(8,128)(2,1)S(1)}, bf16[320,512]{1,0:T(8,128)(2,1)S(1)}, u32[]{:S(2)}, u32[]{:S(2)}) %collective-permute-start.3) | collective-permute-done | bytes 327712 | tf_op jit(solution)/shard_map/ppermute | solution.py:386
  57.0 3.2 %collective-permute-start.7 = (bf16[320,512]{1,0:T(8,128)(2,1)S(1)}, bf16[320,512]{1,0:T(8,128)(2,1)S(1)}, u32[]{:S(2)}, u32[]{:S(2)}) collective-permute-start(bf16[320,512]{1,0:T(8,128)(2,1)S(1)} %collective-permute-done.6.refs_5_), channel_id=1, source_target_pairs={{0,192},{32,224},{64,0},{96,32},{128,64},{160,96},{192,128},{224,1... | collective-permute-start | bytes 983048 | tf_op jit(solution)/shard_map/ppermute | solution.py:386
  60.3 2.0 %collective-permute-start.9 = (bf16[320,512]{1,0:T(8,128)(2,1)S(1)}, bf16[320,512]{1,0:T(8,128)(2,1)S(1)}, u32[]{:S(2)}, u32[]{:S(2)}) collective-permute-start(bf16[320,512]{1,0:T(8,128)(2,1)S(1)} %get-tuple-element.21.refs_1_), channel_id=1, source_target_pairs={{0,64},{32,96},{64,128},{96,160},{128,192},{160,224},{192,0},{224,... | collective-permute-start | bytes 983048 | tf_op jit(solution)/shard_map/ppermute | solution.py:386
  62.3 6.5 %collective-permute-done.4.refs_0_ = bf16[320,512]{1,0:T(8,128)(2,1)S(1)} collective-permute-done((bf16[320,512]{1,0:T(8,128)(2,1)S(1)}, bf16[320,512]{1,0:T(8,128)(2,1)S(1)}, u32[]{:S(2)}, u32[]{:S(2)}) %collective-permute-start.4) | collective-permute-done | bytes 327712 | tf_op jit(solution)/shard_map/ppermute | solution.py:386
  72.6 3.2 %collective-permute-start.18 = (bf16[2,192,1024]{2,1,0:T(8,128)(2,1)S(1)}, bf16[2,192,1024]{2,1,0:T(8,128)(2,1)S(1)}, u32[]{:S(2)}, u32[]{:S(2)}) collective-permute-start(bf16[2,192,1024]{2,1,0:T(8,128)(2,1)S(1)} %get-tuple-element.28), channel_id=1, source_target_pairs={{0,192},{32,224},{64,0},{96,32},{128,64},{160,96},{192,128},{224,1... | collective-permute-start | bytes 2359304 | tf_op jit(solution)/shard_map/ppermute | solution.py:386
  79.7 1.8 collective-permute-start.2
  81.5 3.1 %shard_map.78.refs_2_ = f32[4,320,192]{2,1,0:T(8,128)S(1)} custom-call(bf16[320,512]{1,0:T(8,128)(2,1)S(1)} %get-tuple-element.20.refs_0_, bf16[320,512]{1,0:T(8,128)(2,1)S(1)} %get-tuple-element.21.refs_1_, bf16[320,512]{1,0:T(8,128)(2,1)S(1)} %collective-permute-done.3.refs_2_, bf16[320,512]{1,0:T(8,128)(2,1)S(1)} %collective-permute-done.9.refs_3_, ...), custom_call_target="tpu_custom_call" | custom-call | tf_op jit(solution)/shard_map/pallas_call | solution.py:62
  84.6 2.0 %shard_map.79 = (f32[4,320,192]{2,1,0:T(8,128)S(1)}, bf16[3,2,192,512]{3,2,1,0:T(8,128)(2,1)S(1)}, bf16[3,2,192,512]{3,2,1,0:T(8,128)(2,1)S(1)}) custom-call(bf16[320,512]{1,0:T(8,128)(2,1)S(1)} %collective-permute-done.4.refs_0_, bf16[320,512]{1,0:T(8,128)(2,1)S(1)} %collective-permute-done.7.refs_1_, f32[4,320,192]{2,1,0:T(8,128)S(1)} %shard_map.78.refs_2_, ...), custom_call_target="tpu_custom_call" | custom-call | tf_op jit(solution)/shard_map/pallas_call | solution.py:62
  86.7 33.9 %collective-permute-done.1.refs_0_ = bf16[640,512]{1,0:T(8,128)(2,1)S(1)} collective-permute-done((bf16[640,512]{1,0:T(8,128)(2,1)S(1)}, bf16[640,512]{1,0:T(8,128)(2,1)S(1)}, u32[]{:S(2)}, u32[]{:S(2)}) %collective-permute-start.1) | collective-permute-done | bytes 655392 | tf_op jit(solution)/shard_map/ppermute | solution.py:386
  123.0 2.1 %collective-permute-start.14 = (bf16[160,384]{1,0:T(8,128)(2,1)S(1)}, bf16[160,384]{1,0:T(8,128)(2,1)S(1)}, u32[]{:S(2)}, u32[]{:S(2)}) collective-permute-start(bf16[160,384]{1,0:T(8,128)(2,1)S(1)} %get-tuple-element.26.refs_1_.refs_0_), channel_id=1, source_target_pairs={{0,192},{32,224},{64,0},{96,32},{128,64},{160,96},{192,128},{224,1... | collective-permute-start | bytes 368648 | tf_op jit(solution)/shard_map/ppermute | solution.py:386
  127.7 2.4 %collective-permute-start.13 = (bf16[160,384]{1,0:T(8,128)(2,1)S(1)}, bf16[160,384]{1,0:T(8,128)(2,1)S(1)}, u32[]{:S(2)}, u32[]{:S(2)}) collective-permute-start(bf16[160,384]{1,0:T(8,128)(2,1)S(1)} %get-tuple-element.25.refs_0_), channel_id=1, source_target_pairs={{0,192},{32,224},{64,0},{96,32},{128,64},{160,96},{192,128},{224,1... | collective-permute-start | bytes 368648 | tf_op jit(solution)/shard_map/ppermute | solution.py:386
  130.7 1.9 shard_map.83.refs_8_.refs_4_
  133.1 1.9 collective-permute-start.21
  137.1 1.9 collective-permute-start.20
  141.2 3.5 %collective-permute-done.20.other0 = bf16[320,512]{1,0:T(8,128)(2,1)S(1)} collective-permute-done((bf16[320,512]{1,0:T(8,128)(2,1)S(1)}, bf16[320,512]{1,0:T(8,128)(2,1)S(1)}, u32[]{:S(2)}, u32[]{:S(2)}) %collective-permute-start.20) | collective-permute-done | bytes 327712 | tf_op jit(solution)/shard_map/ppermute | solution.py:386
  145.7 33.8 %all_to_all.20 = bf16[32,80,128]{2,1,0:T(8,128)(2,1)S(1)} all-to-all(bf16[32,80,128]{2,1,0:T(8,128)(2,1)S(1)} %shard_map.87), channel_id=1, replica_groups=mesh['rep'=8,'ep'=32] {'ep'}, dimensions={0} | all-to-all | bytes 1310720 | tf_op jit(solution)/shard_map/all_to_all | solution.py:390
  181.3 9.7 %all_to_all.21.arrived = bf16[8,8,512]{2,1,0:T(8,128)(2,1)S(1)} all-to-all(bf16[8,8,512]{2,1,0:T(8,128)(2,1)S(1)} %bitcast.19), channel_id=1, replica_groups=mesh['rep'=8,'ep'=32] {'rep'}, dimensions={0} | all-to-all | bytes 131072 | tf_op jit(solution)/shard_map/all_to_all | solution.py:390
  (55 shorter events, 29.8 us)
Async XLA Ops:
  1.6 10.8 %all-to-all-start = ((bf16[8,8,512]{2,1,0:T(8,128)(2,1)}), bf16[8,8,512]{2,1,0:T(8,128)(2,1)S(1)}, u32[]{:S(2)}, u32[]{:S(2)}) async-start(bf16[8,8,512]{2,1,0:T(8,128)(2,1)} %shard_map.73), calls=%async_computation | async-start | bytes 131072 | tf_op jit(solution)/shard_map/all_to_all | solution.py:390
  13.8 32.9 %all-to-all-start.1 = ((bf16[32,80,128]{2,1,0:T(8,128)(2,1)}), bf16[32,80,128]{2,1,0:T(8,128)(2,1)S(1)}, u32[]{:S(2)}, u32[]{:S(2)}) async-start(bf16[32,80,128]{2,1,0:T(8,128)(2,1)} %bitcast.5), calls=%async_computation.1 | async-start | bytes 1310720 | tf_op jit(solution)/shard_map/all_to_all | solution.py:390
  47.6 9.4 %collective-permute-start.3 = (bf16[320,512]{1,0:T(8,128)(2,1)S(1)}, bf16[320,512]{1,0:T(8,128)(2,1)S(1)}, u32[]{:S(2)}, u32[]{:S(2)}) collective-permute-start(bf16[320,512]{1,0:T(8,128)(2,1)S(1)} %get-tuple-element.20.refs_0_), channel_id=1, source_target_pairs={{0,64},{32,96},{64,128},{96,160},{128,192},{160,224},{192,0},{224,... | collective-permute-start | bytes 983048 | tf_op jit(solution)/shard_map/ppermute | solution.py:386
  48.3 8.8 %collective-permute-start.6 = (bf16[320,512]{1,0:T(8,128)(2,1)S(1)}, bf16[320,512]{1,0:T(8,128)(2,1)S(1)}, u32[]{:S(2)}, u32[]{:S(2)}) collective-permute-start(bf16[320,512]{1,0:T(8,128)(2,1)S(1)} %get-tuple-element.21.refs_1_), channel_id=1, source_target_pairs={{0,192},{32,224},{64,0},{96,32},{128,64},{160,96},{192,128},{224,1... | collective-permute-start | bytes 983048 | tf_op jit(solution)/shard_map/ppermute | solution.py:386
  51.0 26.1 %collective-permute-start = (bf16[640,512]{1,0:T(8,128)(2,1)S(1)}, bf16[640,512]{1,0:T(8,128)(2,1)S(1)}, u32[]{:S(2)}, u32[]{:S(2)}) collective-permute-start(bf16[640,512]{1,0:T(8,128)(2,1)S(1)} %get-tuple-element.19), channel_id=1, source_target_pairs={{0,32},{32,0},{64,96},{96,64},{128,160},{160,128},{192,224},{224,1... | collective-permute-start | bytes 1966088 | tf_op jit(solution)/shard_map/ppermute | solution.py:386
  57.0 11.8 %collective-permute-start.4 = (bf16[320,512]{1,0:T(8,128)(2,1)S(1)}, bf16[320,512]{1,0:T(8,128)(2,1)S(1)}, u32[]{:S(2)}, u32[]{:S(2)}) collective-permute-start(bf16[320,512]{1,0:T(8,128)(2,1)S(1)} %collective-permute-done.3.refs_2_), channel_id=1, source_target_pairs={{0,64},{32,96},{64,128},{96,160},{128,192},{160,224},{192,0},{224,... | collective-permute-start | bytes 983048 | tf_op jit(solution)/shard_map/ppermute | solution.py:386
  57.0 13.6 %collective-permute-start.7 = (bf16[320,512]{1,0:T(8,128)(2,1)S(1)}, bf16[320,512]{1,0:T(8,128)(2,1)S(1)}, u32[]{:S(2)}, u32[]{:S(2)}) collective-permute-start(bf16[320,512]{1,0:T(8,128)(2,1)S(1)} %collective-permute-done.6.refs_5_), channel_id=1, source_target_pairs={{0,192},{32,224},{64,0},{96,32},{128,64},{160,96},{192,128},{224,1... | collective-permute-start | bytes 983048 | tf_op jit(solution)/shard_map/ppermute | solution.py:386
  60.3 12.2 %collective-permute-start.10 = (bf16[320,512]{1,0:T(8,128)(2,1)S(1)}, bf16[320,512]{1,0:T(8,128)(2,1)S(1)}, u32[]{:S(2)}, u32[]{:S(2)}) collective-permute-start(bf16[320,512]{1,0:T(8,128)(2,1)S(1)} %get-tuple-element.20.refs_0_), channel_id=1, source_target_pairs={{0,192},{32,224},{64,0},{96,32},{128,64},{160,96},{192,128},{224,1... | collective-permute-start | bytes 983048 | tf_op jit(solution)/shard_map/ppermute | solution.py:386
  60.3 12.3 %collective-permute-start.9 = (bf16[320,512]{1,0:T(8,128)(2,1)S(1)}, bf16[320,512]{1,0:T(8,128)(2,1)S(1)}, u32[]{:S(2)}, u32[]{:S(2)}) collective-permute-start(bf16[320,512]{1,0:T(8,128)(2,1)S(1)} %get-tuple-element.21.refs_1_), channel_id=1, source_target_pairs={{0,64},{32,96},{64,128},{96,160},{128,192},{160,224},{192,0},{224,... | collective-permute-start | bytes 983048 | tf_op jit(solution)/shard_map/ppermute | solution.py:386
  68.8 9.5 %collective-permute-start.5 = (bf16[320,512]{1,0:T(8,128)(2,1)S(1)}, bf16[320,512]{1,0:T(8,128)(2,1)S(1)}, u32[]{:S(2)}, u32[]{:S(2)}) collective-permute-start(bf16[320,512]{1,0:T(8,128)(2,1)S(1)} %collective-permute-done.4.refs_0_), channel_id=1, source_target_pairs={{0,32},{32,0},{64,96},{96,64},{128,160},{160,128},{192,224},{224,1... | collective-permute-start | bytes 983048 | tf_op jit(solution)/shard_map/ppermute | solution.py:386
  70.6 9.1 %collective-permute-start.8 = (bf16[320,512]{1,0:T(8,128)(2,1)S(1)}, bf16[320,512]{1,0:T(8,128)(2,1)S(1)}, u32[]{:S(2)}, u32[]{:S(2)}) collective-permute-start(bf16[320,512]{1,0:T(8,128)(2,1)S(1)} %collective-permute-done.7.refs_1_), channel_id=1, source_target_pairs={{0,32},{32,0},{64,96},{96,64},{128,160},{160,128},{192,224},{224,1... | collective-permute-start | bytes 983048 | tf_op jit(solution)/shard_map/ppermute | solution.py:386
  72.5 52.7 %collective-permute-start.17 = (bf16[2,192,1024]{2,1,0:T(8,128)(2,1)S(1)}, bf16[2,192,1024]{2,1,0:T(8,128)(2,1)S(1)}, u32[]{:S(2)}, u32[]{:S(2)}) collective-permute-start(bf16[2,192,1024]{2,1,0:T(8,128)(2,1)S(1)} %get-tuple-element.27), channel_id=1, source_target_pairs={{0,64},{32,96},{64,128},{96,160},{128,192},{160,224},{192,0},{224,... | collective-permute-start | bytes 2359304 | tf_op jit(solution)/shard_map/ppermute | solution.py:386
  72.6 54.3 %collective-permute-start.18 = (bf16[2,192,1024]{2,1,0:T(8,128)(2,1)S(1)}, bf16[2,192,1024]{2,1,0:T(8,128)(2,1)S(1)}, u32[]{:S(2)}, u32[]{:S(2)}) collective-permute-start(bf16[2,192,1024]{2,1,0:T(8,128)(2,1)S(1)} %get-tuple-element.28), channel_id=1, source_target_pairs={{0,192},{32,224},{64,0},{96,32},{128,64},{160,96},{192,128},{224,1... | collective-permute-start | bytes 2359304 | tf_op jit(solution)/shard_map/ppermute | solution.py:386
  77.1 50.7 %collective-permute-start.19 = (bf16[2,192,1024]{2,1,0:T(8,128)(2,1)S(1)}, bf16[2,192,1024]{2,1,0:T(8,128)(2,1)S(1)}, u32[]{:S(2)}, u32[]{:S(2)}) collective-permute-start(bf16[2,192,1024]{2,1,0:T(8,128)(2,1)S(1)} %shard_map.82), channel_id=1, source_target_pairs={{0,128},{32,160},{64,192},{96,224},{128,0},{160,32},{192,64},{224,... | collective-permute-start | bytes 2359304 | tf_op jit(solution)/shard_map/ppermute | solution.py:386
  78.3 42.2 %collective-permute-start.1 = (bf16[640,512]{1,0:T(8,128)(2,1)S(1)}, bf16[640,512]{1,0:T(8,128)(2,1)S(1)}, u32[]{:S(2)}, u32[]{:S(2)}) collective-permute-start(bf16[640,512]{1,0:T(8,128)(2,1)S(1)} %collective-permute-done.refs_6_), channel_id=1, source_target_pairs={{0,64},{32,96},{64,128},{96,160},{128,192},{160,224},{192,0},{224,... | collective-permute-start | bytes 1966088 | tf_op jit(solution)/shard_map/ppermute | solution.py:386
  79.7 40.8 %collective-permute-start.2 = (bf16[640,512]{1,0:T(8,128)(2,1)S(1)}, bf16[640,512]{1,0:T(8,128)(2,1)S(1)}, u32[]{:S(2)}, u32[]{:S(2)}) collective-permute-start(bf16[640,512]{1,0:T(8,128)(2,1)S(1)} %collective-permute-done.refs_6_), channel_id=1, source_target_pairs={{0,192},{32,224},{64,0},{96,32},{128,64},{160,96},{192,128},{224,1... | collective-permute-start | bytes 1966088 | tf_op jit(solution)/shard_map/ppermute | solution.py:386
  121.8 8.3 %collective-permute-start.12 = (bf16[160,384]{1,0:T(8,128)(2,1)S(1)}, bf16[160,384]{1,0:T(8,128)(2,1)S(1)}, u32[]{:S(2)}, u32[]{:S(2)}) collective-permute-start(bf16[160,384]{1,0:T(8,128)(2,1)S(1)} %get-tuple-element.26.refs_1_.refs_0_), channel_id=1, source_target_pairs={{0,64},{32,96},{64,128},{96,160},{128,192},{160,224},{192,0},{224,... | collective-permute-start | bytes 368648 | tf_op jit(solution)/shard_map/ppermute | solution.py:386
  123.0 9.6 %collective-permute-start.14 = (bf16[160,384]{1,0:T(8,128)(2,1)S(1)}, bf16[160,384]{1,0:T(8,128)(2,1)S(1)}, u32[]{:S(2)}, u32[]{:S(2)}) collective-permute-start(bf16[160,384]{1,0:T(8,128)(2,1)S(1)} %get-tuple-element.26.refs_1_.refs_0_), channel_id=1, source_target_pairs={{0,192},{32,224},{64,0},{96,32},{128,64},{160,96},{192,128},{224,1... | collective-permute-start | bytes 368648 | tf_op jit(solution)/shard_map/ppermute | solution.py:386
  125.1 7.5 %collective-permute-start.16 = (bf16[160,384]{1,0:T(8,128)(2,1)S(1)}, bf16[160,384]{1,0:T(8,128)(2,1)S(1)}, u32[]{:S(2)}, u32[]{:S(2)}) collective-permute-start(bf16[160,384]{1,0:T(8,128)(2,1)S(1)} %get-tuple-element.26.refs_1_.refs_0_), channel_id=1, source_target_pairs={{0,128},{32,160},{64,192},{96,224},{128,0},{160,32},{192,64},{224,... | collective-permute-start | bytes 368648 | tf_op jit(solution)/shard_map/ppermute | solution.py:386
  126.9 8.1 %collective-permute-start.11 = (bf16[160,384]{1,0:T(8,128)(2,1)S(1)}, bf16[160,384]{1,0:T(8,128)(2,1)S(1)}, u32[]{:S(2)}, u32[]{:S(2)}) collective-permute-start(bf16[160,384]{1,0:T(8,128)(2,1)S(1)} %get-tuple-element.25.refs_0_), channel_id=1, source_target_pairs={{0,64},{32,96},{64,128},{96,160},{128,192},{160,224},{192,0},{224,... | collective-permute-start | bytes 368648 | tf_op jit(solution)/shard_map/ppermute | solution.py:386
  127.7 7.3 %collective-permute-start.13 = (bf16[160,384]{1,0:T(8,128)(2,1)S(1)}, bf16[160,384]{1,0:T(8,128)(2,1)S(1)}, u32[]{:S(2)}, u32[]{:S(2)}) collective-permute-start(bf16[160,384]{1,0:T(8,128)(2,1)S(1)} %get-tuple-element.25.refs_0_), channel_id=1, source_target_pairs={{0,192},{32,224},{64,0},{96,32},{128,64},{160,96},{192,128},{224,1... | collective-permute-start | bytes 368648 | tf_op jit(solution)/shard_map/ppermute | solution.py:386
  130.1 6.4 %collective-permute-start.15 = (bf16[160,384]{1,0:T(8,128)(2,1)S(1)}, bf16[160,384]{1,0:T(8,128)(2,1)S(1)}, u32[]{:S(2)}, u32[]{:S(2)}) collective-permute-start(bf16[160,384]{1,0:T(8,128)(2,1)S(1)} %get-tuple-element.25.refs_0_), channel_id=1, source_target_pairs={{0,128},{32,160},{64,192},{96,224},{128,0},{160,32},{192,64},{224,... | collective-permute-start | bytes 368648 | tf_op jit(solution)/shard_map/ppermute | solution.py:386
  133.1 8.0 %collective-permute-start.21 = (bf16[320,512]{1,0:T(8,128)(2,1)S(1)}, bf16[320,512]{1,0:T(8,128)(2,1)S(1)}, u32[]{:S(2)}, u32[]{:S(2)}) collective-permute-start(bf16[320,512]{1,0:T(8,128)(2,1)S(1)} %shard_map.86), channel_id=1, source_target_pairs={{0,32},{32,0},{64,96},{96,64},{128,160},{160,128},{192,224},{224,1... | collective-permute-start | bytes 983048 | tf_op jit(solution)/shard_map/ppermute | solution.py:386
  137.1 7.6 %collective-permute-start.20 = (bf16[320,512]{1,0:T(8,128)(2,1)S(1)}, bf16[320,512]{1,0:T(8,128)(2,1)S(1)}, u32[]{:S(2)}, u32[]{:S(2)}) collective-permute-start(bf16[320,512]{1,0:T(8,128)(2,1)S(1)} %shard_map.85), channel_id=1, source_target_pairs={{0,32},{32,0},{64,96},{96,64},{128,160},{160,128},{192,224},{224,1... | collective-permute-start | bytes 983048 | tf_op jit(solution)/shard_map/ppermute | solution.py:386
  (5 other events, 27.8 us)

commit v5 on v4

--- a/solution.py
+++ b/solution.py
@@ -80,8 +80,14 @@
         out[part] = both[:, part * COLS : (part + 1) * COLS]
 
 
+def by_place(ref):
+    return jnp.concatenate(
+        [ref[step, place] for place in range(N_REP) for step in range(STEPS)], axis=0
+    )
+
+
 def positions(ids):
-    chosen = ids[...]
+    chosen = by_place(ids)
     expert = lax.broadcasted_iota(jnp.int32, (ALL_ROWS, EXPERTS), 1)
     hits = [chosen[:, which : which + 1] == expert for which in range(TOPK)]
     member = sum(jnp.where(hit, 1.0, 0.0) for hit in hits)
@@ -126,7 +132,8 @@
 
 def tables_kernel(ids, weights, keep, sort, unsort):
     hits, position = positions(ids)
-    shares = weights[...] / jnp.sum(weights[...], axis=-1, keepdims=True)
+    shares = by_place(weights)
+    shares = shares / jnp.sum(shares, axis=-1, keepdims=True)
     share = sum(
         jnp.where(hit, shares[:, which : which + 1], 0.0) for which, hit in enumerate(hits)
     )
@@ -195,21 +202,27 @@
         copy.wait()
 
 
-def cut_kernel(aheads, weights, *refs):
-    outs, sems = refs[:-1], refs[-1]
-    copies = []
-    for out, ahead in zip(outs, aheads):
-        for local in range(LOCAL):
-            for start in range(0, FR, FR // 4):
-                rows = pl.ds(start, FR // 4)
-                copies.append(
-                    pltpu.make_async_copy(
-                        weights.at[local, rows, slab(ahead)],
-                        out.at[local, rows, :],
-                        sems.at[len(copies)],
-                    )
-                )
-    run_all(copies)
+def cut_copies(aheads, weights, outs, sems):
+    return [
+        pltpu.make_async_copy(weights.at[:, :, slab(ahead)], out, sems.at[index])
+        for index, (ahead, out) in enumerate(zip(aheads, outs))
+    ]
+
+
+def far_kernel(weights, out, sems):
+    run_all(cut_copies((2,), weights, (out,), sems))
+
+
+def near_kernel(weights, all_ids, near_next, near_before, send, ids, sems):
+    copies = cut_copies((1, 3), weights, (near_next, near_before), sems)
+    fetch = pltpu.make_async_copy(all_ids, ids, sems.at[2])
+    fetch.start()
+    for copy in copies:
+        copy.start()
+    fetch.wait()
+    send_table_kernel(ids, send)
+    for copy in copies:
+        copy.wait()
 
 
 def receive_kernel(arrived, table, *outs):
@@ -415,25 +428,26 @@
     )
     own = swap(normed, "rep")
 
-    def cut(*aheads):
-        return call(
-            partial(cut_kernel, aheads),
-            [sds((LOCAL, FR, 2 * COLS), bf16)] * len(aheads),
-            (w_down,),
-            memory={0: HBM},
-            scratch=[pltpu.SemaphoreType.DMA((8 * len(aheads),))],
-        )
-
-    near_next, near_before = cut(1, 3)
+    ids = expert_ids.reshape(STEPS, N_REP, ROWS, TOPK)
+    weights = route_weights.reshape(STEPS, N_REP, ROWS, TOPK)
+    slots = STEPS * N_EP * CHUNK
+    part = sds((LOCAL, FR, 2 * COLS), bf16)
+    near_next, near_before, send = call(
+        near_kernel,
+        [part, part, sds((slots, Q * ALL_ROWS), bf16)],
+        (w_down, ids),
+        memory={0: HBM, 1: HBM},
+        scratch=[
+            pltpu.VMEM((STEPS, N_REP, ROWS, TOPK), jnp.int32),
+            pltpu.SemaphoreType.DMA((3,)),
+        ],
+    )
+    far = call(
+        far_kernel, part, (w_down,), memory={0: HBM}, scratch=[pltpu.SemaphoreType.DMA((1,))]
+    )
     from_before = go(near_next, NEXT)
     from_next = go(near_before, BEFORE)
-    from_far = go(cut(2)[0], ACROSS)
-
-    ids = expert_ids.reshape(STEPS, N_REP, ROWS, TOPK).swapaxes(0, 1).reshape(ALL_ROWS, TOPK)
-    weights = route_weights.reshape(STEPS, N_REP, ROWS, TOPK).swapaxes(0, 1)
-    weights = weights.reshape(ALL_ROWS, TOPK)
-    slots = STEPS * N_EP * CHUNK
-    send = call(send_table_kernel, sds((slots, Q * ALL_ROWS), bf16), (ids,))
+    from_far = go(far, ACROSS)
     keep, sort, unsort = call(
         tables_kernel,
         [
@@ -504,7 +518,7 @@
     mine = down(0, f32, *units)
     back = call(return_kernel, sds((N_EP, STEPS * CHUNK, LANES), bf16), (mine, *others, unsort))
     back = swap(back, "ep").reshape(slots, LANES)
-    mixed = call(mix_kernel, sds((ALL_ROWS, COLS), bf16), (back, keep), hbm=(1,))
+    mixed = call(mix_kernel, sds((ALL_ROWS, COLS), bf16), (back, keep))
     mixed = swap(mixed.reshape(N_REP, STEPS * ROWS, COLS), "rep")
     out = call(final_kernel, sds((STEPS, ROWS, D), bf16), (mixed,))
     return out[:, None, None]

time: 193 us -> 191 us (0.990)
  Pallas kernels: 25.3 us -> 23.1 us
    pallas_call x17 -> x16, Pallas kernels: 25.3 us -> 23.1 us  [call(): pl.pallas_call(kernel, out_shape=out_shapes, in_specs=[memory.get(at, VME...]
  transfers between devices with their start and end apart: 24 -> 24, of which waited for: 8 -> 10; matrix products, arithmetic and copies ran while one was open for 0% -> 0% of each run, Pallas kernels for 9% -> 9%
where the time goes in v5:
time: 191 us
  waiting for transfers between devices  71.3 us (37%)
  starting transfers between devices  49.5 us (26%)
  blocking collectives  43.8 us (23%)
  Pallas kernels  23.1 us (12%)
  local copies, waits for them, and re-layouts  2.7 us (1%)
    ppermute x22, waiting for transfers between devices, go(): return lax.ppermute(value, 'rep', pairs)  52.5 us
    all_to_all x2, blocking collectives, swap(): return lax.all_to_all(value, axis, split_axis=0, concat_axis=0, tiled=True)  43.8 us
    ppermute x22, starting transfers between devices, go(): return lax.ppermute(value, 'rep', pairs)  33.1 us
    pallas_call x16, Pallas kernels, call(): pl.pallas_call(kernel, out_shape=out_shapes, in_specs=[memory.get(at, VME...  23.1 us
    all_to_all x2, waiting for transfers between devices, swap(): return lax.all_to_all(value, axis, split_axis=0, concat_axis=0, tiled=True)  18.9 us
    all_to_all x2, starting transfers between devices, swap(): return lax.all_to_all(value, axis, split_axis=0, concat_axis=0, tiled=True)  16.3 us
  transfers between devices with their start and end apart: 24, of which 10 were waited for; matrix products, arithmetic and copies ran while one was open for 0% of the time, Pallas kernels for 9%

profile of v5, /device:TPU:8, one launch (start us, length us, event | category | flops | bytes accessed | tf_op | source)
XLA Modules:
  0.0 190.5 jit_solution(4302375037114894241)
XLA Ops:
  1.6 5.8 %all-to-all-start = ((bf16[8,8,512]{2,1,0:T(8,128)(2,1)}), bf16[8,8,512]{2,1,0:T(8,128)(2,1)S(1)}, u32[]{:S(2)}, u32[]{:S(2)}) async-start(bf16[8,8,512]{2,1,0:T(8,128)(2,1)} %shard_map.73), calls=%async_computation | async-start | bytes 131072 | tf_op jit(solution)/shard_map/all_to_all | solution.py:403
  7.4 2.6 %shard_map.74 = (bf16[2,192,1024]{2,1,0:T(8,128)(2,1)S(1)}, bf16[2,192,1024]{2,1,0:T(8,128)(2,1)S(1)}, bf16[2560,256]{1,0:T(8,128)(2,1)S(1)}) custom-call(bf16[2,192,4096]{2,1,0:T(8,128)(2,1)} %all_own.1, s32[2,8,4,8]{3,2,1,0:T(4,128)} %bitcast.12), custom_call_target="tpu_custom_call" | custom-call | tf_op jit(solution)/shard_map/pallas_call | solution.py:62
  13.8 10.6 %all-to-all-start.1 = ((bf16[32,80,128]{2,1,0:T(8,128)(2,1)}), bf16[32,80,128]{2,1,0:T(8,128)(2,1)S(1)}, u32[]{:S(2)}, u32[]{:S(2)}) async-start(bf16[32,80,128]{2,1,0:T(8,128)(2,1)} %bitcast.3), calls=%async_computation.1 | async-start | bytes 1310720 | tf_op jit(solution)/shard_map/all_to_all | solution.py:403
  24.4 3.1 %shard_map.76 = (bf16[256,2560]{1,0:T(8,128)(2,1)S(1)}, bf16[640,640]{1,0:T(8,128)(2,1)S(1)}, bf16[640,640]{1,0:T(8,128)(2,1)S(1)}) custom-call(s32[2,8,4,8]{3,2,1,0:T(4,128)S(1)} %bitcast.13, f32[2,8,4,8]{3,2,1,0:T(4,128)S(1)} %bitcast.14), custom_call_target="tpu_custom_call" | custom-call | tf_op jit(solution)/shard_map/pallas_call | solution.py:62
  28.4 18.2 %all-to-all-done.1.arrived = bf16[32,80,128]{2,1,0:T(8,128)(2,1)S(1)} async-done(((bf16[32,80,128]{2,1,0:T(8,128)(2,1)}), bf16[32,80,128]{2,1,0:T(8,128)(2,1)S(1)}, u32[]{:S(2)}, u32[]{:S(2)}) %all-to-all-start.1) | async-done | bytes 655392 | tf_op jit(solution)/shard_map/all_to_all | solution.py:403
  48.5 2.4 %collective-permute-start.6 = (bf16[320,512]{1,0:T(8,128)(2,1)S(1)}, bf16[320,512]{1,0:T(8,128)(2,1)S(1)}, u32[]{:S(2)}, u32[]{:S(2)}) collective-permute-start(bf16[320,512]{1,0:T(8,128)(2,1)S(1)} %get-tuple-element.23.refs_1_), channel_id=1, source_target_pairs={{0,192},{32,224},{64,0},{96,32},{128,64},{160,96},{192,128},{224,1... | collective-permute-start | bytes 983048 | tf_op jit(solution)/shard_map/ppermute | solution.py:399
  52.8 4.3 %collective-permute-done.3.refs_2_ = bf16[320,512]{1,0:T(8,128)(2,1)S(1)} collective-permute-done((bf16[320,512]{1,0:T(8,128)(2,1)S(1)}, bf16[320,512]{1,0:T(8,128)(2,1)S(1)}, u32[]{:S(2)}, u32[]{:S(2)}) %collective-permute-start.3) | collective-permute-done | bytes 327712 | tf_op jit(solution)/shard_map/ppermute | solution.py:399
  57.0 3.2 %collective-permute-start.7 = (bf16[320,512]{1,0:T(8,128)(2,1)S(1)}, bf16[320,512]{1,0:T(8,128)(2,1)S(1)}, u32[]{:S(2)}, u32[]{:S(2)}) collective-permute-start(bf16[320,512]{1,0:T(8,128)(2,1)S(1)} %collective-permute-done.6.refs_5_), channel_id=1, source_target_pairs={{0,192},{32,224},{64,0},{96,32},{128,64},{160,96},{192,128},{224,1... | collective-permute-start | bytes 983048 | tf_op jit(solution)/shard_map/ppermute | solution.py:399
  60.3 2.0 %collective-permute-start.9 = (bf16[320,512]{1,0:T(8,128)(2,1)S(1)}, bf16[320,512]{1,0:T(8,128)(2,1)S(1)}, u32[]{:S(2)}, u32[]{:S(2)}) collective-permute-start(bf16[320,512]{1,0:T(8,128)(2,1)S(1)} %get-tuple-element.23.refs_1_), channel_id=1, source_target_pairs={{0,64},{32,96},{64,128},{96,160},{128,192},{160,224},{192,0},{224,... | collective-permute-start | bytes 983048 | tf_op jit(solution)/shard_map/ppermute | solution.py:399
  62.3 6.5 %collective-permute-done.4.refs_0_ = bf16[320,512]{1,0:T(8,128)(2,1)S(1)} collective-permute-done((bf16[320,512]{1,0:T(8,128)(2,1)S(1)}, bf16[320,512]{1,0:T(8,128)(2,1)S(1)}, u32[]{:S(2)}, u32[]{:S(2)}) %collective-permute-start.4) | collective-permute-done | bytes 327712 | tf_op jit(solution)/shard_map/ppermute | solution.py:399
  68.8 1.8 collective-permute-start.5
  72.5 3.0 %collective-permute-start.18 = (bf16[2,192,1024]{2,1,0:T(8,128)(2,1)S(1)}, bf16[2,192,1024]{2,1,0:T(8,128)(2,1)S(1)}, u32[]{:S(2)}, u32[]{:S(2)}) collective-permute-start(bf16[2,192,1024]{2,1,0:T(8,128)(2,1)S(1)} %copy-done.5), channel_id=1, source_target_pairs={{0,192},{32,224},{64,0},{96,32},{128,64},{160,96},{192,128},{224,1... | collective-permute-start | bytes 2359304 | tf_op jit(solution)/shard_map/ppermute | solution.py:399
  79.6 1.8 collective-permute-start.2
  81.4 3.1 %shard_map.78.refs_2_ = f32[4,320,192]{2,1,0:T(8,128)S(1)} custom-call(bf16[320,512]{1,0:T(8,128)(2,1)S(1)} %get-tuple-element.22.refs_0_, bf16[320,512]{1,0:T(8,128)(2,1)S(1)} %get-tuple-element.23.refs_1_, bf16[320,512]{1,0:T(8,128)(2,1)S(1)} %collective-permute-done.3.refs_2_, bf16[320,512]{1,0:T(8,128)(2,1)S(1)} %collective-permute-done.9.refs_3_, ...), custom_call_target="tpu_custom_call" | custom-call | tf_op jit(solution)/shard_map/pallas_call | solution.py:62
  84.5 2.0 %shard_map.79 = (f32[4,320,192]{2,1,0:T(8,128)S(1)}, bf16[3,2,192,512]{3,2,1,0:T(8,128)(2,1)S(1)}, bf16[3,2,192,512]{3,2,1,0:T(8,128)(2,1)S(1)}) custom-call(bf16[320,512]{1,0:T(8,128)(2,1)S(1)} %collective-permute-done.4.refs_0_, bf16[320,512]{1,0:T(8,128)(2,1)S(1)} %collective-permute-done.7.refs_1_, f32[4,320,192]{2,1,0:T(8,128)S(1)} %shard_map.78.refs_2_, ...), custom_call_target="tpu_custom_call" | custom-call | tf_op jit(solution)/shard_map/pallas_call | solution.py:62
  86.5 34.2 %collective-permute-done.1.refs_0_ = bf16[640,512]{1,0:T(8,128)(2,1)S(1)} collective-permute-done((bf16[640,512]{1,0:T(8,128)(2,1)S(1)}, bf16[640,512]{1,0:T(8,128)(2,1)S(1)}, u32[]{:S(2)}, u32[]{:S(2)}) %collective-permute-start.1) | collective-permute-done | bytes 655392 | tf_op jit(solution)/shard_map/ppermute | solution.py:399
  123.0 2.3 %collective-permute-start.14 = (bf16[160,384]{1,0:T(8,128)(2,1)S(1)}, bf16[160,384]{1,0:T(8,128)(2,1)S(1)}, u32[]{:S(2)}, u32[]{:S(2)}) collective-permute-start(bf16[160,384]{1,0:T(8,128)(2,1)S(1)} %get-tuple-element.28.refs_1_.refs_0_), channel_id=1, source_target_pairs={{0,192},{32,224},{64,0},{96,32},{128,64},{160,96},{192,128},{224,1... | collective-permute-start | bytes 368648 | tf_op jit(solution)/shard_map/ppermute | solution.py:399
  127.8 2.3 %collective-permute-start.13 = (bf16[160,384]{1,0:T(8,128)(2,1)S(1)}, bf16[160,384]{1,0:T(8,128)(2,1)S(1)}, u32[]{:S(2)}, u32[]{:S(2)}) collective-permute-start(bf16[160,384]{1,0:T(8,128)(2,1)S(1)} %get-tuple-element.27.refs_0_), channel_id=1, source_target_pairs={{0,192},{32,224},{64,0},{96,32},{128,64},{160,96},{192,128},{224,1... | collective-permute-start | bytes 368648 | tf_op jit(solution)/shard_map/ppermute | solution.py:399
  130.9 1.9 shard_map.82.refs_8_.refs_4_
  133.4 1.9 collective-permute-start.21
  137.1 1.9 collective-permute-start.20
  141.1 3.5 %collective-permute-done.20.other0 = bf16[320,512]{1,0:T(8,128)(2,1)S(1)} collective-permute-done((bf16[320,512]{1,0:T(8,128)(2,1)S(1)}, bf16[320,512]{1,0:T(8,128)(2,1)S(1)}, u32[]{:S(2)}, u32[]{:S(2)}) %collective-permute-start.20) | collective-permute-done | bytes 327712 | tf_op jit(solution)/shard_map/ppermute | solution.py:399
  145.6 34.1 %all_to_all.20 = bf16[32,80,128]{2,1,0:T(8,128)(2,1)S(1)} all-to-all(bf16[32,80,128]{2,1,0:T(8,128)(2,1)S(1)} %shard_map.86), channel_id=1, replica_groups=mesh['rep'=8,'ep'=32] {'ep'}, dimensions={0} | all-to-all | bytes 1310720 | tf_op jit(solution)/shard_map/all_to_all | solution.py:403
  180.2 9.6 %all_to_all.21.arrived = bf16[8,8,512]{2,1,0:T(8,128)(2,1)S(1)} all-to-all(bf16[8,8,512]{2,1,0:T(8,128)(2,1)S(1)} %bitcast.11), channel_id=1, replica_groups=mesh['rep'=8,'ep'=32] {'rep'}, dimensions={0} | all-to-all | bytes 131072 | tf_op jit(solution)/shard_map/all_to_all | solution.py:403
  (62 shorter events, 28.1 us)
Async XLA Ops:
  1.6 10.8 %all-to-all-start = ((bf16[8,8,512]{2,1,0:T(8,128)(2,1)}), bf16[8,8,512]{2,1,0:T(8,128)(2,1)S(1)}, u32[]{:S(2)}, u32[]{:S(2)}) async-start(bf16[8,8,512]{2,1,0:T(8,128)(2,1)} %shard_map.73), calls=%async_computation | async-start | bytes 131072 | tf_op jit(solution)/shard_map/all_to_all | solution.py:403
  13.8 32.8 %all-to-all-start.1 = ((bf16[32,80,128]{2,1,0:T(8,128)(2,1)}), bf16[32,80,128]{2,1,0:T(8,128)(2,1)S(1)}, u32[]{:S(2)}, u32[]{:S(2)}) async-start(bf16[32,80,128]{2,1,0:T(8,128)(2,1)} %bitcast.3), calls=%async_computation.1 | async-start | bytes 1310720 | tf_op jit(solution)/shard_map/all_to_all | solution.py:403
  47.6 9.4 %collective-permute-start.3 = (bf16[320,512]{1,0:T(8,128)(2,1)S(1)}, bf16[320,512]{1,0:T(8,128)(2,1)S(1)}, u32[]{:S(2)}, u32[]{:S(2)}) collective-permute-start(bf16[320,512]{1,0:T(8,128)(2,1)S(1)} %get-tuple-element.22.refs_0_), channel_id=1, source_target_pairs={{0,64},{32,96},{64,128},{96,160},{128,192},{160,224},{192,0},{224,... | collective-permute-start | bytes 983048 | tf_op jit(solution)/shard_map/ppermute | solution.py:399
  48.5 8.5 %collective-permute-start.6 = (bf16[320,512]{1,0:T(8,128)(2,1)S(1)}, bf16[320,512]{1,0:T(8,128)(2,1)S(1)}, u32[]{:S(2)}, u32[]{:S(2)}) collective-permute-start(bf16[320,512]{1,0:T(8,128)(2,1)S(1)} %get-tuple-element.23.refs_1_), channel_id=1, source_target_pairs={{0,192},{32,224},{64,0},{96,32},{128,64},{160,96},{192,128},{224,1... | collective-permute-start | bytes 983048 | tf_op jit(solution)/shard_map/ppermute | solution.py:399
  51.0 25.7 %collective-permute-start = (bf16[640,512]{1,0:T(8,128)(2,1)S(1)}, bf16[640,512]{1,0:T(8,128)(2,1)S(1)}, u32[]{:S(2)}, u32[]{:S(2)}) collective-permute-start(bf16[640,512]{1,0:T(8,128)(2,1)S(1)} %get-tuple-element.21), channel_id=1, source_target_pairs={{0,32},{32,0},{64,96},{96,64},{128,160},{160,128},{192,224},{224,1... | collective-permute-start | bytes 1966088 | tf_op jit(solution)/shard_map/ppermute | solution.py:399
  57.0 11.8 %collective-permute-start.4 = (bf16[320,512]{1,0:T(8,128)(2,1)S(1)}, bf16[320,512]{1,0:T(8,128)(2,1)S(1)}, u32[]{:S(2)}, u32[]{:S(2)}) collective-permute-start(bf16[320,512]{1,0:T(8,128)(2,1)S(1)} %collective-permute-done.3.refs_2_), channel_id=1, source_target_pairs={{0,64},{32,96},{64,128},{96,160},{128,192},{160,224},{192,0},{224,... | collective-permute-start | bytes 983048 | tf_op jit(solution)/shard_map/ppermute | solution.py:399
  57.0 13.6 %collective-permute-start.7 = (bf16[320,512]{1,0:T(8,128)(2,1)S(1)}, bf16[320,512]{1,0:T(8,128)(2,1)S(1)}, u32[]{:S(2)}, u32[]{:S(2)}) collective-permute-start(bf16[320,512]{1,0:T(8,128)(2,1)S(1)} %collective-permute-done.6.refs_5_), channel_id=1, source_target_pairs={{0,192},{32,224},{64,0},{96,32},{128,64},{160,96},{192,128},{224,1... | collective-permute-start | bytes 983048 | tf_op jit(solution)/shard_map/ppermute | solution.py:399
  60.3 11.5 %collective-permute-start.10 = (bf16[320,512]{1,0:T(8,128)(2,1)S(1)}, bf16[320,512]{1,0:T(8,128)(2,1)S(1)}, u32[]{:S(2)}, u32[]{:S(2)}) collective-permute-start(bf16[320,512]{1,0:T(8,128)(2,1)S(1)} %get-tuple-element.22.refs_0_), channel_id=1, source_target_pairs={{0,192},{32,224},{64,0},{96,32},{128,64},{160,96},{192,128},{224,1... | collective-permute-start | bytes 983048 | tf_op jit(solution)/shard_map/ppermute | solution.py:399
  60.3 12.2 %collective-permute-start.9 = (bf16[320,512]{1,0:T(8,128)(2,1)S(1)}, bf16[320,512]{1,0:T(8,128)(2,1)S(1)}, u32[]{:S(2)}, u32[]{:S(2)}) collective-permute-start(bf16[320,512]{1,0:T(8,128)(2,1)S(1)} %get-tuple-element.23.refs_1_), channel_id=1, source_target_pairs={{0,64},{32,96},{64,128},{96,160},{128,192},{160,224},{192,0},{224,... | collective-permute-start | bytes 983048 | tf_op jit(solution)/shard_map/ppermute | solution.py:399
  68.8 9.4 %collective-permute-start.5 = (bf16[320,512]{1,0:T(8,128)(2,1)S(1)}, bf16[320,512]{1,0:T(8,128)(2,1)S(1)}, u32[]{:S(2)}, u32[]{:S(2)}) collective-permute-start(bf16[320,512]{1,0:T(8,128)(2,1)S(1)} %collective-permute-done.4.refs_0_), channel_id=1, source_target_pairs={{0,32},{32,0},{64,96},{96,64},{128,160},{160,128},{192,224},{224,1... | collective-permute-start | bytes 983048 | tf_op jit(solution)/shard_map/ppermute | solution.py:399
  70.6 9.0 %collective-permute-start.8 = (bf16[320,512]{1,0:T(8,128)(2,1)S(1)}, bf16[320,512]{1,0:T(8,128)(2,1)S(1)}, u32[]{:S(2)}, u32[]{:S(2)}) collective-permute-start(bf16[320,512]{1,0:T(8,128)(2,1)S(1)} %collective-permute-done.7.refs_1_), channel_id=1, source_target_pairs={{0,32},{32,0},{64,96},{96,64},{128,160},{160,128},{192,224},{224,1... | collective-permute-start | bytes 983048 | tf_op jit(solution)/shard_map/ppermute | solution.py:399
  71.8 53.6 %collective-permute-start.17 = (bf16[2,192,1024]{2,1,0:T(8,128)(2,1)}, bf16[2,192,1024]{2,1,0:T(8,128)(2,1)S(1)}, u32[]{:S(2)}, u32[]{:S(2)}) collective-permute-start(bf16[2,192,1024]{2,1,0:T(8,128)(2,1)} %copy-done.6), channel_id=1, source_target_pairs={{0,64},{32,96},{64,128},{96,160},{128,192},{160,224},{192,0},{224,... | collective-permute-start | bytes 2359304 | tf_op jit(solution)/shard_map/ppermute | solution.py:399
  72.5 54.4 %collective-permute-start.18 = (bf16[2,192,1024]{2,1,0:T(8,128)(2,1)S(1)}, bf16[2,192,1024]{2,1,0:T(8,128)(2,1)S(1)}, u32[]{:S(2)}, u32[]{:S(2)}) collective-permute-start(bf16[2,192,1024]{2,1,0:T(8,128)(2,1)S(1)} %copy-done.5), channel_id=1, source_target_pairs={{0,192},{32,224},{64,0},{96,32},{128,64},{160,96},{192,128},{224,1... | collective-permute-start | bytes 2359304 | tf_op jit(solution)/shard_map/ppermute | solution.py:399
  76.7 51.1 %collective-permute-start.19 = (bf16[2,192,1024]{2,1,0:T(8,128)(2,1)S(1)}, bf16[2,192,1024]{2,1,0:T(8,128)(2,1)S(1)}, u32[]{:S(2)}, u32[]{:S(2)}) collective-permute-start(bf16[2,192,1024]{2,1,0:T(8,128)(2,1)S(1)} %shard_map.81), channel_id=1, source_target_pairs={{0,128},{32,160},{64,192},{96,224},{128,0},{160,32},{192,64},{224,... | collective-permute-start | bytes 2359304 | tf_op jit(solution)/shard_map/ppermute | solution.py:399
  78.2 42.6 %collective-permute-start.1 = (bf16[640,512]{1,0:T(8,128)(2,1)S(1)}, bf16[640,512]{1,0:T(8,128)(2,1)S(1)}, u32[]{:S(2)}, u32[]{:S(2)}) collective-permute-start(bf16[640,512]{1,0:T(8,128)(2,1)S(1)} %collective-permute-done.refs_6_), channel_id=1, source_target_pairs={{0,64},{32,96},{64,128},{96,160},{128,192},{160,224},{192,0},{224,... | collective-permute-start | bytes 1966088 | tf_op jit(solution)/shard_map/ppermute | solution.py:399
  79.6 41.1 %collective-permute-start.2 = (bf16[640,512]{1,0:T(8,128)(2,1)S(1)}, bf16[640,512]{1,0:T(8,128)(2,1)S(1)}, u32[]{:S(2)}, u32[]{:S(2)}) collective-permute-start(bf16[640,512]{1,0:T(8,128)(2,1)S(1)} %collective-permute-done.refs_6_), channel_id=1, source_target_pairs={{0,192},{32,224},{64,0},{96,32},{128,64},{160,96},{192,128},{224,1... | collective-permute-start | bytes 1966088 | tf_op jit(solution)/shard_map/ppermute | solution.py:399
  122.0 8.1 %collective-permute-start.12 = (bf16[160,384]{1,0:T(8,128)(2,1)S(1)}, bf16[160,384]{1,0:T(8,128)(2,1)S(1)}, u32[]{:S(2)}, u32[]{:S(2)}) collective-permute-start(bf16[160,384]{1,0:T(8,128)(2,1)S(1)} %get-tuple-element.28.refs_1_.refs_0_), channel_id=1, source_target_pairs={{0,64},{32,96},{64,128},{96,160},{128,192},{160,224},{192,0},{224,... | collective-permute-start | bytes 368648 | tf_op jit(solution)/shard_map/ppermute | solution.py:399
  123.0 9.8 %collective-permute-start.14 = (bf16[160,384]{1,0:T(8,128)(2,1)S(1)}, bf16[160,384]{1,0:T(8,128)(2,1)S(1)}, u32[]{:S(2)}, u32[]{:S(2)}) collective-permute-start(bf16[160,384]{1,0:T(8,128)(2,1)S(1)} %get-tuple-element.28.refs_1_.refs_0_), channel_id=1, source_target_pairs={{0,192},{32,224},{64,0},{96,32},{128,64},{160,96},{192,128},{224,1... | collective-permute-start | bytes 368648 | tf_op jit(solution)/shard_map/ppermute | solution.py:399
  125.3 7.5 %collective-permute-start.16 = (bf16[160,384]{1,0:T(8,128)(2,1)S(1)}, bf16[160,384]{1,0:T(8,128)(2,1)S(1)}, u32[]{:S(2)}, u32[]{:S(2)}) collective-permute-start(bf16[160,384]{1,0:T(8,128)(2,1)S(1)} %get-tuple-element.28.refs_1_.refs_0_), channel_id=1, source_target_pairs={{0,128},{32,160},{64,192},{96,224},{128,0},{160,32},{192,64},{224,... | collective-permute-start | bytes 368648 | tf_op jit(solution)/shard_map/ppermute | solution.py:399
  126.9 8.4 %collective-permute-start.11 = (bf16[160,384]{1,0:T(8,128)(2,1)S(1)}, bf16[160,384]{1,0:T(8,128)(2,1)S(1)}, u32[]{:S(2)}, u32[]{:S(2)}) collective-permute-start(bf16[160,384]{1,0:T(8,128)(2,1)S(1)} %get-tuple-element.27.refs_0_), channel_id=1, source_target_pairs={{0,64},{32,96},{64,128},{96,160},{128,192},{160,224},{192,0},{224,... | collective-permute-start | bytes 368648 | tf_op jit(solution)/shard_map/ppermute | solution.py:399
  127.8 7.4 %collective-permute-start.13 = (bf16[160,384]{1,0:T(8,128)(2,1)S(1)}, bf16[160,384]{1,0:T(8,128)(2,1)S(1)}, u32[]{:S(2)}, u32[]{:S(2)}) collective-permute-start(bf16[160,384]{1,0:T(8,128)(2,1)S(1)} %get-tuple-element.27.refs_0_), channel_id=1, source_target_pairs={{0,192},{32,224},{64,0},{96,32},{128,64},{160,96},{192,128},{224,1... | collective-permute-start | bytes 368648 | tf_op jit(solution)/shard_map/ppermute | solution.py:399
  130.1 6.4 %collective-permute-start.15 = (bf16[160,384]{1,0:T(8,128)(2,1)S(1)}, bf16[160,384]{1,0:T(8,128)(2,1)S(1)}, u32[]{:S(2)}, u32[]{:S(2)}) collective-permute-start(bf16[160,384]{1,0:T(8,128)(2,1)S(1)} %get-tuple-element.27.refs_0_), channel_id=1, source_target_pairs={{0,128},{32,160},{64,192},{96,224},{128,0},{160,32},{192,64},{224,... | collective-permute-start | bytes 368648 | tf_op jit(solution)/shard_map/ppermute | solution.py:399
  133.4 7.8 %collective-permute-start.21 = (bf16[320,512]{1,0:T(8,128)(2,1)S(1)}, bf16[320,512]{1,0:T(8,128)(2,1)S(1)}, u32[]{:S(2)}, u32[]{:S(2)}) collective-permute-start(bf16[320,512]{1,0:T(8,128)(2,1)S(1)} %shard_map.85), channel_id=1, source_target_pairs={{0,32},{32,0},{64,96},{96,64},{128,160},{160,128},{192,224},{224,1... | collective-permute-start | bytes 983048 | tf_op jit(solution)/shard_map/ppermute | solution.py:399
  137.1 7.6 %collective-permute-start.20 = (bf16[320,512]{1,0:T(8,128)(2,1)S(1)}, bf16[320,512]{1,0:T(8,128)(2,1)S(1)}, u32[]{:S(2)}, u32[]{:S(2)}) collective-permute-start(bf16[320,512]{1,0:T(8,128)(2,1)S(1)} %shard_map.84), channel_id=1, source_target_pairs={{0,32},{32,0},{64,96},{96,64},{128,160},{160,128},{192,224},{224,1... | collective-permute-start | bytes 983048 | tf_op jit(solution)/shard_map/ppermute | solution.py:399
  (10 other events, 72.7 us)
